TPU v7x, 256 devices: a whole 4x4x8 slice. The times are simulated.
256 devices in a mesh: region: 64 (over x, z, core), level: 4 (over y).
Axes of the slice: x: 4, y: 4, z: 8, core: 2. Of those that a mesh axis runs over, the one named last changes fastest.
Arguments:
- ensemble: bfloat16 [4, 256, 262144], P('level', None, 'region'), may hold values from -6 to 6
- obs_anomaly: bfloat16 [4, 65536, 256], P('level', 'region'), may hold values from -6 to 6
- innovation: bfloat16 [4, 65536], P('level', 'region'), may hold values from -18 to 18
- obs_precision: bfloat16 [4, 65536], P('level', 'region'), may hold values from 0.019897461 to 0.29882812
- owner_region: int32 [4, 65536, 1], P('level', 'region'), may hold values from 0 to 63; in each aligned block of 1024 rows (0 to 1023, 1024 to 2047, ..., all dimensions but the last counted through in order) at most 24 rows name the same one
- neighbours: int32 [64, 3], replicated, may hold values from 0 to 63, all different within a row
Outputs:
- analysis: bfloat16 [4, 256, 262144], P('level', None, 'region')
Inputs may be any that keep to these rules, and one draw needn't show every extreme that they name: `owner_region`: among the 1024 observations of one device (aligned blocks), no region is named more than 24 times, a bound that some block reaches. `neighbours`: each row lists 3 different regions; every region is listed by some row.
All inputs are finite; a program needn't handle non-finite values.
Results may differ from a plain program's by a relative error of at most 0.0059.
Values may be sent and summed in bfloat16 or wider, within the bound.
No kernel may reach another device: no remote copies, remote signals or barrier semaphores. Data moves between devices by JAX's collectives and lax.ppermute only.
A program may use at most 64 MiB of HBM per device.

v0:
```python
import math

import jax
import jax.numpy as jnp
from jax import lax
from jax.sharding import PartitionSpec as P

NSTEPS = 4


TAPER = 0.6


def cut_along(value, dim, count):
    before, after = (value.shape[:dim], value.shape[dim + 1 :])
    return jnp.moveaxis(value.reshape(*before, count, -1, *after), dim, 0)


def sum_at_owner(value, axis, dim):
    count = lax.axis_size(axis)
    pieces = lax.all_to_all(cut_along(value, dim, count), axis, 0, 0, tiled=True)
    return jnp.sum(pieces, axis=0)


def neighbour_weights(neighbours):
    region_ids = jnp.arange(neighbours.shape[0], dtype=jnp.int32)
    weights = (region_ids[:, None] == region_ids[None, :]).astype(jnp.float32)
    for listed in range(neighbours.shape[1]):
        hit = (neighbours[:, listed][:, None] == region_ids[None, :]).astype(jnp.float32)
        weights = weights + TAPER ** (listed + 1) * hit
    return weights


def inverse_root(matrix):
    order_size = matrix.shape[0]
    identity = jnp.eye(order_size, dtype=jnp.float32)
    norm_scale = 0.5 * jnp.sqrt(jnp.sum(matrix * matrix))
    root_iter = matrix / norm_scale
    inverse_iter = identity
    for newton_step in range(NSTEPS):
        correction = 1.5 * identity - 0.5 * jnp.dot(
            inverse_iter, root_iter, precision=lax.Precision.HIGHEST
        )
        root_iter = jnp.dot(root_iter, correction, precision=lax.Precision.HIGHEST)
        inverse_iter = jnp.dot(correction, inverse_iter, precision=lax.Precision.HIGHEST)
    return inverse_iter / jnp.sqrt(norm_scale)


def analysis_weights(covariance, innovation_sum):
    order_size = covariance.shape[0]
    identity = jnp.eye(order_size, dtype=jnp.float32)
    precision_matrix = covariance + (order_size - 1.0) * identity
    root = inverse_root(precision_matrix)
    inner = jnp.dot(root, innovation_sum, precision=lax.Precision.HIGHEST)
    mean_shift = jnp.dot(root, inner, precision=lax.Precision.HIGHEST)
    return (math.sqrt(order_size - 1.0) * root + mean_shift[:, None]).astype(jnp.bfloat16)


def update_columns(column_block, transform):
    average = jnp.mean(column_block.astype(jnp.float32), axis=0)
    anomaly = (column_block.astype(jnp.float32) - average[None, :]).astype(jnp.bfloat16)
    combined = lax.dot_general(
        transform, anomaly, (((0,), (0,)), ((), ())), preferred_element_type=jnp.float32
    )
    return (combined + average[None, :]).astype(jnp.bfloat16)


def level_factor(distance, levels):
    factor = jnp.zeros(distance.shape, jnp.float32)
    for apart in range(levels):
        factor = factor + 0.5**apart * (distance == apart).astype(jnp.float32)
    return factor


def body(ensemble, obs_anomaly, innovation, obs_precision, owner_region, neighbours):
    regions = lax.axis_size("region")
    levels = lax.axis_size("level")
    my_level = lax.axis_index("level")
    members = obs_anomaly.shape[2]
    local_obs = obs_anomaly.shape[1]
    capacity = 3 * local_obs // (2 * regions)
    slot_count = (neighbours.shape[1] + 1) * capacity
    region_weight = neighbour_weights(neighbours)
    owner_ids = owner_region[0, :, 0]
    region_ids = jnp.arange(regions, dtype=jnp.int32)
    owner_table = (owner_ids[:, None] == region_ids[None, :]).astype(jnp.float32)
    dest_weight = jnp.dot(owner_table, region_weight.T, precision=lax.Precision.HIGHEST)
    live = dest_weight > 0
    position = jnp.cumsum(live.astype(jnp.int32), axis=0) - 1
    gain = (dest_weight * obs_precision[0].astype(jnp.float32)[:, None]).astype(jnp.bfloat16)
    slot_ids = jnp.arange(slot_count, dtype=jnp.int32)
    placement = jnp.logical_and(
        live.T[:, None, :], position.T[:, None, :] == slot_ids[None, :, None]
    )
    place_float = placement.astype(jnp.float32)
    send_rows = jnp.einsum(
        "rso,om->rsm",
        placement.astype(jnp.bfloat16),
        obs_anomaly[0],
        preferred_element_type=jnp.float32,
    ).astype(jnp.bfloat16)
    send_gain = jnp.einsum(
        "rso,or->rs", place_float, gain.astype(jnp.float32), precision=lax.Precision.HIGHEST
    ).astype(jnp.bfloat16)
    send_innov = jnp.einsum(
        "rso,o->rs", place_float, innovation[0].astype(jnp.float32), precision=lax.Precision.HIGHEST
    ).astype(jnp.bfloat16)
    received = (
        lax.all_to_all(send_rows, "region", split_axis=0, concat_axis=0, tiled=True),
        lax.all_to_all(send_gain, "region", split_axis=0, concat_axis=0, tiled=True),
        lax.all_to_all(send_innov, "region", split_axis=0, concat_axis=0, tiled=True),
    )
    routed_rows = received[0].reshape(-1, members)
    routed_gain = received[1].reshape(-1)
    routed_innov = received[2].reshape(-1)
    weighted = (routed_gain.astype(jnp.float32)[:, None] * routed_rows.astype(jnp.float32)).astype(
        jnp.bfloat16
    )
    own_cov = jnp.dot(weighted.T, routed_rows, preferred_element_type=jnp.float32)
    own_sum = jnp.dot(routed_innov, weighted, preferred_element_type=jnp.float32)
    stacked = jnp.tile(own_cov, (levels, 1))
    target_level = jnp.arange(members * lax.axis_size("level"), dtype=jnp.int32) // members
    factor = level_factor(jnp.abs(target_level - my_level), levels)
    covariance = sum_at_owner(factor[:, None] * stacked, "level", 0)
    level_ids = jnp.arange(levels, dtype=jnp.int32)
    sum_terms = level_factor(jnp.abs(level_ids - my_level), levels)[:, None] * own_sum[None, :]
    all_sums = lax.psum(sum_terms, "level")
    innovation_sum = lax.dynamic_index_in_dim(all_sums, my_level, 0, keepdims=False)
    transform = analysis_weights(covariance, innovation_sum)
    return update_columns(ensemble[0], transform)[None]


def solution(mesh):
    return jax.shard_map(
        body,
        mesh=mesh,
        in_specs=(
            P("level", None, "region"),
            P("level", "region", None),
            P("level", "region"),
            P("level", "region"),
            P("level", "region", None),
            P(),
        ),
        out_specs=P("level", None, "region"),
        check_vma=False,
    )
```

profile of v0, /device:TPU:1, one launch (start us, length us, event | category | flops | bytes accessed | tf_op | source)
XLA Modules:
  0.0 175.6 jit_solution(10290218327440279134)
XLA Ops:
  0.0 0.8 slice_bitcast_fusion.2
  0.8 0.7 convert_element_type.111
  1.5 1.2 fusion.32
  2.9 18.0 %reduce-window.6 = s32[64,8,128]{2,1,0:T(8,128)S(1)} reduce-window(s32[64,8,128]{2,1,0:T(8,128)S(1)} %bitcast.82, s32[]{:T(128)} %constant.70.clone.1), window={size=1x1x128 pad=0_0x0_0x127_0}, to_apply=%region_0.0 | reduce-window | flops 8323072 | bytes 524292 | tf_op jit(solution)/shard_map/reduce-window
  21.5 4.8 %fusion.5 = f32[64,1,96]{2,1,0:T(1,128)S(1)} fusion(s32[64,1024]{1,0:T(8,128)S(1)} %bitcast.84, pred[64,1024]{1,0:T(8,128)(4,1)S(1)} %get-tuple-element.6, bf16[1024,64,1]{0,1,2:T(8,128)(2,1)S(1)} %fusion.37), kind=kOutput, calls=%fused_computation.4 | convolution fusion | flops 25165824 | bytes 483328 | tf_op jit(solution)/shard_map/rso,or->rs/dot_general | solution.py:102
  26.2 0.6 copy.17
  26.9 13.0 %all-to-all-start = ((bf16[64,1,96]{2,1,0:T(2,128)(2,1)}), bf16[64,1,96]{2,1,0:T(2,128)(2,1)S(1)}, u32[]{:S(2)}, u32[]{:S(2)}) async-start(bf16[64,1,96]{2,1,0:T(2,128)(2,1)} %copy.17), calls=%async_computation | async-start | bytes 65536 | tf_op jit(solution)/shard_map/all_to_all | solution.py:110
  39.9 6.9 %fusion.21 = bf16[64,96,256]{2,1,0:T(8,128)(2,1)} fusion(s32[64,1024]{1,0:T(8,128)S(1)} %bitcast.85, pred[64,1024]{1,0:T(8,128)(4,1)S(1)} %get-tuple-element.6, bf16[1,1024,256]{2,1,0:T(8,128)(2,1)S(1)} %copy-done), kind=kOutput, calls=%fused_computation.23 | convolution fusion | flops 3235381248 | bytes 3997696 | tf_op jit(solution)/shard_map/rso,om->rsm/dot_general | solution.py:96
  46.8 2.3 %all-to-all-done = bf16[64,1,96]{2,1,0:T(2,128)(2,1)S(1)} async-done(((bf16[64,1,96]{2,1,0:T(2,128)(2,1)}), bf16[64,1,96]{2,1,0:T(2,128)(2,1)S(1)}, u32[]{:S(2)}, u32[]{:S(2)}) %all-to-all-start) | async-done | bytes 12320 | tf_op jit(solution)/shard_map/all_to_all | solution.py:110
  49.1 8.3 %all-to-all-start.1 = ((bf16[64,96,256]{2,1,0:T(8,128)(2,1)}), bf16[64,96,256]{2,1,0:T(8,128)(2,1)}, u32[]{:S(2)}, u32[]{:S(2)}) async-start(bf16[64,96,256]{2,1,0:T(8,128)(2,1)} %fusion.21), calls=%async_computation.1 | async-start | bytes 6291456 | tf_op jit(solution)/shard_map/all_to_all | solution.py:109
  57.4 4.7 %fusion.1 = f32[1,64,96]{2,0,1:T(1,128)S(1)} fusion(s32[64,1024]{1,0:T(8,128)S(1)} %bitcast.86, pred[64,1024]{1,0:T(8,128)(4,1)S(1)} %get-tuple-element.6, bf16[1,1024]{1,0:T(2,128)(2,1)S(1)} %copy-done.2), kind=kOutput, calls=%fused_computation.2 | convolution fusion | flops 25165824 | bytes 354304 | tf_op jit(solution)/shard_map/rso,o->rs/dot_general | solution.py:105
  62.1 0.6 copy.18
  63.2 67.6 %all-to-all-done.1 = bf16[64,96,256]{2,1,0:T(8,128)(2,1)} async-done(((bf16[64,96,256]{2,1,0:T(8,128)(2,1)}), bf16[64,96,256]{2,1,0:T(8,128)(2,1)}, u32[]{:S(2)}, u32[]{:S(2)}) %all-to-all-start.1) | async-done | bytes 3145760 | tf_op jit(solution)/shard_map/all_to_all | solution.py:109
  130.8 5.7 %all-to-all-start.3 = ((bf16[64,1,96]{2,1,0:T(2,128)(2,1)}), bf16[64,1,96]{2,1,0:T(2,128)(2,1)S(1)}, u32[]{:S(2)}, u32[]{:S(2)}) async-start(bf16[64,1,96]{2,1,0:T(2,128)(2,1)} %copy.18), calls=%async_computation.3 | async-start | bytes 65536 | tf_op jit(solution)/shard_map/all_to_all | solution.py:111
  136.5 4.8 %fusion.30 = f32[256,256]{1,0:T(8,128)S(1)} fusion(bf16[64,96,256]{2,1,0:T(8,128)(2,1)} %all-to-all-done.1, f32[64,96]{1,0:T(8,128)S(1)} %bitcast.89), kind=kOutput, calls=%fused_computation.34 | convolution fusion | flops 810024960 | bytes 3432448 | tf_op jit(solution)/shard_map/dot_general | solution.py:119
  141.3 1.2 broadcast_multiply_fusion
  142.5 3.3 %all-to-all-done.3 = bf16[64,1,96]{2,1,0:T(2,128)(2,1)S(1)} async-done(((bf16[64,1,96]{2,1,0:T(2,128)(2,1)}), bf16[64,1,96]{2,1,0:T(2,128)(2,1)S(1)}, u32[]{:S(2)}, u32[]{:S(2)}) %all-to-all-start.3) | async-done | bytes 12320 | tf_op jit(solution)/shard_map/all_to_all | solution.py:111
  145.9 4.3 %all-to-all-start.2 = ((f32[4,256,256]{2,1,0:T(8,128)}), f32[4,256,256]{2,1,0:T(8,128)}, u32[]{:S(2)}, u32[]{:S(2)}) async-start(f32[4,256,256]{2,1,0:T(8,128)} %broadcast_multiply_fusion), calls=%async_computation.2 | async-start | bytes 2097152 | tf_op jit(solution)/shard_map/all_to_all | solution.py:21
  150.2 2.6 %fusion.15 = f32[1,256,1]{1,0,2:T(1,128)S(1)} fusion(bf16[64,96,256]{2,1,0:T(8,128)(2,1)} %all-to-all-done.1, f32[64,96]{1,0:T(8,128)S(1)} %bitcast.90, bf16[64,1,96]{2,1,0:T(2,128)(2,1)S(1)} %all-to-all-done.3), kind=kOutput, calls=%fused_computation.17 | convolution fusion | flops 7864320 | bytes 3183616 | tf_op jit(solution)/shard_map/dot_general | solution.py:120
  152.8 13.1 %psum.7 = f32[4,256]{1,0:T(4,128)S(1)} all-reduce(f32[4,256]{1,0:T(4,128)S(1)} %broadcast_multiply_fusion.2), channel_id=1, replica_groups=mesh['region'=64,'level'=4] {'level'}, use_global_device_ids=true, to_apply=%region_4.5 | all-reduce | flops 1024 | bytes 8192 | tf_op jit(solution)/shard_map/psum | solution.py:127
  165.9 1.3 reduce_sum.27
  167.2 0.7 multiply_reduce_fusion
  169.0 0.4 fusion.40
  169.7 0.4 fusion.28
  170.1 0.4 fusion.78
  170.4 0.4 fusion.77
  170.8 0.4 fusion.27
  171.2 0.4 fusion.79
  171.6 0.4 fusion.80
  172.0 0.4 fusion.26
  172.4 0.4 convolution_divide_fusion
  173.4 2.2 %fusion.14 = bf16[1,256,4096]{2,1,0:T(8,128)(2,1)} fusion(bf16[1,256,4096]{2,1,0:T(8,128)(2,1)S(1)} %copy-done.1, f32[4096]{0:T(1024)S(1)} %broadcast_multiply_fusion.1, f32[256,256]{1,0:T(8,128)S(1)} %convolution_divide_fusion, f32[256]{0:T(256)S(1)} %bitcast.93), kind=kOutput, calls=%fused_computation.16 | convolution fusion | flops 542310400 | bytes 4473856 | tf_op jit(solution)/shard_map/dot_general | solution.py:62
  (29 shorter events, 2.4 us)
Async XLA Ops:
  0.0 39.9 %copy-start = (bf16[1,1024,256]{2,1,0:T(8,128)(2,1)S(1)}, bf16[1,1024,256]{2,1,0:T(8,128)(2,1)}, u32[]{:S(2)}) copy-start(bf16[1,1024,256]{2,1,0:T(8,128)(2,1)} %param.7) | copy-start | bytes 1572868
  26.9 22.2 %all-to-all-start = ((bf16[64,1,96]{2,1,0:T(2,128)(2,1)}), bf16[64,1,96]{2,1,0:T(2,128)(2,1)S(1)}, u32[]{:S(2)}, u32[]{:S(2)}) async-start(bf16[64,1,96]{2,1,0:T(2,128)(2,1)} %copy.17), calls=%async_computation | async-start | bytes 65536 | tf_op jit(solution)/shard_map/all_to_all | solution.py:110
  46.8 10.7 %copy-start.2 = (bf16[1,1024]{1,0:T(2,128)(2,1)S(1)}, bf16[1,1024]{1,0:T(2,128)(2,1)}, u32[]{:S(2)}) copy-start(bf16[1,1024]{1,0:T(2,128)(2,1)} %param.8) | copy-start | bytes 6148
  49.1 81.7 %all-to-all-start.1 = ((bf16[64,96,256]{2,1,0:T(8,128)(2,1)}), bf16[64,96,256]{2,1,0:T(8,128)(2,1)}, u32[]{:S(2)}, u32[]{:S(2)}) async-start(bf16[64,96,256]{2,1,0:T(8,128)(2,1)} %fusion.21), calls=%async_computation.1 | async-start | bytes 6291456 | tf_op jit(solution)/shard_map/all_to_all | solution.py:109
  57.4 5.3 %copy-start.1 = (bf16[1,256,4096]{2,1,0:T(8,128)(2,1)S(1)}, bf16[1,256,4096]{2,1,0:T(8,128)(2,1)}, u32[]{:S(2)}) copy-start(bf16[1,256,4096]{2,1,0:T(8,128)(2,1)} %param.6) | copy-start | bytes 6291460
  130.8 15.1 %all-to-all-start.3 = ((bf16[64,1,96]{2,1,0:T(2,128)(2,1)}), bf16[64,1,96]{2,1,0:T(2,128)(2,1)S(1)}, u32[]{:S(2)}, u32[]{:S(2)}) async-start(bf16[64,1,96]{2,1,0:T(2,128)(2,1)} %copy.18), calls=%async_computation.3 | async-start | bytes 65536 | tf_op jit(solution)/shard_map/all_to_all | solution.py:111
  145.9 20.1 %all-to-all-start.2 = ((f32[4,256,256]{2,1,0:T(8,128)}), f32[4,256,256]{2,1,0:T(8,128)}, u32[]{:S(2)}, u32[]{:S(2)}) async-start(f32[4,256,256]{2,1,0:T(8,128)} %broadcast_multiply_fusion), calls=%async_computation.2 | async-start | bytes 2097152 | tf_op jit(solution)/shard_map/all_to_all | solution.py:21
where the time goes:
time: 176 us
  waiting for transfers between devices  73.3 us (42%)
  matrix products  31.8 us (18%)
  starting transfers between devices  31.3 us (18%)
  other arithmetic  22.6 us (13%)
  blocking collectives  13.1 us (7%)
  local copies, waits for them, and re-layouts  2.54 us (1%)
    all_to_all x1, waiting for transfers between devices, body(): lax.all_to_all(send_rows, 'region', split_axis=0, concat_axis=0, tiled=True)  67.6 us
    another operation x2, other arithmetic  18 us
    psum x1, blocking collectives, body(): all_sums = lax.psum(sum_terms, 'level')  13.1 us
    all_to_all x1, starting transfers between devices, body(): lax.all_to_all(send_gain, 'region', split_axis=0, concat_axis=0, tiled=True)  13 us
    all_to_all x1, starting transfers between devices, body(): lax.all_to_all(send_rows, 'region', split_axis=0, concat_axis=0, tiled=True)  8.29 us
    dot_general x1, matrix products, body(): jnp.einsum('rso,om->rsm', placement.astype(jnp.bfloat16), obs_anomaly[0],...  6.88 us
    all_to_all x1, starting transfers between devices, body(): lax.all_to_all(send_innov, 'region', split_axis=0, concat_axis=0, tiled=T...  5.74 us
    dot_general x1, matrix products, body(): jnp.dot(weighted.T, routed_rows, preferred_element_type=jnp.float32)  4.79 us
  transfers between devices with their start and end apart: 4, of which 3 were waited for; matrix products, arithmetic and copies ran while one was open for 12% of the time, Pallas kernels for 0%

commit v1 on v0

v1 whole, which is shorter than its diff:
```python
import functools
import math

import jax
import jax.numpy as jnp
from jax import lax
from jax.experimental import pallas as pl
from jax.experimental.pallas import tpu as pltpu
from jax.sharding import PartitionSpec as P

NSTEPS = 4
TAPER = 0.6
DECAY = 0.5
LANES = 128
BF16 = jnp.bfloat16
F32 = jnp.float32


def iota(shape, dim):
    return lax.broadcasted_iota(jnp.int32, shape, dim)


def dot(left, right, dims=((1,), (0,))):
    return lax.dot_general(left, right, (dims, ((), ())), preferred_element_type=F32)


def split(value):
    high = value.astype(BF16)
    return high, (value - high.astype(F32)).astype(BF16)


def dot3(left, right):
    lh, ll = left
    rh, rl = right
    return dot(lh, rh) + (dot(lh, rl) + dot(ll, rh))


def place_kernel(regions, capacity, owner_ref, precision_ref, obs_ref, rows_ref):
    count = owner_ref.shape[1]
    blocks = count // LANES
    region_ids = iota((regions, LANES), 0)
    earlier = (iota((LANES, LANES), 0) < iota((LANES, LANES), 1)).astype(BF16)
    counter = jnp.concatenate([earlier, jnp.ones((LANES, LANES), BF16)], axis=1)
    owners = owner_ref[...]
    named = [region_ids == owners[:, b * LANES : (b + 1) * LANES] for b in range(blocks)]
    table = jnp.concatenate([hit.astype(F32).astype(BF16) for hit in named], axis=0)
    ranks = dot(table, counter)
    base = (region_ids * capacity).astype(F32)
    pieces = []
    for b in range(blocks):
        part = ranks[b * regions : (b + 1) * regions]
        slot = jnp.where(named[b], part[:, :LANES] + base, 0.0)
        pieces.append(jnp.sum(slot, axis=0, keepdims=True))
        base = base + part[:, LANES:]
    slots = jnp.concatenate(pieces, axis=1).astype(jnp.int32)
    scale = jnp.sqrt(precision_ref[...].astype(F32))
    obs = obs_ref[...]
    step = 256
    for start in range(0, regions * capacity, step):
        hit = slots == iota((step, count), 0) + start
        placed = jnp.where(hit, scale, 0.0).astype(BF16)
        rows_ref[start : start + step, :] = dot(placed, obs).astype(BF16)


def innovation_kernel(owner_ref, precision_ref, innovation_ref, obs_ref, sums_ref):
    count = owner_ref.shape[1]
    factor = precision_ref[...].astype(F32) * innovation_ref[...].astype(F32)
    table = jnp.where(iota((LANES, count), 0) == owner_ref[...], factor, 0.0).astype(BF16)
    sums_ref[...] = dot(obs_ref[...], table, ((0,), (1,)))


def weight_kernel(regions, levels, neigh, neighbours_ref, high_ref, low_ref, wide_ref):
    size = 2 * regions * levels
    per = 2 * levels
    table = neighbours_ref[...]
    lanes = iota((regions, LANES), 1)
    weight = (iota((regions, LANES), 0) == lanes).astype(F32)
    for listed in range(neigh):
        weight = weight + TAPER ** (listed + 1) * (table[:, listed : listed + 1] == lanes).astype(F32)
    wide = jnp.broadcast_to(weight[:, None, :], (regions, per, LANES)).reshape(size, LANES)
    wide_ref[...] = wide
    high, low = split(wide[:, :regions])
    spread = (iota((regions, size), 1) // per == iota((regions, size), 0)).astype(F32).astype(BF16)
    full = dot(high, spread) + dot(low, spread)
    row = iota((size, size), 0) % per
    col = iota((size, size), 1) % per
    apart = jnp.abs(row // 2 - col // 2)
    factor = jnp.zeros((size, size), F32)
    for distance in range(levels):
        factor = jnp.where(apart == distance, DECAY**distance, factor)
    full = full * jnp.where(row % 2 == col % 2, factor, 0.0)
    high, low = split(full)
    high_ref[...] = high
    low_ref[...] = low


def covariance_kernel(rows_ref, sums_ref, message_ref, scratch_ref):
    half = LANES
    rows = rows_ref[...]
    total = dot(rows, rows, ((0,), (0,)))
    above = iota((half, half), 0) <= iota((half, half), 1)
    same = iota((half, half), 0) == iota((half, half), 1)
    corner = total[half:, half:]
    packed = jnp.concatenate([jnp.where(above, total[:half, :half], corner), total[:half, half:]], axis=0)
    diagonal = jnp.sum(jnp.where(same, corner, 0.0), axis=1, keepdims=True)
    diagonal = jnp.concatenate([diagonal, jnp.zeros_like(diagonal)], axis=0)
    extra = jnp.where(iota((2 * half, LANES), 1) == LANES // 2, diagonal, sums_ref[...])
    scratch_ref[pl.ds(0, 2 * half, 2), :] = packed
    scratch_ref[pl.ds(1, 2 * half, 2), :] = extra
    message_ref[...] = scratch_ref[...].astype(BF16)


def mix_kernel(levels, message_ref, high_ref, low_ref, wide_ref, mixed_ref):
    size = message_ref.shape[0]
    per = 2 * levels
    message = message_ref[...]
    mixed = dot(high_ref[...], message) + dot(low_ref[...], message)
    row = iota((per, size), 0)
    col = iota((per, size), 1)
    apart = jnp.abs(row // 2 - (col % per) // 2)
    factor = jnp.zeros((per, size), F32)
    for distance in range(levels):
        factor = jnp.where(apart == distance, DECAY**distance, factor)
    factor = jnp.where((row % 2 == 1) & (col % 2 == 1), factor, 0.0)
    level_sums = dot(factor.astype(BF16), message)
    level_sums = jnp.where(iota((per, LANES), 1) < LANES // 2, level_sums, 0.0)
    spread = jnp.broadcast_to(level_sums[None], (size // per, per, LANES)).reshape(size, LANES)
    sums = jnp.sum(wide_ref[...] * spread, axis=1, keepdims=True)
    high = sums.astype(BF16).astype(F32)
    odd = iota((size, LANES), 0) % 2 == 1
    lane = iota((size, LANES), 1)
    mixed = jnp.where(odd & (lane == 0), high, mixed)
    mixed = jnp.where(odd & (lane == 1), sums - high, mixed)
    mixed_ref[...] = mixed.astype(BF16)


def transform_kernel(message_ref, transform_ref, scratch_ref):
    half = LANES
    size = 2 * half
    scratch_ref[...] = message_ref[...].astype(F32)
    packed = scratch_ref[pl.ds(0, size, 2), :]
    extra = scratch_ref[pl.ds(1, size, 2), :]
    tri = packed[:half]
    tri_t = tri.T
    cross = packed[half:]
    row = iota((half, half), 0)
    col = iota((half, half), 1)
    first = jnp.where(row <= col, tri, tri_t)
    second = jnp.where(row > col, tri, tri_t)
    second = jnp.where(row == col, extra[:half, half // 2 : half // 2 + 1], second)
    matrix = jnp.concatenate(
        [jnp.concatenate([first, cross], axis=1), jnp.concatenate([cross.T, second], axis=1)], axis=0
    )
    same = iota((size, size), 0) == iota((size, size), 1)
    matrix = matrix + jnp.where(same, size - 1.0, 0.0)
    innovation = extra[:, 0:1] + extra[:, 1:2]
    squares = jnp.sum(jnp.sum(matrix * matrix, axis=0, keepdims=True), axis=1, keepdims=True)
    norm_scale = 0.5 * jnp.sqrt(squares)
    diagonal = jnp.where(same, 1.5, 0.0)
    root_iter = matrix / norm_scale
    correction = diagonal - 0.5 * root_iter
    inverse_iter = correction
    root_iter = dot3(split(root_iter), split(correction))
    for newton_step in range(1, NSTEPS):
        inverse_split = split(inverse_iter)
        root_split = split(root_iter)
        correction = split(diagonal - 0.5 * dot3(inverse_split, root_split))
        if newton_step < NSTEPS - 1:
            root_iter = dot3(root_split, correction)
        inverse_iter = dot3(correction, inverse_split)
    root = inverse_iter / jnp.sqrt(norm_scale)
    root_split = split(root)
    inner = dot3(root_split, split(jnp.broadcast_to(innovation, (size, LANES))))
    mean_shift = dot3(root_split, split(inner))[:, 0:1]
    transform_ref[...] = (math.sqrt(size - 1.0) * root + mean_shift).astype(BF16)


def call(kernel, shapes, *args, scratch=()):
    return pl.pallas_call(
        kernel,
        out_shape=shapes,
        in_specs=[pl.BlockSpec(memory_space=pltpu.VMEM)] * len(args),
        out_specs=jax.tree.map(lambda _: pl.BlockSpec(memory_space=pltpu.VMEM), shapes),
        scratch_shapes=scratch,
    )(*args)


def update_columns(column_block, transform):
    average = jnp.mean(column_block.astype(F32), axis=0)
    anomaly = (column_block.astype(F32) - average[None, :]).astype(BF16)
    combined = dot(transform, anomaly, ((0,), (0,)))
    return (combined + average[None, :]).astype(BF16)


def exchange(message, axes, count):
    blocks = message.reshape(count, -1, message.shape[1])
    return lax.all_to_all(blocks, axes, 0, 0, tiled=True).reshape(message.shape)


def body(ensemble, obs_anomaly, innovation, obs_precision, owner_region, neighbours):
    regions = lax.axis_size("region")
    levels = lax.axis_size("level")
    members = obs_anomaly.shape[2]
    local_obs = obs_anomaly.shape[1]
    capacity = 3 * local_obs // (2 * regions)
    size = 2 * regions * levels
    owners = owner_region.reshape(1, local_obs)
    obs = obs_anomaly[0]
    shape = jax.ShapeDtypeStruct
    rows = call(
        functools.partial(place_kernel, regions, capacity),
        shape((regions * capacity, members), BF16),
        owners,
        obs_precision,
        obs,
    )
    routed = exchange(rows, "region", regions)
    sums = call(
        innovation_kernel, shape((members, LANES), F32), owners, obs_precision, innovation, obs
    )
    high, low, wide = call(
        functools.partial(weight_kernel, regions, levels, neighbours.shape[1]),
        (shape((size, size), BF16), shape((size, size), BF16), shape((size, LANES), F32)),
        neighbours,
    )
    message = call(
        covariance_kernel,
        shape((size, LANES), BF16),
        routed,
        sums,
        scratch=[pltpu.VMEM((size, LANES), F32)],
    )
    message = exchange(message, ("region", "level"), regions * levels)
    message = call(
        functools.partial(mix_kernel, levels), shape((size, LANES), BF16), message, high, low, wide
    )
    message = exchange(message, ("region", "level"), regions * levels)
    transform = call(
        transform_kernel,
        shape((members, members), BF16),
        message,
        scratch=[pltpu.VMEM((size, LANES), F32)],
    )
    return update_columns(ensemble[0], transform)[None]


def solution(mesh):
    return jax.shard_map(
        body,
        mesh=mesh,
        in_specs=(
            P("level", None, "region"),
            P("level", "region", None),
            P("level", "region"),
            P("level", "region"),
            P("level", "region", None),
            P(),
        ),
        out_specs=P("level", None, "region"),
        check_vma=False,
    )
```

time: 176 us -> 94.9 us (0.54)
  waiting for transfers between devices: 73.3 us -> 42.6 us
  matrix products: 31.8 us -> 2.99 us
  other arithmetic: 22.6 us -> 0.35 us
  Pallas kernels: 0 us -> 17.7 us
  blocking collectives: 13.1 us -> 0 us
  starting transfers between devices: 31.3 us -> 27.9 us
    all_to_all x4 -> x3, waiting for transfers between devices: 73.3 us -> 42.6 us  [exchange(): return lax.all_to_all(blocks, axes, 0, 0, tiled=True).reshape(message.shape)]
    dot_general x20 -> x1, matrix products: 31.8 us -> 2.99 us  [dot(): lax.dot_general(left, right, (dims, ((), ())), preferred_element_type=F32)]
    another operation x2 -> x0, other arithmetic: 18 us -> none
    pallas_call x0 -> x6, Pallas kernels: none -> 17.7 us  [call(): pl.pallas_call(kernel, out_shape=shapes, in_specs=[pl.BlockSpec(memory_sp...]
    psum x1 -> x0, blocking collectives: 13.1 us -> none  [body(): all_sums = lax.psum(sum_terms, 'level')]
    all_to_all x4 -> x3, starting transfers between devices: 31.3 us -> 27.9 us  [exchange(): return lax.all_to_all(blocks, axes, 0, 0, tiled=True).reshape(message.shape)]
    unnamed x8 -> x11, local copies, waits for them, and re-layouts: 0.11 us -> 2.9 us
    reduce_sum x3 -> x1, other arithmetic: 2.33 us -> 0.34 us  [update_columns(): average = jnp.mean(column_block.astype(F32), axis=0)]
  transfers between devices with their start and end apart: 4 -> 3, of which waited for: 3 -> 3; matrix products, arithmetic and copies ran while one was open for 12% -> 1% of each run, Pallas kernels for 0% -> 5%
where the time goes in v1:
time: 94.9 us; the launch traced here: 94.4 us
  waiting for transfers between devices  42.6 us (45%)
  starting transfers between devices  27.9 us (29%)
  Pallas kernels  17.7 us (19%)
  matrix products  2.99 us (3%)
  local copies, waits for them, and re-layouts  2.9 us (3%)
    all_to_all x3, waiting for transfers between devices, exchange(): return lax.all_to_all(blocks, axes, 0, 0, tiled=True).reshape(message.shape)  42.6 us
    all_to_all x3, starting transfers between devices, exchange(): return lax.all_to_all(blocks, axes, 0, 0, tiled=True).reshape(message.shape)  27.9 us
    pallas_call x6, Pallas kernels, call(): pl.pallas_call(kernel, out_shape=shapes, in_specs=[pl.BlockSpec(memory_sp...  17.7 us
    dot_general x1, matrix products, dot(): lax.dot_general(left, right, (dims, ((), ())), preferred_element_type=F32)  2.99 us
    unnamed x11, local copies, waits for them, and re-layouts  2.9 us
  transfers between devices with their start and end apart: 3, of which 3 were waited for; matrix products, arithmetic and copies ran while one was open for 1% of the time, Pallas kernels for 5%

profile of v1, /device:TPU:1, one launch (start us, length us, event | category | flops | bytes accessed | tf_op | source)
XLA Modules:
  0.0 94.4 jit_solution(13989647208738244750)
XLA Ops:
  0.0 3.1 %shard_map.64 = bf16[1536,256]{1,0:T(8,128)(2,1)} custom-call(s32[1,1024]{1,0:T(1,128)} %bitcast.26, bf16[1,1024]{1,0:T(2,128)(2,1)} %precision_ref.3, bf16[1024,256]{1,0:T(8,128)(2,1)} %bitcast.20), custom_call_target="tpu_custom_call" | custom-call | tf_op jit(solution)/shard_map/pallas_call | solution.py:179
  3.1 0.0 copy-start.4
  3.1 13.1 %all-to-all-start = ((bf16[64,24,256]{2,1,0:T(8,128)(2,1)}), bf16[64,24,256]{2,1,0:T(8,128)(2,1)S(1)}, u32[]{:S(2)}, u32[]{:S(2)}) async-start(bf16[64,24,256]{2,1,0:T(8,128)(2,1)} %bitcast.19), calls=%async_computation | async-start | bytes 1572864 | tf_op jit(solution)/shard_map/all_to_all | solution.py:197
  16.2 0.0 copy-start
  16.2 2.2 %shard_map.65.sums_ref = f32[256,128]{1,0:T(8,128)} custom-call(s32[1,1024]{1,0:T(1,128)} %bitcast.27, bf16[1,1024]{1,0:T(2,128)(2,1)} %precision_ref.3, bf16[1,1024]{1,0:T(2,128)(2,1)} %innovation_ref.1, bf16[1024,256]{1,0:T(8,128)(2,1)} %bitcast.21), custom_call_target="tpu_custom_call" | custom-call | tf_op jit(solution)/shard_map/pallas_call | solution.py:179
  18.5 20.7 %all-to-all-done = bf16[64,24,256]{2,1,0:T(8,128)(2,1)S(1)} async-done(((bf16[64,24,256]{2,1,0:T(8,128)(2,1)}), bf16[64,24,256]{2,1,0:T(8,128)(2,1)S(1)}, u32[]{:S(2)}, u32[]{:S(2)}) %all-to-all-start) | async-done | bytes 786464 | tf_op jit(solution)/shard_map/all_to_all | solution.py:197
  39.1 0.0 copy-start.1
  39.1 0.9 copy-done.1
  40.0 2.4 %shard_map.66 = bf16[512,128]{1,0:T(8,128)(2,1)} custom-call(bf16[1536,256]{1,0:T(8,128)(2,1)} %bitcast.18, f32[256,128]{1,0:T(8,128)} %shard_map.65.sums_ref), custom_call_target="tpu_custom_call" | custom-call | tf_op jit(solution)/shard_map/pallas_call | solution.py:179
  42.4 8.9 %all-to-all-start.1 = ((bf16[256,2,128]{2,1,0:T(2,128)(2,1)}), bf16[256,2,128]{2,1,0:T(2,128)(2,1)S(1)}, u32[]{:S(2)}, u32[]{:S(2)}) async-start(bf16[256,2,128]{2,1,0:T(2,128)(2,1)} %bitcast.25), calls=%async_computation.1 | async-start | bytes 262144 | tf_op jit(solution)/shard_map/all_to_all | solution.py:197
  51.3 0.0 copy-done.4
  51.3 0.7 copy.7.neighbours_ref
  52.0 2.8 %shard_map.67 = (bf16[512,512]{1,0:T(8,128)(2,1)}, bf16[512,512]{1,0:T(8,128)(2,1)}, f32[512,128]{1,0:T(8,128)}) custom-call(s32[64,3]{1,0:T(8,128)} %copy.7.neighbours_ref), custom_call_target="tpu_custom_call" | custom-call | tf_op jit(solution)/shard_map/pallas_call | solution.py:179
  54.8 9.4 %all-to-all-done.1 = bf16[256,2,128]{2,1,0:T(2,128)(2,1)S(1)} async-done(((bf16[256,2,128]{2,1,0:T(2,128)(2,1)}), bf16[256,2,128]{2,1,0:T(2,128)(2,1)S(1)}, u32[]{:S(2)}, u32[]{:S(2)}) %all-to-all-start.1) | async-done | bytes 131104 | tf_op jit(solution)/shard_map/all_to_all | solution.py:197
  64.1 0.0 copy-start.2
  64.1 0.7 copy-done.2
  64.8 2.6 %shard_map.68 = bf16[512,128]{1,0:T(8,128)(2,1)} custom-call(bf16[512,128]{1,0:T(8,128)(2,1)} %bitcast.22, bf16[512,512]{1,0:T(8,128)(2,1)} %get-tuple-element.8.high_ref, bf16[512,512]{1,0:T(8,128)(2,1)} %get-tuple-element.9.low_ref, f32[512,128]{1,0:T(8,128)} %get-tuple-element.10.wide_ref), custom_call_target="tpu_custom_call" | custom-call | tf_op jit(solution)/shard_map/pallas_call | solution.py:179
  67.3 5.9 %all-to-all-start.2 = ((bf16[256,2,128]{2,1,0:T(2,128)(2,1)}), bf16[256,2,128]{2,1,0:T(2,128)(2,1)S(1)}, u32[]{:S(2)}, u32[]{:S(2)}) async-start(bf16[256,2,128]{2,1,0:T(2,128)(2,1)} %bitcast.23), calls=%async_computation.2 | async-start | bytes 262144 | tf_op jit(solution)/shard_map/all_to_all | solution.py:197
  73.2 0.0 copy-done
  73.2 0.3 convert_reduce_fusion
  73.6 12.6 %all-to-all-done.2 = bf16[256,2,128]{2,1,0:T(2,128)(2,1)S(1)} async-done(((bf16[256,2,128]{2,1,0:T(2,128)(2,1)}), bf16[256,2,128]{2,1,0:T(2,128)(2,1)S(1)}, u32[]{:S(2)}, u32[]{:S(2)}) %all-to-all-start.2) | async-done | bytes 131104 | tf_op jit(solution)/shard_map/all_to_all | solution.py:197
  86.2 0.0 copy-start.3
  86.2 0.7 copy-done.3
  86.8 4.6 %shard_map.69 = bf16[256,256]{1,0:T(8,128)(2,1)} custom-call(bf16[512,128]{1,0:T(8,128)(2,1)} %bitcast.24), custom_call_target="tpu_custom_call" | custom-call | tf_op jit(solution)/shard_map/pallas_call | solution.py:179
  91.4 3.0 %fusion.1 = bf16[1,256,4096]{2,1,0:T(8,128)(2,1)} fusion(bf16[256,256]{1,0:T(8,128)(2,1)} %shard_map.69, bf16[1,256,4096]{2,1,0:T(8,128)(2,1)S(1)} %copy-done, f32[4096]{0:T(1024)S(1)} %broadcast_multiply_fusion), kind=kOutput, calls=%fused_computation.4 | convolution fusion | flops 542113792 | bytes 4341760 | tf_op jit(solution)/shard_map/dot_general | solution.py:24
  (1 shorter events, 0.0 us)
Async XLA Ops:
  3.1 48.2 %copy-start.4 = (s32[64,3]{0,1:T(4,128)S(1)}, s32[64,3]{0,1:T(4,128)}, u32[]{:S(2)}) copy-start(s32[64,3]{0,1:T(4,128)} %param.11) | copy-start | bytes 2308
  3.1 36.0 %all-to-all-start = ((bf16[64,24,256]{2,1,0:T(8,128)(2,1)}), bf16[64,24,256]{2,1,0:T(8,128)(2,1)S(1)}, u32[]{:S(2)}, u32[]{:S(2)}) async-start(bf16[64,24,256]{2,1,0:T(8,128)(2,1)} %bitcast.19), calls=%async_computation | async-start | bytes 1572864 | tf_op jit(solution)/shard_map/all_to_all | solution.py:197
  16.2 57.0 %copy-start = (bf16[1,256,4096]{2,1,0:T(8,128)(2,1)S(1)}, bf16[1,256,4096]{2,1,0:T(8,128)(2,1)}, u32[]{:S(2)}) copy-start(bf16[1,256,4096]{2,1,0:T(8,128)(2,1)} %param.6) | copy-start | bytes 6291460
  39.1 0.9 copy-start.1
  42.4 21.7 %all-to-all-start.1 = ((bf16[256,2,128]{2,1,0:T(2,128)(2,1)}), bf16[256,2,128]{2,1,0:T(2,128)(2,1)S(1)}, u32[]{:S(2)}, u32[]{:S(2)}) async-start(bf16[256,2,128]{2,1,0:T(2,128)(2,1)} %bitcast.25), calls=%async_computation.1 | async-start | bytes 262144 | tf_op jit(solution)/shard_map/all_to_all | solution.py:197
  64.1 0.7 copy-start.2
  67.3 18.8 %all-to-all-start.2 = ((bf16[256,2,128]{2,1,0:T(2,128)(2,1)}), bf16[256,2,128]{2,1,0:T(2,128)(2,1)S(1)}, u32[]{:S(2)}, u32[]{:S(2)}) async-start(bf16[256,2,128]{2,1,0:T(2,128)(2,1)} %bitcast.23), calls=%async_computation.2 | async-start | bytes 262144 | tf_op jit(solution)/shard_map/all_to_all | solution.py:197
  86.2 0.7 copy-start.3

commit v2 on v1

v2 whole, which is shorter than its diff:
```python
import functools
import math

import jax
import jax.numpy as jnp
from jax import lax
from jax.experimental import pallas as pl
from jax.experimental.pallas import tpu as pltpu
from jax.sharding import PartitionSpec as P

NSTEPS = 4
TAPER = 0.6
DECAY = 0.5
LANES = 128
COLUMNS, PLANES, CORES = 4, 8, 2
PAIR = 2
GROUPS = PLANES // PAIR
EXTRA = 8
VMEM_LIMIT = 16 << 20
BF16 = jnp.bfloat16
F32 = jnp.float32


def iota(shape, dim):
    return lax.broadcasted_iota(jnp.int32, shape, dim)


def dot(left, right, dims=((1,), (0,))):
    return lax.dot_general(left, right, (dims, ((), ())), preferred_element_type=F32)


def split(value):
    high = value.astype(BF16)
    return high, (value - high.astype(F32)).astype(BF16)


def dot3(left, right, dims=((1,), (0,))):
    lh, ll = left
    rh, rl = right
    return dot(lh, rh, dims) + (dot(lh, rl, dims) + dot(ll, rh, dims))


def region_parts(region):
    return region // (PLANES * CORES), region // CORES % PLANES, region % CORES


def site(region):
    x, z, core = region_parts(region)
    place = (core * PAIR + z % PAIR) * COLUMNS + x
    return place * GROUPS + z // PAIR


def region_at(place, group):
    core, z, x = place // (PAIR * COLUMNS), place // COLUMNS % PAIR, place % COLUMNS
    return (x * PLANES + group * PAIR + z) * CORES + core


def weights_transposed(listed):
    neigh, regions = listed.shape
    owner = iota((regions, regions), 0)
    weight = (owner == iota((regions, regions), 1)).astype(F32)
    for place in range(neigh):
        weight = weight + TAPER ** (place + 1) * (listed[place : place + 1, :] == owner).astype(F32)
    return weight


def onehot(hit):
    return hit.astype(F32).astype(BF16)


def place_kernel(
    regions, capacity, owner_ref, precision_ref, innovation_ref, obs_ref, listed_ref, rows_ref
):
    count = owner_ref.shape[1]
    blocks = count // LANES
    region_ids = iota((regions, LANES), 0)
    earlier = iota((LANES, LANES), 0) < iota((LANES, LANES), 1)
    counter = jnp.concatenate([onehot(earlier), jnp.ones((LANES, LANES), BF16)], axis=1)
    owners = owner_ref[...]
    named = [region_ids == owners[:, b * LANES : (b + 1) * LANES] for b in range(blocks)]
    ranks = dot(jnp.concatenate([onehot(hit) for hit in named], axis=0), counter)
    base = (site(region_ids) * capacity).astype(F32)
    pieces = []
    for b in range(blocks):
        part = ranks[b * regions : (b + 1) * regions]
        slot = jnp.where(named[b], part[:, :LANES] + base, 0.0)
        pieces.append(jnp.sum(slot, axis=0, keepdims=True))
        base = base + part[:, LANES:]
    slots = jnp.concatenate(pieces, axis=1).astype(jnp.int32)
    precision = precision_ref[...].astype(F32)
    scale = jnp.sqrt(precision)
    obs = obs_ref[...]

    factor = precision * innovation_ref[...].astype(F32)
    hit = iota((regions, count), 0) == owners
    sums = split(dot(jnp.where(hit, factor, 0.0).astype(BF16), obs))
    half = obs[:, LANES:].astype(F32)
    squares = split(dot(jnp.where(hit, precision, 0.0).astype(BF16), (half * half).astype(BF16)))
    weight = split(weights_transposed(listed_ref[...]))
    sites = regions // GROUPS
    row = iota((regions, sites * EXTRA), 1)
    place, item = row // EXTRA, row % EXTRA

    def chosen(group, valid):
        pick = onehot((iota((regions, sites * EXTRA), 0) == region_at(place, group)) & valid)
        return split(dot(weight[0], pick) + dot(weight[1], pick))

    over = ((0,), (0,))
    second = (item - GROUPS) * 2
    is_diag = (item >= GROUPS) & (item < GROUPS + GROUPS // 2)
    extra = dot3(chosen(item, item < GROUPS), sums, over)
    left = dot3(chosen(second, is_diag), squares, over)
    right = dot3(chosen(second + 1, is_diag), squares, over)
    extra = (extra + jnp.concatenate([left, right], axis=1)).astype(BF16)

    span = GROUPS * capacity
    at_once = 4
    for start in range(0, sites, at_once):
        hit = slots == iota((at_once * span, count), 0) + start * span
        placed = dot(jnp.where(hit, scale, 0.0).astype(BF16), obs).astype(BF16)
        for k in range(at_once):
            at = (start + k) * (span + EXTRA)
            rows_ref[at : at + span, :] = placed[k * span : (k + 1) * span]
            rows_ref[at + span : at + span + EXTRA, :] = extra[(start + k) * EXTRA : (start + k + 1) * EXTRA]


def weight_kernel(levels, listed_ref, high_ref, low_ref):
    size, columns = high_ref.shape
    weight = split(weights_transposed(listed_ref[...]))
    regions = listed_ref.shape[1]
    expand = onehot(iota((regions, size), 0) == iota((regions, size), 1) // levels)
    rows = split(dot(weight[0], expand) + dot(weight[1], expand))
    col = iota((regions, columns), 1)
    x, z, core = region_parts(col // (levels * GROUPS))
    owner = (x * PLANES + (col % GROUPS) * PAIR + z % PAIR) * CORES + core
    spread = onehot(iota((regions, columns), 0) == owner)
    over = ((0,), (0,))
    full = dot(rows[0], spread, over) + dot(rows[1], spread, over)
    apart = jnp.abs(iota((size, columns), 0) % levels - iota((size, columns), 1) // GROUPS % levels)
    factor = jnp.zeros((size, columns), F32)
    for distance in range(levels):
        factor = jnp.where(apart == distance, DECAY**distance, factor)
    high, low = split(full * factor)
    high_ref[...] = high
    low_ref[...] = low


def covariance_kernel(capacity, rows_ref, message_ref, sums_ref, scratch_ref):
    half = LANES
    members = rows_ref.shape[2]
    above = iota((half, half), 0) <= iota((half, half), 1)
    for group in range(GROUPS):
        rows = rows_ref[:, group * capacity : (group + 1) * capacity, :].reshape(-1, members)
        total = dot(rows, rows, ((0,), (0,)))
        corner = jnp.where(above, total[:half, :half], total[half:, half:])
        packed = jnp.concatenate([corner, total[:half, half:]], axis=0)
        scratch_ref[pl.ds(group, members, GROUPS), :] = packed
    message_ref[...] = scratch_ref[...].astype(BF16)
    span = GROUPS * capacity
    sums_ref[...] = jnp.sum(rows_ref[:, span : span + EXTRA, :].astype(F32), axis=0)


def mix_kernel(message_ref, high_ref, low_ref, mixed_ref):
    message = message_ref[...]
    mixed_ref[...] = dot(high_ref[...], message) + dot(low_ref[...], message)


def transform_kernel(packed_ref, extra_ref, transform_ref):
    half = LANES
    size = 2 * half
    tri = packed_ref[:half, :]
    tri_t = tri.T
    cross = packed_ref[half:, :]
    row = iota((half, half), 0)
    col = iota((half, half), 1)
    first = jnp.where(row <= col, tri, tri_t)
    second = jnp.where(row > col, tri, tri_t)
    second = jnp.where(row == col, extra_ref[:, size:], second)
    matrix = jnp.concatenate(
        [jnp.concatenate([first, cross], axis=1), jnp.concatenate([cross.T, second], axis=1)], axis=0
    )
    same = iota((size, size), 0) == iota((size, size), 1)
    matrix = matrix + jnp.where(same, size - 1.0, 0.0)
    squares = jnp.sum(jnp.sum(matrix * matrix, axis=0, keepdims=True), axis=1, keepdims=True)
    norm_scale = 0.5 * jnp.sqrt(squares)
    diagonal = jnp.where(same, 1.5, 0.0)
    root_iter = matrix / norm_scale
    correction = diagonal - 0.5 * root_iter
    inverse_iter = correction
    root_iter = dot3(split(root_iter), split(correction))
    for newton_step in range(1, NSTEPS):
        inverse_split = split(inverse_iter)
        root_split = split(root_iter)
        correction = split(diagonal - 0.5 * dot3(inverse_split, root_split))
        if newton_step < NSTEPS - 1:
            root_iter = dot3(root_split, correction)
        inverse_iter = dot3(correction, inverse_split)
    root = inverse_iter / jnp.sqrt(norm_scale)
    root_split = split(root)
    innovation = jnp.broadcast_to(extra_ref[:, :size], (8, size))
    inner = dot3(split(innovation), root_split)
    mean_shift = dot3(split(inner), root_split)[0:1, :]
    transform_ref[...] = (math.sqrt(size - 1.0) * root + mean_shift).astype(BF16)


def call(kernel, shapes, *args, scratch=()):
    return pl.pallas_call(
        kernel,
        out_shape=shapes,
        in_specs=[pl.BlockSpec(memory_space=pltpu.VMEM)] * len(args),
        out_specs=jax.tree.map(lambda _: pl.BlockSpec(memory_space=pltpu.VMEM), shapes),
        scratch_shapes=scratch,
        compiler_params=pltpu.CompilerParams(vmem_limit_bytes=VMEM_LIMIT),
    )(*args)


def update_columns(column_block, transposed):
    average = jnp.mean(column_block.astype(F32), axis=0)
    anomaly = (column_block.astype(F32) - average[None, :]).astype(BF16)
    combined = dot(transposed, anomaly)
    return (combined + average[None, :]).astype(BF16)


def exchange(message, axes, count, groups=None):
    blocks = message.reshape(count, -1, message.shape[-1])
    return lax.all_to_all(blocks, axes, 0, 0, tiled=True, axis_index_groups=groups)


def body(ensemble, obs_anomaly, innovation, obs_precision, owner_region, neighbours):
    regions = lax.axis_size("region")
    levels = lax.axis_size("level")
    my_region = lax.axis_index("region")
    my_level = lax.axis_index("level")
    members = obs_anomaly.shape[2]
    local_obs = obs_anomaly.shape[1]
    capacity = 3 * local_obs // (2 * regions)
    places = regions // GROUPS
    devices = regions * levels
    owners = owner_region.reshape(1, local_obs)
    listed = neighbours.T
    shape = jax.ShapeDtypeStruct
    rows = call(
        functools.partial(place_kernel, regions, capacity),
        shape((places * (GROUPS * capacity + EXTRA), members), BF16),
        owners,
        obs_precision,
        innovation,
        obs_anomaly[0],
        listed,
    )
    near = [[region_at(place, group) for place in range(places)] for group in range(GROUPS)]
    routed = exchange(rows, "region", places, near)
    high, low = call(
        functools.partial(weight_kernel, levels),
        (shape((devices, devices * GROUPS), BF16), shape((devices, devices * GROUPS), BF16)),
        listed,
    )
    message, sums = call(
        functools.partial(covariance_kernel, capacity),
        (shape((members * GROUPS, LANES), BF16), shape((EXTRA, members), F32)),
        routed,
        scratch=[pltpu.VMEM((members * GROUPS, LANES), F32)],
    )
    message = exchange(message, ("region", "level"), devices).reshape(-1, LANES)

    my_group = my_region // CORES % PLANES // PAIR
    diagonals = sums[GROUPS : GROUPS + GROUPS // 2].reshape(GROUPS, LANES)
    parts = jnp.concatenate([sums[:GROUPS], diagonals], axis=1)
    part = lax.dynamic_slice_in_dim(parts, my_group, 1, 0)
    for ahead in range(1, GROUPS):
        sent = lax.dynamic_slice_in_dim(parts, (my_group + ahead) % GROUPS, 1, 0)
        pairs = []
        for region in range(regions):
            x, z, core = region_parts(region)
            pairs.append((region, (x * PLANES + (z + PAIR * ahead) % PLANES) * CORES + core))
        part = part + lax.ppermute(sent, "region", pairs)
    extra = part
    for ahead in range(1, levels):
        arrived = lax.ppermute(part, "level", [(o, (o + ahead) % levels) for o in range(levels)])
        apart = jnp.abs(my_level - (my_level - ahead) % levels)
        factor = sum(DECAY**distance * (apart == distance).astype(F32) for distance in range(levels))
        extra = extra + factor * arrived

    mixed = call(mix_kernel, shape((devices, LANES), F32), message, high, low)
    packed = exchange(mixed, ("region", "level"), devices).reshape(devices, LANES)
    transposed = call(transform_kernel, shape((members, members), BF16), packed, extra)
    return update_columns(ensemble[0], transposed)[None]


def solution(mesh):
    return jax.shard_map(
        body,
        mesh=mesh,
        in_specs=(
            P("level", None, "region"),
            P("level", "region", None),
            P("level", "region"),
            P("level", "region"),
            P("level", "region", None),
            P(),
        ),
        out_specs=P("level", None, "region"),
        check_vma=False,
    )
```

time: 94.9 us -> 81.1 us (0.85)
  waiting for transfers between devices: 42.6 us -> 27.3 us
  starting transfers between devices: 27.9 us -> 38.2 us
  Pallas kernels: 17.7 us -> 8.64 us
    all_to_all x3, waiting for transfers between devices: 42.6 us -> 23.9 us  [exchange(): lax.all_to_all(blocks, axes, 0, 0, tiled=True, axis_index_groups=groups)]
    ppermute x0 -> x6, starting transfers between devices: none -> 13.8 us  [the longest x3 9.85 us: body(): part = part + lax.ppermute(sent, 'region', pairs)]
    pallas_call x6 -> x5, Pallas kernels: 17.7 us -> 8.64 us  [call(): pl.pallas_call(kernel, out_shape=shapes, in_specs=[pl.BlockSpec(memory_sp...]
    all_to_all x3, starting transfers between devices: 27.9 us -> 24.4 us  [exchange(): lax.all_to_all(blocks, axes, 0, 0, tiled=True, axis_index_groups=groups)]
    ppermute x0 -> x6, waiting for transfers between devices: none -> 3.31 us  [the longest x3 3.3 us: body(): lax.ppermute(part, 'level', [(o, (o + ahead) % levels) for o in range(lev...]
    unnamed x11 -> x14, local copies, waits for them, and re-layouts: 2.9 us -> 3.79 us
  transfers between devices with their start and end apart: 3 -> 9, of which waited for: 3 -> 5; matrix products, arithmetic and copies ran while one was open for 1% -> 1% of each run, Pallas kernels for 5% -> 3%
where the time goes in v2:
time: 81.1 us; the launch traced here: 80.7 us
  starting transfers between devices  38.2 us (47%)
  waiting for transfers between devices  27.3 us (34%)
  Pallas kernels  8.64 us (11%)
  local copies, waits for them, and re-layouts  3.81 us (5%)
  matrix products  2.13 us (3%)
    all_to_all x3, starting transfers between devices, exchange(): lax.all_to_all(blocks, axes, 0, 0, tiled=True, axis_index_groups=groups)  24.4 us
    all_to_all x3, waiting for transfers between devices, exchange(): lax.all_to_all(blocks, axes, 0, 0, tiled=True, axis_index_groups=groups)  23.9 us
    ppermute x3, starting transfers between devices, body(): part = part + lax.ppermute(sent, 'region', pairs)  9.85 us
    pallas_call x5, Pallas kernels, call(): pl.pallas_call(kernel, out_shape=shapes, in_specs=[pl.BlockSpec(memory_sp...  8.64 us
    ppermute x3, starting transfers between devices, body(): lax.ppermute(part, 'level', [(o, (o + ahead) % levels) for o in range(lev...  3.93 us
    unnamed x14, local copies, waits for them, and re-layouts  3.79 us
    ppermute x3, waiting for transfers between devices, body(): lax.ppermute(part, 'level', [(o, (o + ahead) % levels) for o in range(lev...  3.3 us
    dot_general x1, matrix products, dot(): lax.dot_general(left, right, (dims, ((), ())), preferred_element_type=F32)  2.13 us
  transfers between devices with their start and end apart: 9, of which 5 were waited for; matrix products, arithmetic and copies ran while one was open for 1% of the time, Pallas kernels for 3%

profile of v2, /device:TPU:1, one launch (start us, length us, event | category | flops | bytes accessed | tf_op | source)
XLA Modules:
  0.0 80.7 jit_solution(17339367704263971203)
XLA Ops:
  0.0 1.0 %copy-done = bf16[1,1024,256]{2,1,0:T(8,128)(2,1)S(1)} copy-done((bf16[1,1024,256]{2,1,0:T(8,128)(2,1)S(1)}, bf16[1,1024,256]{2,1,0:T(8,128)(2,1)}, u32[]{:S(2)}) %copy-start) | copy-done | bytes 524312
  1.0 0.7 copy-done.1
  1.7 0.7 copy-done.3
  2.4 0.7 copy-done.4
  3.1 0.7 copy-done.5
  3.8 2.6 %shard_map.64 = bf16[1664,256]{1,0:T(8,128)(2,1)} custom-call(s32[1,1024]{1,0:T(1,128)S(1)} %bitcast.25, bf16[1,1024]{1,0:T(2,128)(2,1)S(1)} %copy-done.4, bf16[1,1024]{1,0:T(2,128)(2,1)S(1)} %copy-done.5, bf16[1024,256]{1,0:T(8,128)(2,1)S(1)} %bitcast.21, s32[3,64]{1,0:T(4,128)S(1)} %bitcast.23), custom_call_target="tpu_custom_call" | custom-call | tf_op jit(solution)/shard_map/pallas_call | solution.py:207
  6.3 7.2 %all-to-all-start = ((bf16[16,104,256]{2,1,0:T(8,128)(2,1)}), bf16[16,104,256]{2,1,0:T(8,128)(2,1)S(1)}, u32[]{:S(2)}, u32[]{:S(2)}) async-start(bf16[16,104,256]{2,1,0:T(8,128)(2,1)} %bitcast.3), calls=%async_computation | async-start | bytes 1703936 | tf_op jit(solution)/shard_map/all_to_all | solution.py:226
  13.7 13.9 %all-to-all-done.rows_ref = bf16[16,104,256]{2,1,0:T(8,128)(2,1)S(1)} async-done(((bf16[16,104,256]{2,1,0:T(8,128)(2,1)}), bf16[16,104,256]{2,1,0:T(8,128)(2,1)S(1)}, u32[]{:S(2)}, u32[]{:S(2)}) %all-to-all-start) | async-done | bytes 852000 | tf_op jit(solution)/shard_map/all_to_all | solution.py:226
  27.6 1.2 %shard_map.65 = (bf16[1024,128]{1,0:T(8,128)(2,1)}, f32[8,256]{1,0:T(8,128)S(1)}) custom-call(bf16[16,104,256]{2,1,0:T(8,128)(2,1)S(1)} %all-to-all-done.rows_ref), custom_call_target="tpu_custom_call" | custom-call | tf_op jit(solution)/shard_map/pallas_call | solution.py:207
  28.8 11.5 %all-to-all-start.1 = ((bf16[256,4,128]{2,1,0:T(4,128)(2,1)}), bf16[256,4,128]{2,1,0:T(4,128)(2,1)S(1)}, u32[]{:S(2)}, u32[]{:S(2)}) async-start(bf16[256,4,128]{2,1,0:T(4,128)(2,1)} %bitcast.4), calls=%async_computation.1 | async-start | bytes 524288 | tf_op jit(solution)/shard_map/all_to_all | solution.py:226
  40.3 0.0 copy-done.6
  40.3 0.3 convert_reduce_fusion
  40.7 2.7 %collective-permute-start = (f32[1,384]{1,0:T(1,128)S(1)}, f32[1,384]{1,0:T(1,128)S(1)}, u32[]{:S(2)}, u32[]{:S(2)}) collective-permute-start(f32[1,384]{1,0:T(1,128)S(1)} %get-tuple-element.13), channel_id=1, source_target_pairs={{0,16},{4,20},{8,24},{12,28},{16,32},{20,36},{24,40},{28,44},{32,4... | collective-permute-start | bytes 4616 | tf_op jit(solution)/shard_map/ppermute | solution.py:276
  43.4 4.4 %collective-permute-start.1 = (f32[1,384]{1,0:T(1,128)S(1)}, f32[1,384]{1,0:T(1,128)S(1)}, u32[]{:S(2)}, u32[]{:S(2)}) collective-permute-start(f32[1,384]{1,0:T(1,128)S(1)} %get-tuple-element.14), channel_id=1, source_target_pairs={{0,32},{4,36},{8,40},{12,44},{16,48},{20,52},{24,56},{28,60},{32,0... | collective-permute-start | bytes 4616 | tf_op jit(solution)/shard_map/ppermute | solution.py:276
  47.8 2.8 %collective-permute-start.2 = (f32[1,384]{1,0:T(1,128)S(1)}, f32[1,384]{1,0:T(1,128)S(1)}, u32[]{:S(2)}, u32[]{:S(2)}) collective-permute-start(f32[1,384]{1,0:T(1,128)S(1)} %get-tuple-element.15), channel_id=1, source_target_pairs={{0,48},{4,52},{8,56},{12,60},{16,0},{20,4},{24,8},{28,12},{32,16},... | collective-permute-start | bytes 4616 | tf_op jit(solution)/shard_map/ppermute | solution.py:276
  50.6 0.0 copy-done.2
  50.6 0.9 %shard_map.66 = (bf16[256,1024]{1,0:T(8,128)(2,1)S(1)}, bf16[256,1024]{1,0:T(8,128)(2,1)S(1)}) custom-call(s32[3,64]{1,0:T(4,128)S(1)} %bitcast.24), custom_call_target="tpu_custom_call" | custom-call | tf_op jit(solution)/shard_map/pallas_call | solution.py:207
  51.5 4.5 %all-to-all-done.1 = bf16[256,4,128]{2,1,0:T(4,128)(2,1)S(1)} async-done(((bf16[256,4,128]{2,1,0:T(4,128)(2,1)}), bf16[256,4,128]{2,1,0:T(4,128)(2,1)S(1)}, u32[]{:S(2)}, u32[]{:S(2)}) %all-to-all-start.1) | async-done | bytes 262176 | tf_op jit(solution)/shard_map/all_to_all | solution.py:226
  56.0 1.1 %shard_map.67 = f32[256,128]{1,0:T(8,128)} custom-call(bf16[1024,128]{1,0:T(8,128)(2,1)S(1)} %bitcast.20, bf16[256,1024]{1,0:T(8,128)(2,1)S(1)} %get-tuple-element.10.high_ref, bf16[256,1024]{1,0:T(8,128)(2,1)S(1)} %get-tuple-element.11.low_ref), custom_call_target="tpu_custom_call" | custom-call | tf_op jit(solution)/shard_map/pallas_call | solution.py:207
  57.1 5.7 %all-to-all-start.2 = ((f32[256,1,128]{2,1,0:T(1,128)}), f32[256,1,128]{2,1,0:T(1,128)S(1)}, u32[]{:S(2)}, u32[]{:S(2)}) async-start(f32[256,1,128]{2,1,0:T(1,128)} %bitcast.7), calls=%async_computation.2 | async-start | bytes 262144 | tf_op jit(solution)/shard_map/all_to_all | solution.py:226
  62.8 0.0 collective-permute-done
  62.9 0.0 collective-permute-done.1
  62.9 0.0 collective-permute-done.2
  62.9 2.8 %collective-permute-start.5 = (f32[1,384]{1,0:T(1,128)S(1)}, f32[1,384]{1,0:T(1,128)S(1)}, u32[]{:S(2)}, u32[]{:S(2)}) collective-permute-start(f32[1,384]{1,0:T(1,128)S(1)} %add_add_fusion), channel_id=1, source_target_pairs={{0,3},{1,0},{2,1},{3,2},{4,7},{5,4},{6,5},{7,6},{8,11},{9,8},{10,9... | collective-permute-start | bytes 4616 | tf_op jit(solution)/shard_map/ppermute | solution.py:279
  65.7 0.4 collective-permute-start.4
  66.2 0.6 collective-permute-start.3
  66.8 0.0 collective-permute-done.5
  66.8 3.1 %collective-permute-done.4 = f32[1,384]{1,0:T(1,128)S(1)} collective-permute-done((f32[1,384]{1,0:T(1,128)S(1)}, f32[1,384]{1,0:T(1,128)S(1)}, u32[]{:S(2)}, u32[]{:S(2)}) %collective-permute-start.4) | collective-permute-done | bytes 1568 | tf_op jit(solution)/shard_map/ppermute | solution.py:279
  70.0 0.2 collective-permute-done.3
  70.1 5.6 %all-to-all-done.2 = f32[256,1,128]{2,1,0:T(1,128)S(1)} async-done(((f32[256,1,128]{2,1,0:T(1,128)}), f32[256,1,128]{2,1,0:T(1,128)S(1)}, u32[]{:S(2)}, u32[]{:S(2)}) %all-to-all-start.2) | async-done | bytes 131104 | tf_op jit(solution)/shard_map/all_to_all | solution.py:226
  75.7 2.8 %shard_map.68 = bf16[256,256]{1,0:T(8,128)(2,1)S(1)} custom-call(f32[256,128]{1,0:T(8,128)S(1)} %bitcast.22, f32[1,384]{1,0:T(1,128)S(1)} %multiply_add_fusion.extra_ref), custom_call_target="tpu_custom_call" | custom-call | tf_op jit(solution)/shard_map/pallas_call | solution.py:207
  78.6 2.1 %fusion.1 = bf16[1,256,4096]{2,1,0:T(8,128)(2,1)} fusion(bf16[256,256]{1,0:T(8,128)(2,1)S(1)} %shard_map.68, bf16[1,256,4096]{2,1,0:T(8,128)(2,1)S(1)} %copy-done.6, f32[4096]{0:T(1024)S(1)} %broadcast_multiply_fusion), kind=kOutput, calls=%fused_computation.4 | convolution fusion | flops 542113792 | bytes 4341760 | tf_op jit(solution)/shard_map/dot_general | solution.py:29
  (14 shorter events, 0.1 us)
Async XLA Ops:
  0.0 1.0 %copy-start = (bf16[1,1024,256]{2,1,0:T(8,128)(2,1)S(1)}, bf16[1,1024,256]{2,1,0:T(8,128)(2,1)}, u32[]{:S(2)}) copy-start(bf16[1,1024,256]{2,1,0:T(8,128)(2,1)} %param.7) | copy-start | bytes 1572868
  1.0 0.7 copy-start.1
  1.7 0.7 copy-start.3
  2.4 0.7 copy-start.4
  3.1 0.7 copy-start.5
  3.8 36.5 %copy-start.6 = (bf16[1,256,4096]{2,1,0:T(8,128)(2,1)S(1)}, bf16[1,256,4096]{2,1,0:T(8,128)(2,1)}, u32[]{:S(2)}) copy-start(bf16[1,256,4096]{2,1,0:T(8,128)(2,1)} %param.6) | copy-start | bytes 6291460
  6.3 21.2 %all-to-all-start = ((bf16[16,104,256]{2,1,0:T(8,128)(2,1)}), bf16[16,104,256]{2,1,0:T(8,128)(2,1)S(1)}, u32[]{:S(2)}, u32[]{:S(2)}) async-start(bf16[16,104,256]{2,1,0:T(8,128)(2,1)} %bitcast.3), calls=%async_computation | async-start | bytes 1703936 | tf_op jit(solution)/shard_map/all_to_all | solution.py:226
  13.5 37.1 %copy-start.2 = (s32[64,3]{0,1:T(4,128)S(1)}, s32[64,3]{0,1:T(4,128)}, u32[]{:S(2)}) copy-start(s32[64,3]{0,1:T(4,128)} %param.11) | copy-start | bytes 2308
  28.8 27.3 %all-to-all-start.1 = ((bf16[256,4,128]{2,1,0:T(4,128)(2,1)}), bf16[256,4,128]{2,1,0:T(4,128)(2,1)S(1)}, u32[]{:S(2)}, u32[]{:S(2)}) async-start(bf16[256,4,128]{2,1,0:T(4,128)(2,1)} %bitcast.4), calls=%async_computation.1 | async-start | bytes 524288 | tf_op jit(solution)/shard_map/all_to_all | solution.py:226
  40.7 22.1 %collective-permute-start = (f32[1,384]{1,0:T(1,128)S(1)}, f32[1,384]{1,0:T(1,128)S(1)}, u32[]{:S(2)}, u32[]{:S(2)}) collective-permute-start(f32[1,384]{1,0:T(1,128)S(1)} %get-tuple-element.13), channel_id=1, source_target_pairs={{0,16},{4,20},{8,24},{12,28},{16,32},{20,36},{24,40},{28,44},{32,4... | collective-permute-start | bytes 4616 | tf_op jit(solution)/shard_map/ppermute | solution.py:276
  43.4 19.4 %collective-permute-start.1 = (f32[1,384]{1,0:T(1,128)S(1)}, f32[1,384]{1,0:T(1,128)S(1)}, u32[]{:S(2)}, u32[]{:S(2)}) collective-permute-start(f32[1,384]{1,0:T(1,128)S(1)} %get-tuple-element.14), channel_id=1, source_target_pairs={{0,32},{4,36},{8,40},{12,44},{16,48},{20,52},{24,56},{28,60},{32,0... | collective-permute-start | bytes 4616 | tf_op jit(solution)/shard_map/ppermute | solution.py:276
  47.8 15.1 %collective-permute-start.2 = (f32[1,384]{1,0:T(1,128)S(1)}, f32[1,384]{1,0:T(1,128)S(1)}, u32[]{:S(2)}, u32[]{:S(2)}) collective-permute-start(f32[1,384]{1,0:T(1,128)S(1)} %get-tuple-element.15), channel_id=1, source_target_pairs={{0,48},{4,52},{8,56},{12,60},{16,0},{20,4},{24,8},{28,12},{32,16},... | collective-permute-start | bytes 4616 | tf_op jit(solution)/shard_map/ppermute | solution.py:276
  57.1 18.6 %all-to-all-start.2 = ((f32[256,1,128]{2,1,0:T(1,128)}), f32[256,1,128]{2,1,0:T(1,128)S(1)}, u32[]{:S(2)}, u32[]{:S(2)}) async-start(f32[256,1,128]{2,1,0:T(1,128)} %bitcast.7), calls=%async_computation.2 | async-start | bytes 262144 | tf_op jit(solution)/shard_map/all_to_all | solution.py:226
  62.9 3.9 %collective-permute-start.5 = (f32[1,384]{1,0:T(1,128)S(1)}, f32[1,384]{1,0:T(1,128)S(1)}, u32[]{:S(2)}, u32[]{:S(2)}) collective-permute-start(f32[1,384]{1,0:T(1,128)S(1)} %add_add_fusion), channel_id=1, source_target_pairs={{0,3},{1,0},{2,1},{3,2},{4,7},{5,4},{6,5},{7,6},{8,11},{9,8},{10,9... | collective-permute-start | bytes 4616 | tf_op jit(solution)/shard_map/ppermute | solution.py:279
  65.7 4.2 %collective-permute-start.4 = (f32[1,384]{1,0:T(1,128)S(1)}, f32[1,384]{1,0:T(1,128)S(1)}, u32[]{:S(2)}, u32[]{:S(2)}) collective-permute-start(f32[1,384]{1,0:T(1,128)S(1)} %add_add_fusion), channel_id=1, source_target_pairs={{0,2},{1,3},{2,0},{3,1},{4,6},{5,7},{6,4},{7,5},{8,10},{9,11},{10,... | collective-permute-start | bytes 4616 | tf_op jit(solution)/shard_map/ppermute | solution.py:279
  66.2 3.9 %collective-permute-start.3 = (f32[1,384]{1,0:T(1,128)S(1)}, f32[1,384]{1,0:T(1,128)S(1)}, u32[]{:S(2)}, u32[]{:S(2)}) collective-permute-start(f32[1,384]{1,0:T(1,128)S(1)} %add_add_fusion), channel_id=1, source_target_pairs={{0,1},{1,2},{2,3},{3,0},{4,5},{5,6},{6,7},{7,4},{8,9},{9,10},{10,1... | collective-permute-start | bytes 4616 | tf_op jit(solution)/shard_map/ppermute | solution.py:279

commit v3 on v2

--- a/solution.py
+++ b/solution.py
@@ -11,12 +11,13 @@
 NSTEPS = 4
 TAPER = 0.6
 DECAY = 0.5
-LANES = 128
+LANES, SUBLANES = 128, 8
 COLUMNS, PLANES, CORES = 4, 8, 2
 PAIR = 2
 GROUPS = PLANES // PAIR
 EXTRA = 8
 VMEM_LIMIT = 16 << 20
+FIRST_LIMIT = 62 << 20
 BF16 = jnp.bfloat16
 F32 = jnp.float32
 
@@ -124,58 +125,91 @@
             rows_ref[at + span : at + span + EXTRA, :] = extra[(start + k) * EXTRA : (start + k + 1) * EXTRA]
 
 
-def weight_kernel(levels, listed_ref, high_ref, low_ref):
-    size, columns = high_ref.shape
+def weight_kernel(listed_ref, high_ref, low_ref):
+    size = high_ref.shape[0]
     weight = split(weights_transposed(listed_ref[...]))
     regions = listed_ref.shape[1]
-    expand = onehot(iota((regions, size), 0) == iota((regions, size), 1) // levels)
+    expand = onehot(iota((regions, size), 0) == iota((regions, size), 1) // SUBLANES)
     rows = split(dot(weight[0], expand) + dot(weight[1], expand))
-    col = iota((regions, columns), 1)
-    x, z, core = region_parts(col // (levels * GROUPS))
-    owner = (x * PLANES + (col % GROUPS) * PAIR + z % PAIR) * CORES + core
-    spread = onehot(iota((regions, columns), 0) == owner)
+    at = iota((regions, size), 1) // SUBLANES
+    spread = onehot(iota((regions, size), 0) == region_at(at // GROUPS, at % GROUPS))
     over = ((0,), (0,))
     full = dot(rows[0], spread, over) + dot(rows[1], spread, over)
-    apart = jnp.abs(iota((size, columns), 0) % levels - iota((size, columns), 1) // GROUPS % levels)
-    factor = jnp.zeros((size, columns), F32)
-    for distance in range(levels):
-        factor = jnp.where(apart == distance, DECAY**distance, factor)
-    high, low = split(full * factor)
+    same = iota((size, size), 0) % SUBLANES == iota((size, size), 1) % SUBLANES
+    high, low = split(jnp.where(same, full, 0.0))
     high_ref[...] = high
     low_ref[...] = low
 
 
-def covariance_kernel(capacity, rows_ref, message_ref, sums_ref, scratch_ref):
+def covariance_kernel(capacity, rows_ref, message_ref, sums_ref):
     half = LANES
     members = rows_ref.shape[2]
+    places = message_ref.shape[0]
+    piece = members // places
     above = iota((half, half), 0) <= iota((half, half), 1)
     for group in range(GROUPS):
         rows = rows_ref[:, group * capacity : (group + 1) * capacity, :].reshape(-1, members)
         total = dot(rows, rows, ((0,), (0,)))
         corner = jnp.where(above, total[:half, :half], total[half:, half:])
-        packed = jnp.concatenate([corner, total[:half, half:]], axis=0)
-        scratch_ref[pl.ds(group, members, GROUPS), :] = packed
-    message_ref[...] = scratch_ref[...].astype(BF16)
+        packed = jnp.concatenate([corner, total[:half, half:]], axis=0).astype(BF16)
+        message_ref[:, group * piece : (group + 1) * piece, :] = packed.reshape(places, piece, LANES)
     span = GROUPS * capacity
     sums_ref[...] = jnp.sum(rows_ref[:, span : span + EXTRA, :].astype(F32), axis=0)
 
 
 def mix_kernel(message_ref, high_ref, low_ref, mixed_ref):
-    message = message_ref[...]
-    mixed_ref[...] = dot(high_ref[...], message) + dot(low_ref[...], message)
-
-
-def transform_kernel(packed_ref, extra_ref, transform_ref):
+    places, rows, _ = message_ref.shape
+    regions, piece, _ = mixed_ref.shape
+    message = message_ref[...].reshape(regions, piece, LANES)
+    parts = [
+        message[:, at : at + SUBLANES, :].reshape(regions * SUBLANES, LANES) for at in range(0, piece, SUBLANES)
+    ]
+    wide = jnp.concatenate(parts, axis=1)
+    mixed = (dot(high_ref[...], wide) + dot(low_ref[...], wide)).astype(BF16)
+    for part in range(len(parts)):
+        at = part * SUBLANES
+        block = mixed[:, part * LANES : (part + 1) * LANES]
+        mixed_ref[:, at : at + SUBLANES, :] = block.reshape(regions, SUBLANES, LANES)
+
+
+def gather_kernel(pieces_ref, extra_ref, own_ref, sent_ref):
+    regions, piece, _ = pieces_ref.shape
+    size = regions // GROUPS * piece
+    for place in range(regions // GROUPS):
+        total = pieces_ref[region_at(place, 0)].astype(F32)
+        for group in range(1, GROUPS):
+            total = total + pieces_ref[region_at(place, group)].astype(F32)
+        own_ref[place * piece : (place + 1) * piece, :] = total
+        sent_ref[place * piece : (place + 1) * piece, :] = total.astype(BF16)
+    extra = extra_ref[...]
+    high = extra.astype(BF16).astype(F32)
+    low = extra - high
+    rows = [value[:, at : at + LANES] for value in (high, low) for at in range(0, 3 * LANES, LANES)]
+    rows = jnp.concatenate(rows + [jnp.zeros((2, LANES), F32)], axis=0)
+    own_ref[size:, :] = rows
+    sent_ref[size:, :] = rows.astype(BF16)
+
+
+def transform_kernel(levels, level_ref, own_ref, *refs):
     half = LANES
     size = 2 * half
-    tri = packed_ref[:half, :]
+    transform_ref = refs[-1]
+    level = level_ref[0]
+    everything = own_ref[...]
+    for ahead in range(1, levels):
+        source = lax.rem(level + (levels - ahead), levels)
+        apart = jnp.abs(level - source)
+        factor = jnp.where(apart == 1, DECAY, jnp.where(apart == 2, DECAY**2, DECAY**3))
+        everything = everything + factor * refs[ahead - 1][...].astype(F32)
+    extra = everything[size : size + 3] + everything[size + 3 : size + 6]
+    tri = everything[:half]
     tri_t = tri.T
-    cross = packed_ref[half:, :]
+    cross = everything[half:size]
     row = iota((half, half), 0)
     col = iota((half, half), 1)
     first = jnp.where(row <= col, tri, tri_t)
     second = jnp.where(row > col, tri, tri_t)
-    second = jnp.where(row == col, extra_ref[:, size:], second)
+    second = jnp.where(row == col, extra[2:3], second)
     matrix = jnp.concatenate(
         [jnp.concatenate([first, cross], axis=1), jnp.concatenate([cross.T, second], axis=1)], axis=0
     )
@@ -197,20 +231,22 @@
         inverse_iter = dot3(correction, inverse_split)
     root = inverse_iter / jnp.sqrt(norm_scale)
     root_split = split(root)
-    innovation = jnp.broadcast_to(extra_ref[:, :size], (8, size))
+    innovation = jnp.concatenate([extra[0:1], extra[1:2]], axis=1)
+    innovation = jnp.broadcast_to(innovation, (SUBLANES, size))
     inner = dot3(split(innovation), root_split)
     mean_shift = dot3(split(inner), root_split)[0:1, :]
     transform_ref[...] = (math.sqrt(size - 1.0) * root + mean_shift).astype(BF16)
 
 
-def call(kernel, shapes, *args, scratch=()):
+def call(kernel, shapes, *args, scratch=(), limit=VMEM_LIMIT, scalars=0):
+    spaces = [pltpu.SMEM] * scalars + [pltpu.VMEM] * (len(args) - scalars)
     return pl.pallas_call(
         kernel,
         out_shape=shapes,
-        in_specs=[pl.BlockSpec(memory_space=pltpu.VMEM)] * len(args),
+        in_specs=[pl.BlockSpec(memory_space=space) for space in spaces],
         out_specs=jax.tree.map(lambda _: pl.BlockSpec(memory_space=pltpu.VMEM), shapes),
         scratch_shapes=scratch,
-        compiler_params=pltpu.CompilerParams(vmem_limit_bytes=VMEM_LIMIT),
+        compiler_params=pltpu.CompilerParams(vmem_limit_bytes=limit),
     )(*args)
 
 
@@ -235,7 +271,6 @@
     local_obs = obs_anomaly.shape[1]
     capacity = 3 * local_obs // (2 * regions)
     places = regions // GROUPS
-    devices = regions * levels
     owners = owner_region.reshape(1, local_obs)
     listed = neighbours.T
     shape = jax.ShapeDtypeStruct
@@ -247,21 +282,23 @@
         innovation,
         obs_anomaly[0],
         listed,
+        limit=FIRST_LIMIT,
     )
     near = [[region_at(place, group) for place in range(places)] for group in range(GROUPS)]
     routed = exchange(rows, "region", places, near)
+    piece = members // places
     high, low = call(
-        functools.partial(weight_kernel, levels),
-        (shape((devices, devices * GROUPS), BF16), shape((devices, devices * GROUPS), BF16)),
-        listed,
+        weight_kernel, (shape((regions * SUBLANES, regions * SUBLANES), BF16),) * 2, listed
     )
     message, sums = call(
         functools.partial(covariance_kernel, capacity),
-        (shape((members * GROUPS, LANES), BF16), shape((EXTRA, members), F32)),
+        (shape((places, GROUPS * piece, LANES), BF16), shape((EXTRA, members), F32)),
         routed,
-        scratch=[pltpu.VMEM((members * GROUPS, LANES), F32)],
-    )
-    message = exchange(message, ("region", "level"), devices).reshape(-1, LANES)
+    )
+    message = lax.all_to_all(message, "region", 0, 0, tiled=True, axis_index_groups=near)
+    mixed = call(mix_kernel, shape((regions, piece, LANES), BF16), message, high, low)
+    mixed, sums = lax.optimization_barrier((mixed, sums))
+    pieces = lax.all_to_all(mixed, "region", 0, 0, tiled=True)
 
     my_group = my_region // CORES % PLANES // PAIR
     diagonals = sums[GROUPS : GROUPS + GROUPS // 2].reshape(GROUPS, LANES)
@@ -274,16 +311,23 @@
             x, z, core = region_parts(region)
             pairs.append((region, (x * PLANES + (z + PAIR * ahead) % PLANES) * CORES + core))
         part = part + lax.ppermute(sent, "region", pairs)
-    extra = part
-    for ahead in range(1, levels):
-        arrived = lax.ppermute(part, "level", [(o, (o + ahead) % levels) for o in range(levels)])
-        apart = jnp.abs(my_level - (my_level - ahead) % levels)
-        factor = sum(DECAY**distance * (apart == distance).astype(F32) for distance in range(levels))
-        extra = extra + factor * arrived
-
-    mixed = call(mix_kernel, shape((devices, LANES), F32), message, high, low)
-    packed = exchange(mixed, ("region", "level"), devices).reshape(devices, LANES)
-    transposed = call(transform_kernel, shape((members, members), BF16), packed, extra)
+
+    height = members + SUBLANES
+    own, sent = call(
+        gather_kernel, (shape((height, LANES), F32), shape((height, LANES), BF16)), pieces, part
+    )
+    arrived = [
+        lax.ppermute(sent, "level", [(o, (o + ahead) % levels) for o in range(levels)])
+        for ahead in range(1, levels)
+    ]
+    transposed = call(
+        functools.partial(transform_kernel, levels),
+        shape((members, members), BF16),
+        my_level.astype(jnp.int32).reshape(1),
+        own,
+        *arrived,
+        scalars=1,
+    )
     return update_columns(ensemble[0], transposed)[None]
 
 

time: 81.1 us -> 74.4 us (0.917)
  blocking collectives: 0 us -> 21.2 us
  starting transfers between devices: 38.2 us -> 25.5 us
  waiting for transfers between devices: 27.3 us -> 15.1 us
  local copies, waits for them, and re-layouts: 3.81 us -> 0.03 us
  Pallas kernels: 8.64 us -> 9.56 us
    all_to_all x0 -> x1, blocking collectives: none -> 21.2 us  [exchange(): lax.all_to_all(blocks, axes, 0, 0, tiled=True, axis_index_groups=groups)]
    all_to_all x3 -> x2, waiting for transfers between devices: 23.9 us -> 7.55 us  [the longest x1 6.95 us: body(): lax.all_to_all(message, 'region', 0, 0, tiled=True, axis_index_groups=near)]
    all_to_all x3 -> x2, starting transfers between devices: 24.4 us -> 12.7 us  [the longest x1 9.25 us: body(): pieces = lax.all_to_all(mixed, 'region', 0, 0, tiled=True)]
    unnamed x14 -> x4, local copies, waits for them, and re-layouts: 3.79 us -> 0.01 us
    ppermute x3, waiting for transfers between devices: 0.01 us -> 2.14 us  [body(): part = part + lax.ppermute(sent, 'region', pairs)]
    ppermute x3, waiting for transfers between devices: 3.3 us -> 5.41 us  [body(): lax.ppermute(sent, 'level', [(o, (o + ahead) % levels) for o in range(lev...]
    ppermute x3, starting transfers between devices: 9.85 us -> 8.92 us  [body(): part = part + lax.ppermute(sent, 'region', pairs)]
    pallas_call x5 -> x6, Pallas kernels: 8.64 us -> 9.56 us  [call(): pl.pallas_call(kernel, out_shape=shapes, in_specs=[pl.BlockSpec(memory_sp...]
  transfers between devices with their start and end apart: 9 -> 8, of which waited for: 5 -> 6; matrix products, arithmetic and copies ran while one was open for 1% -> 1% of each run, Pallas kernels for 3% -> 1%
where the time goes in v3:
time: 74.4 us; the launch traced here: 74.1 us
  starting transfers between devices  25.5 us (34%)
  blocking collectives  21.2 us (28%)
  waiting for transfers between devices  15.1 us (20%)
  Pallas kernels  9.56 us (13%)
  matrix products  2.13 us (3%)
    all_to_all x1, blocking collectives, exchange(): lax.all_to_all(blocks, axes, 0, 0, tiled=True, axis_index_groups=groups)  21.2 us
    pallas_call x6, Pallas kernels, call(): pl.pallas_call(kernel, out_shape=shapes, in_specs=[pl.BlockSpec(memory_sp...  9.56 us
    all_to_all x1, starting transfers between devices, body(): pieces = lax.all_to_all(mixed, 'region', 0, 0, tiled=True)  9.25 us
    ppermute x3, starting transfers between devices, body(): part = part + lax.ppermute(sent, 'region', pairs)  8.92 us
    all_to_all x1, waiting for transfers between devices, body(): lax.all_to_all(message, 'region', 0, 0, tiled=True, axis_index_groups=near)  6.95 us
    ppermute x3, waiting for transfers between devices, body(): lax.ppermute(sent, 'level', [(o, (o + ahead) % levels) for o in range(lev...  5.41 us
    ppermute x3, starting transfers between devices, body(): lax.ppermute(sent, 'level', [(o, (o + ahead) % levels) for o in range(lev...  3.85 us
    all_to_all x1, starting transfers between devices, body(): lax.all_to_all(message, 'region', 0, 0, tiled=True, axis_index_groups=near)  3.49 us
  transfers between devices with their start and end apart: 8, of which 6 were waited for; matrix products, arithmetic and copies ran while one was open for 1% of the time, Pallas kernels for 1%

profile of v3, /device:TPU:1, one launch (start us, length us, event | category | flops | bytes accessed | tf_op | source)
XLA Modules:
  0.0 74.1 jit_solution(16714927323255185624)
XLA Ops:
  0.0 0.0 copy-start
  0.0 3.6 %shard_map.64 = bf16[1664,256]{1,0:T(8,128)(2,1)} custom-call(s32[1,1024]{1,0:T(1,128)} %bitcast.19, bf16[1,1024]{1,0:T(2,128)(2,1)} %precision_ref.1, bf16[1,1024]{1,0:T(2,128)(2,1)} %innovation_ref.1, bf16[1024,256]{1,0:T(8,128)(2,1)} %bitcast.18, s32[3,64]{1,0:T(4,128)} %bitcast.15), custom_call_target="tpu_custom_call" | custom-call | tf_op jit(solution)/shard_map/pallas_call | solution.py:243
  3.6 21.2 %all_to_all.15.rows_ref = bf16[16,104,256]{2,1,0:T(8,128)(2,1)S(1)} all-to-all(bf16[16,104,256]{2,1,0:T(8,128)(2,1)} %bitcast.17), channel_id=1, replica_groups={{0,64,128,192,8,72,136,200,4,68,132,196,12,76,140,204},{16,80,144,208,2..., dimensions={0} | all-to-all | bytes 1703936 | tf_op jit(solution)/shard_map/all_to_all | solution.py:262
  24.8 0.0 copy-start.1
  24.8 1.2 %shard_map.65 = (bf16[16,64,128]{2,1,0:T(8,128)(2,1)}, f32[8,256]{1,0:T(8,128)S(1)}) custom-call(bf16[16,104,256]{2,1,0:T(8,128)(2,1)S(1)} %all_to_all.15.rows_ref), custom_call_target="tpu_custom_call" | custom-call | tf_op jit(solution)/shard_map/pallas_call | solution.py:243
  26.0 3.5 %all-to-all-start.1 = ((bf16[16,64,128]{2,1,0:T(8,128)(2,1)}), bf16[16,64,128]{2,1,0:T(8,128)(2,1)S(1)}, u32[]{:S(2)}, u32[]{:S(2)}) async-start(bf16[16,64,128]{2,1,0:T(8,128)(2,1)} %get-tuple-element.13), calls=%async_computation.1 | async-start | bytes 524288 | tf_op jit(solution)/shard_map/all_to_all | solution.py:298
  29.6 0.0 copy-done
  29.6 0.7 shard_map.66
  30.3 7.0 %all-to-all-done.1.message_ref = bf16[16,64,128]{2,1,0:T(8,128)(2,1)S(1)} async-done(((bf16[16,64,128]{2,1,0:T(8,128)(2,1)}), bf16[16,64,128]{2,1,0:T(8,128)(2,1)S(1)}, u32[]{:S(2)}, u32[]{:S(2)}) %all-to-all-start.1) | async-done | bytes 262176 | tf_op jit(solution)/shard_map/all_to_all | solution.py:298
  37.3 1.1 %shard_map.67 = bf16[64,16,128]{2,1,0:T(8,128)(2,1)} custom-call(bf16[16,64,128]{2,1,0:T(8,128)(2,1)S(1)} %all-to-all-done.1.message_ref, bf16[512,512]{1,0:T(8,128)(2,1)S(1)} %get-tuple-element.14.high_ref, bf16[512,512]{1,0:T(8,128)(2,1)S(1)} %get-tuple-element.15.low_ref), custom_call_target="tpu_custom_call" | custom-call | tf_op jit(solution)/shard_map/pallas_call | solution.py:243
  38.4 9.2 %all-to-all-start.2 = ((bf16[64,16,128]{2,1,0:T(8,128)(2,1)}), bf16[64,16,128]{2,1,0:T(8,128)(2,1)S(1)}, u32[]{:S(2)}, u32[]{:S(2)}) async-start(bf16[64,16,128]{2,1,0:T(8,128)(2,1)} %shard_map.67), calls=%async_computation.2 | async-start | bytes 524288 | tf_op jit(solution)/shard_map/all_to_all | solution.py:301
  47.7 2.3 %collective-permute-start = (f32[1,384]{1,0:T(1,128)S(1)}, f32[1,384]{1,0:T(1,128)S(1)}, u32[]{:S(2)}, u32[]{:S(2)}) collective-permute-start(f32[1,384]{1,0:T(1,128)S(1)} %get-tuple-element.21), channel_id=1, source_target_pairs={{0,16},{4,20},{8,24},{12,28},{16,32},{20,36},{24,40},{28,44},{32,4... | collective-permute-start | bytes 4616 | tf_op jit(solution)/shard_map/ppermute | solution.py:313
  50.0 3.3 %collective-permute-start.1 = (f32[1,384]{1,0:T(1,128)S(1)}, f32[1,384]{1,0:T(1,128)S(1)}, u32[]{:S(2)}, u32[]{:S(2)}) collective-permute-start(f32[1,384]{1,0:T(1,128)S(1)} %get-tuple-element.22), channel_id=1, source_target_pairs={{0,32},{4,36},{8,40},{12,44},{16,48},{20,52},{24,56},{28,60},{32,0... | collective-permute-start | bytes 4616 | tf_op jit(solution)/shard_map/ppermute | solution.py:313
  53.3 3.3 %collective-permute-start.2 = (f32[1,384]{1,0:T(1,128)S(1)}, f32[1,384]{1,0:T(1,128)S(1)}, u32[]{:S(2)}, u32[]{:S(2)}) collective-permute-start(f32[1,384]{1,0:T(1,128)S(1)} %get-tuple-element.23), channel_id=1, source_target_pairs={{0,48},{4,52},{8,56},{12,60},{16,0},{20,4},{24,8},{28,12},{32,16},... | collective-permute-start | bytes 4616 | tf_op jit(solution)/shard_map/ppermute | solution.py:313
  56.6 0.0 copy-done.1
  56.6 0.3 convert_reduce_fusion
  57.0 0.0 collective-permute-done
  57.0 2.1 %collective-permute-done.1 = f32[1,384]{1,0:T(1,128)S(1)} collective-permute-done((f32[1,384]{1,0:T(1,128)S(1)}, f32[1,384]{1,0:T(1,128)S(1)}, u32[]{:S(2)}, u32[]{:S(2)}) %collective-permute-start.1) | collective-permute-done | bytes 1568 | tf_op jit(solution)/shard_map/ppermute | solution.py:313
  59.1 0.0 collective-permute-done.2
  59.1 0.6 all-to-all-done.2.pieces_ref
  59.8 2.8 %collective-permute-start.5 = (bf16[264,128]{1,0:T(8,128)(2,1)S(1)}, bf16[264,128]{1,0:T(8,128)(2,1)S(1)}, u32[]{:S(2)}, u32[]{:S(2)}) collective-permute-start(bf16[264,128]{1,0:T(8,128)(2,1)S(1)} %get-tuple-element.20), channel_id=1, source_target_pairs={{0,3},{1,0},{2,1},{3,2},{4,7},{5,4},{6,5},{7,6},{8,11},{9,8},{10,9... | collective-permute-start | bytes 202760 | tf_op jit(solution)/shard_map/ppermute | solution.py:320
  62.6 0.3 collective-permute-start.4
  62.9 0.7 collective-permute-start.3
  63.6 0.3 collective-permute-done.5.refs_2_
  63.9 3.4 %collective-permute-done.4.refs_1_ = bf16[264,128]{1,0:T(8,128)(2,1)S(1)} collective-permute-done((bf16[264,128]{1,0:T(8,128)(2,1)S(1)}, bf16[264,128]{1,0:T(8,128)(2,1)S(1)}, u32[]{:S(2)}, u32[]{:S(2)}) %collective-permute-start.4) | collective-permute-done | bytes 67616 | tf_op jit(solution)/shard_map/ppermute | solution.py:320
  67.3 1.7 %collective-permute-done.3.refs_0_ = bf16[264,128]{1,0:T(8,128)(2,1)S(1)} collective-permute-done((bf16[264,128]{1,0:T(8,128)(2,1)S(1)}, bf16[264,128]{1,0:T(8,128)(2,1)S(1)}, u32[]{:S(2)}, u32[]{:S(2)}) %collective-permute-start.3) | collective-permute-done | bytes 67616 | tf_op jit(solution)/shard_map/ppermute | solution.py:320
  69.1 2.9 %shard_map.69 = bf16[256,256]{1,0:T(8,128)(2,1)S(1)} custom-call(s32[1]{0:T(128)} %bitcast.level_ref, f32[264,128]{1,0:T(8,128)S(1)} %get-tuple-element.19.own_ref, bf16[264,128]{1,0:T(8,128)(2,1)S(1)} %collective-permute-done.3.refs_0_, bf16[264,128]{1,0:T(8,128)(2,1)S(1)} %collective-permute-done.4.refs_1_, bf16[264,128]{1,0:T(8,128)(2,1)S(1)} %collective-permute-done.5.refs_2_), custom_call_target="tpu_custom_call" | custom-call | tf_op jit(solution)/shard_map/pallas_call | solution.py:243
  71.9 2.1 %fusion.1 = bf16[1,256,4096]{2,1,0:T(8,128)(2,1)} fusion(bf16[256,256]{1,0:T(8,128)(2,1)S(1)} %shard_map.69, bf16[1,256,4096]{2,1,0:T(8,128)(2,1)S(1)} %copy-done.1, f32[4096]{0:T(1024)S(1)} %broadcast_multiply_fusion), kind=kOutput, calls=%fused_computation.4 | convolution fusion | flops 542113792 | bytes 4341760 | tf_op jit(solution)/shard_map/dot_general | solution.py:30
  (7 shorter events, 0.1 us)
Async XLA Ops:
  0.0 29.6 %copy-start = (s32[64,3]{0,1:T(4,128)S(1)}, s32[64,3]{0,1:T(4,128)}, u32[]{:S(2)}) copy-start(s32[64,3]{0,1:T(4,128)} %param.11) | copy-start | bytes 2308
  24.8 31.8 %copy-start.1 = (bf16[1,256,4096]{2,1,0:T(8,128)(2,1)S(1)}, bf16[1,256,4096]{2,1,0:T(8,128)(2,1)}, u32[]{:S(2)}) copy-start(bf16[1,256,4096]{2,1,0:T(8,128)(2,1)} %param.6) | copy-start | bytes 6291460
  26.0 11.2 %all-to-all-start.1 = ((bf16[16,64,128]{2,1,0:T(8,128)(2,1)}), bf16[16,64,128]{2,1,0:T(8,128)(2,1)S(1)}, u32[]{:S(2)}, u32[]{:S(2)}) async-start(bf16[16,64,128]{2,1,0:T(8,128)(2,1)} %get-tuple-element.13), calls=%async_computation.1 | async-start | bytes 524288 | tf_op jit(solution)/shard_map/all_to_all | solution.py:298
  38.4 21.3 %all-to-all-start.2 = ((bf16[64,16,128]{2,1,0:T(8,128)(2,1)}), bf16[64,16,128]{2,1,0:T(8,128)(2,1)S(1)}, u32[]{:S(2)}, u32[]{:S(2)}) async-start(bf16[64,16,128]{2,1,0:T(8,128)(2,1)} %shard_map.67), calls=%async_computation.2 | async-start | bytes 524288 | tf_op jit(solution)/shard_map/all_to_all | solution.py:301
  47.7 9.3 %collective-permute-start = (f32[1,384]{1,0:T(1,128)S(1)}, f32[1,384]{1,0:T(1,128)S(1)}, u32[]{:S(2)}, u32[]{:S(2)}) collective-permute-start(f32[1,384]{1,0:T(1,128)S(1)} %get-tuple-element.21), channel_id=1, source_target_pairs={{0,16},{4,20},{8,24},{12,28},{16,32},{20,36},{24,40},{28,44},{32,4... | collective-permute-start | bytes 4616 | tf_op jit(solution)/shard_map/ppermute | solution.py:313
  50.0 9.1 %collective-permute-start.1 = (f32[1,384]{1,0:T(1,128)S(1)}, f32[1,384]{1,0:T(1,128)S(1)}, u32[]{:S(2)}, u32[]{:S(2)}) collective-permute-start(f32[1,384]{1,0:T(1,128)S(1)} %get-tuple-element.22), channel_id=1, source_target_pairs={{0,32},{4,36},{8,40},{12,44},{16,48},{20,52},{24,56},{28,60},{32,0... | collective-permute-start | bytes 4616 | tf_op jit(solution)/shard_map/ppermute | solution.py:313
  53.3 5.8 %collective-permute-start.2 = (f32[1,384]{1,0:T(1,128)S(1)}, f32[1,384]{1,0:T(1,128)S(1)}, u32[]{:S(2)}, u32[]{:S(2)}) collective-permute-start(f32[1,384]{1,0:T(1,128)S(1)} %get-tuple-element.23), channel_id=1, source_target_pairs={{0,48},{4,52},{8,56},{12,60},{16,0},{20,4},{24,8},{28,12},{32,16},... | collective-permute-start | bytes 4616 | tf_op jit(solution)/shard_map/ppermute | solution.py:313
  59.8 4.2 %collective-permute-start.5 = (bf16[264,128]{1,0:T(8,128)(2,1)S(1)}, bf16[264,128]{1,0:T(8,128)(2,1)S(1)}, u32[]{:S(2)}, u32[]{:S(2)}) collective-permute-start(bf16[264,128]{1,0:T(8,128)(2,1)S(1)} %get-tuple-element.20), channel_id=1, source_target_pairs={{0,3},{1,0},{2,1},{3,2},{4,7},{5,4},{6,5},{7,6},{8,11},{9,8},{10,9... | collective-permute-start | bytes 202760 | tf_op jit(solution)/shard_map/ppermute | solution.py:320
  62.6 4.7 %collective-permute-start.4 = (bf16[264,128]{1,0:T(8,128)(2,1)S(1)}, bf16[264,128]{1,0:T(8,128)(2,1)S(1)}, u32[]{:S(2)}, u32[]{:S(2)}) collective-permute-start(bf16[264,128]{1,0:T(8,128)(2,1)S(1)} %get-tuple-element.20), channel_id=1, source_target_pairs={{0,2},{1,3},{2,0},{3,1},{4,6},{5,7},{6,4},{7,5},{8,10},{9,11},{10,... | collective-permute-start | bytes 202760 | tf_op jit(solution)/shard_map/ppermute | solution.py:320
  62.9 6.1 %collective-permute-start.3 = (bf16[264,128]{1,0:T(8,128)(2,1)S(1)}, bf16[264,128]{1,0:T(8,128)(2,1)S(1)}, u32[]{:S(2)}, u32[]{:S(2)}) collective-permute-start(bf16[264,128]{1,0:T(8,128)(2,1)S(1)} %get-tuple-element.20), channel_id=1, source_target_pairs={{0,1},{1,2},{2,3},{3,0},{4,5},{5,6},{6,7},{7,4},{8,9},{9,10},{10,1... | collective-permute-start | bytes 202760 | tf_op jit(solution)/shard_map/ppermute | solution.py:320

commit v4 on v3

--- a/solution.py
+++ b/solution.py
@@ -15,6 +15,7 @@
 COLUMNS, PLANES, CORES = 4, 8, 2
 PAIR = 2
 GROUPS = PLANES // PAIR
+WIDTH = 512
 EXTRA = 8
 VMEM_LIMIT = 16 << 20
 FIRST_LIMIT = 62 << 20
@@ -154,7 +155,12 @@
         packed = jnp.concatenate([corner, total[:half, half:]], axis=0).astype(BF16)
         message_ref[:, group * piece : (group + 1) * piece, :] = packed.reshape(places, piece, LANES)
     span = GROUPS * capacity
-    sums_ref[...] = jnp.sum(rows_ref[:, span : span + EXTRA, :].astype(F32), axis=0)
+    sums = jnp.sum(rows_ref[:, span : span + EXTRA, :].astype(F32), axis=0)
+    for group in range(GROUPS):
+        at, inner = GROUPS + group // 2, group % 2
+        diagonal = sums[at : at + 1, inner * half : (inner + 1) * half]
+        row = jnp.concatenate([sums[group : group + 1], diagonal], axis=1)
+        sums_ref[group // 2, inner : inner + 1, :] = row
 
 
 def mix_kernel(message_ref, high_ref, low_ref, mixed_ref):
@@ -190,10 +196,19 @@
     sent_ref[size:, :] = rows.astype(BF16)
 
 
-def transform_kernel(levels, level_ref, own_ref, *refs):
+def anomaly_kernel(ensemble_ref, average_ref, anomaly_ref):
+    members, columns = ensemble_ref.shape
+    for at in range(0, columns, WIDTH):
+        block = ensemble_ref[:, at : at + WIDTH].astype(F32)
+        average = jnp.sum(block, axis=0, keepdims=True) * (1.0 / members)
+        average_ref[:, at : at + WIDTH] = average
+        anomaly_ref[:, at : at + WIDTH] = (block - average).astype(BF16)
+
+
+def transform_kernel(levels, level_ref, average_ref, anomaly_ref, own_ref, *refs):
     half = LANES
     size = 2 * half
-    transform_ref = refs[-1]
+    output_ref, block_ref, semaphores = refs[-3:]
     level = level_ref[0]
     everything = own_ref[...]
     for ahead in range(1, levels):
@@ -235,26 +250,31 @@
     innovation = jnp.broadcast_to(innovation, (SUBLANES, size))
     inner = dot3(split(innovation), root_split)
     mean_shift = dot3(split(inner), root_split)[0:1, :]
-    transform_ref[...] = (math.sqrt(size - 1.0) * root + mean_shift).astype(BF16)
-
-
-def call(kernel, shapes, *args, scratch=(), limit=VMEM_LIMIT, scalars=0):
+    transform = (math.sqrt(size - 1.0) * root + mean_shift).astype(BF16)
+    copies = []
+    for step, at in enumerate(range(0, anomaly_ref.shape[1], WIDTH)):
+        span = slice(at, at + WIDTH)
+        combined = dot(transform, anomaly_ref[:, span]) + average_ref[:, span]
+        block_ref[:, span] = combined.astype(BF16)
+        copy = pltpu.make_async_copy(
+            block_ref.at[:, span], output_ref.at[:, span], semaphores.at[step]
+        )
+        copy.start()
+        copies.append(copy)
+    for copy in copies:
+        copy.wait()
+
+
+def call(kernel, shapes, *args, scratch=(), limit=VMEM_LIMIT, scalars=0, space=pltpu.VMEM):
     spaces = [pltpu.SMEM] * scalars + [pltpu.VMEM] * (len(args) - scalars)
     return pl.pallas_call(
         kernel,
         out_shape=shapes,
-        in_specs=[pl.BlockSpec(memory_space=space) for space in spaces],
-        out_specs=jax.tree.map(lambda _: pl.BlockSpec(memory_space=pltpu.VMEM), shapes),
+        in_specs=[pl.BlockSpec(memory_space=where) for where in spaces],
+        out_specs=jax.tree.map(lambda _: pl.BlockSpec(memory_space=space), shapes),
         scratch_shapes=scratch,
         compiler_params=pltpu.CompilerParams(vmem_limit_bytes=limit),
     )(*args)
-
-
-def update_columns(column_block, transposed):
-    average = jnp.mean(column_block.astype(F32), axis=0)
-    anomaly = (column_block.astype(F32) - average[None, :]).astype(BF16)
-    combined = dot(transposed, anomaly)
-    return (combined + average[None, :]).astype(BF16)
 
 
 def exchange(message, axes, count, groups=None):
@@ -292,25 +312,31 @@
     )
     message, sums = call(
         functools.partial(covariance_kernel, capacity),
-        (shape((places, GROUPS * piece, LANES), BF16), shape((EXTRA, members), F32)),
+        (shape((places, GROUPS * piece, LANES), BF16), shape((2, GROUPS // 2, members + LANES), F32)),
         routed,
     )
     message = lax.all_to_all(message, "region", 0, 0, tiled=True, axis_index_groups=near)
-    mixed = call(mix_kernel, shape((regions, piece, LANES), BF16), message, high, low)
-    mixed, sums = lax.optimization_barrier((mixed, sums))
-    pieces = lax.all_to_all(mixed, "region", 0, 0, tiled=True)
-
-    my_group = my_region // CORES % PLANES // PAIR
-    diagonals = sums[GROUPS : GROUPS + GROUPS // 2].reshape(GROUPS, LANES)
-    parts = jnp.concatenate([sums[:GROUPS], diagonals], axis=1)
-    part = lax.dynamic_slice_in_dim(parts, my_group, 1, 0)
-    for ahead in range(1, GROUPS):
-        sent = lax.dynamic_slice_in_dim(parts, (my_group + ahead) % GROUPS, 1, 0)
+
+    def other_group(step):
         pairs = []
         for region in range(regions):
             x, z, core = region_parts(region)
-            pairs.append((region, (x * PLANES + (z + PAIR * ahead) % PLANES) * CORES + core))
-        part = part + lax.ppermute(sent, "region", pairs)
+            pairs.append((region, (x * PLANES + (z ^ (step * PAIR))) * CORES + core))
+        return pairs
+
+    my_group = my_region // CORES % PLANES // PAIR
+    near_half, in_half = my_group // 2, my_group % 2
+    swapped = lax.ppermute(
+        lax.dynamic_index_in_dim(sums, 1 - near_half, 0, keepdims=False), "region", other_group(2)
+    )
+    kept = lax.dynamic_index_in_dim(sums, near_half, 0, keepdims=False) + swapped
+    mixed = call(mix_kernel, shape((regions, piece, LANES), BF16), message, high, low)
+    mixed, kept = lax.optimization_barrier((mixed, kept))
+    pieces = lax.all_to_all(mixed, "region", 0, 0, tiled=True)
+    swapped = lax.ppermute(
+        lax.dynamic_slice_in_dim(kept, 1 - in_half, 1, 0), "region", other_group(1)
+    )
+    part = lax.dynamic_slice_in_dim(kept, in_half, 1, 0) + swapped
 
     height = members + SUBLANES
     own, sent = call(
@@ -320,15 +346,26 @@
         lax.ppermute(sent, "level", [(o, (o + ahead) % levels) for o in range(levels)])
         for ahead in range(1, levels)
     ]
-    transposed = call(
+    columns = ensemble.shape[2]
+    average, anomaly = call(
+        anomaly_kernel, (shape((1, columns), F32), shape((members, columns), BF16)), ensemble[0]
+    )
+    analysis = call(
         functools.partial(transform_kernel, levels),
-        shape((members, members), BF16),
+        shape((members, columns), BF16),
         my_level.astype(jnp.int32).reshape(1),
+        average,
+        anomaly,
         own,
         *arrived,
         scalars=1,
-    )
-    return update_columns(ensemble[0], transposed)[None]
+        space=pl.ANY,
+        scratch=[
+            pltpu.VMEM((members, columns), BF16),
+            pltpu.SemaphoreType.DMA((columns // WIDTH,)),
+        ],
+    )
+    return analysis[None]
 
 
 def solution(mesh):

time: 74.4 us -> 75.4 us (1.013)
  Pallas kernels: 9.56 us -> 11.9 us
  matrix products: 2.13 us -> 0 us
  waiting for transfers between devices: 15.1 us -> 17.2 us
  starting transfers between devices: 25.5 us -> 24.7 us
    all_to_all x1, waiting for transfers between devices: 6.95 us -> 0.01 us  [body(): lax.all_to_all(message, 'region', 0, 0, tiled=True, axis_index_groups=near)]
    ppermute x3 -> x2, waiting for transfers between devices: 2.14 us -> 7.36 us  [the longest x1 4.44 us: body(): lax.ppermute(lax.dynamic_slice_in_dim(kept, 1 - in_half, 1, 0), 'region',...]
    all_to_all x1, waiting for transfers between devices: 0.6 us -> 5.16 us  [body(): pieces = lax.all_to_all(mixed, 'region', 0, 0, tiled=True)]
    pallas_call x6 -> x7, Pallas kernels: 9.56 us -> 11.9 us  [call(): pl.pallas_call(kernel, out_shape=shapes, in_specs=[pl.BlockSpec(memory_sp...]
    dot_general x1 -> x0, matrix products: 2.13 us -> none  [dot(): lax.dot_general(left, right, (dims, ((), ())), preferred_element_type=F32)]
    ppermute x3 -> x2, starting transfers between devices: 8.92 us -> 8.43 us  [the longest x1 6.1 us: body(): lax.ppermute(lax.dynamic_index_in_dim(sums, 1 - near_half, 0, keepdims=Fa...]
  transfers between devices with their start and end apart: 8 -> 7, of which waited for: 6 -> 5; matrix products, arithmetic and copies ran while one was open for 1% -> 0% of each run, Pallas kernels for 1% -> 2%
where the time goes in v4:
time: 75.4 us; the launch traced here: 75.1 us
  starting transfers between devices  24.7 us (33%)
  blocking collectives  21.2 us (28%)
  waiting for transfers between devices  17.2 us (23%)
  Pallas kernels  11.9 us (16%)
    all_to_all x1, blocking collectives, exchange(): lax.all_to_all(blocks, axes, 0, 0, tiled=True, axis_index_groups=groups)  21.2 us
    pallas_call x7, Pallas kernels, call(): pl.pallas_call(kernel, out_shape=shapes, in_specs=[pl.BlockSpec(memory_sp...  11.9 us
    all_to_all x1, starting transfers between devices, body(): pieces = lax.all_to_all(mixed, 'region', 0, 0, tiled=True)  8.87 us
    ppermute x1, starting transfers between devices, body(): lax.ppermute(lax.dynamic_index_in_dim(sums, 1 - near_half, 0, keepdims=Fa...  6.1 us
    all_to_all x1, waiting for transfers between devices, body(): pieces = lax.all_to_all(mixed, 'region', 0, 0, tiled=True)  5.16 us
    ppermute x3, waiting for transfers between devices, body(): lax.ppermute(sent, 'level', [(o, (o + ahead) % levels) for o in range(lev...  4.67 us
    ppermute x1, waiting for transfers between devices, body(): lax.ppermute(lax.dynamic_slice_in_dim(kept, 1 - in_half, 1, 0), 'region',...  4.44 us
    ppermute x3, starting transfers between devices, body(): lax.ppermute(sent, 'level', [(o, (o + ahead) % levels) for o in range(lev...  3.85 us
  transfers between devices with their start and end apart: 7, of which 5 were waited for; matrix products, arithmetic and copies ran while one was open for 0% of the time, Pallas kernels for 2%

profile of v4, /device:TPU:1, one launch (start us, length us, event | category | flops | bytes accessed | tf_op | source)
XLA Modules:
  0.0 75.1 jit_solution(3845139602396846206)
XLA Ops:
  0.0 0.0 copy-start.1
  0.0 3.6 %shard_map.65 = bf16[1664,256]{1,0:T(8,128)(2,1)} custom-call(s32[1,1024]{1,0:T(1,128)} %bitcast.16, bf16[1,1024]{1,0:T(2,128)(2,1)} %precision_ref.1, bf16[1,1024]{1,0:T(2,128)(2,1)} %innovation_ref.1, bf16[1024,256]{1,0:T(8,128)(2,1)} %bitcast.15, s32[3,64]{1,0:T(4,128)} %bitcast.12), custom_call_target="tpu_custom_call" | custom-call | tf_op jit(solution)/shard_map/pallas_call | solution.py:270
  3.6 21.2 %all_to_all.15.rows_ref = bf16[16,104,256]{2,1,0:T(8,128)(2,1)S(1)} all-to-all(bf16[16,104,256]{2,1,0:T(8,128)(2,1)} %bitcast.14), channel_id=1, replica_groups={{0,64,128,192,8,72,136,200,4,68,132,196,12,76,140,204},{16,80,144,208,2..., dimensions={0} | all-to-all | bytes 1703936 | tf_op jit(solution)/shard_map/all_to_all | solution.py:282
  24.8 0.0 copy-start
  24.8 1.2 %shard_map.66 = (bf16[16,64,128]{2,1,0:T(8,128)(2,1)}, f32[2,2,384]{2,1,0:T(2,128)S(1)}) custom-call(bf16[16,104,256]{2,1,0:T(8,128)(2,1)S(1)} %all_to_all.15.rows_ref), custom_call_target="tpu_custom_call" | custom-call | tf_op jit(solution)/shard_map/pallas_call | solution.py:270
  26.0 3.5 %all-to-all-start.1 = ((bf16[16,64,128]{2,1,0:T(8,128)(2,1)}), bf16[16,64,128]{2,1,0:T(8,128)(2,1)S(1)}, u32[]{:S(2)}, u32[]{:S(2)}) async-start(bf16[16,64,128]{2,1,0:T(8,128)(2,1)} %get-tuple-element.17), calls=%async_computation.1 | async-start | bytes 524288 | tf_op jit(solution)/shard_map/all_to_all | solution.py:318
  29.6 6.1 %collective-permute-start = (f32[2,384]{1,0:T(2,128)S(1)}, f32[2,384]{1,0:T(2,128)S(1)}, u32[]{:S(2)}, u32[]{:S(2)}) collective-permute-start(f32[2,384]{1,0:T(2,128)S(1)} %dynamic-slice_bitcast_fusion), channel_id=1, source_target_pairs={{0,32},{4,36},{8,40},{12,44},{16,48},{20,52},{24,56},{28,60},{32,0... | collective-permute-start | bytes 9224 | tf_op jit(solution)/shard_map/ppermute | solution.py:329
  35.7 0.0 copy-done.1
  35.7 0.7 shard_map.67
  36.4 2.9 %collective-permute-done = f32[2,384]{1,0:T(2,128)S(1)} collective-permute-done((f32[2,384]{1,0:T(2,128)S(1)}, f32[2,384]{1,0:T(2,128)S(1)}, u32[]{:S(2)}, u32[]{:S(2)}) %collective-permute-start) | collective-permute-done | bytes 3104 | tf_op jit(solution)/shard_map/ppermute | solution.py:329
  39.3 0.0 all-to-all-done.1.message_ref
  39.3 1.1 %shard_map.68 = bf16[64,16,128]{2,1,0:T(8,128)(2,1)} custom-call(bf16[16,64,128]{2,1,0:T(8,128)(2,1)S(1)} %all-to-all-done.1.message_ref, bf16[512,512]{1,0:T(8,128)(2,1)S(1)} %get-tuple-element.18.high_ref, bf16[512,512]{1,0:T(8,128)(2,1)S(1)} %get-tuple-element.19.low_ref), custom_call_target="tpu_custom_call" | custom-call | tf_op jit(solution)/shard_map/pallas_call | solution.py:270
  40.4 8.9 %all-to-all-start.2 = ((bf16[64,16,128]{2,1,0:T(8,128)(2,1)}), bf16[64,16,128]{2,1,0:T(8,128)(2,1)S(1)}, u32[]{:S(2)}, u32[]{:S(2)}) async-start(bf16[64,16,128]{2,1,0:T(8,128)(2,1)} %shard_map.68), calls=%async_computation.2 | async-start | bytes 524288 | tf_op jit(solution)/shard_map/all_to_all | solution.py:335
  49.4 2.3 %collective-permute-start.1 = (f32[1,384]{1,0:T(1,128)S(1)}, f32[1,384]{1,0:T(1,128)S(1)}, u32[]{:S(2)}, u32[]{:S(2)}) collective-permute-start(f32[1,384]{1,0:T(1,128)S(1)} %constant_dynamic-slice_fusion), channel_id=1, source_target_pairs={{0,16},{4,20},{8,24},{12,28},{16,0},{20,4},{24,8},{28,12},{32,48},... | collective-permute-start | bytes 4616 | tf_op jit(solution)/shard_map/ppermute | solution.py:336
  51.7 4.4 %collective-permute-done.1 = f32[1,384]{1,0:T(1,128)S(1)} collective-permute-done((f32[1,384]{1,0:T(1,128)S(1)}, f32[1,384]{1,0:T(1,128)S(1)}, u32[]{:S(2)}, u32[]{:S(2)}) %collective-permute-start.1) | collective-permute-done | bytes 1568 | tf_op jit(solution)/shard_map/ppermute | solution.py:336
  56.1 5.2 %all-to-all-done.2.pieces_ref = bf16[64,16,128]{2,1,0:T(8,128)(2,1)S(1)} async-done(((bf16[64,16,128]{2,1,0:T(8,128)(2,1)}), bf16[64,16,128]{2,1,0:T(8,128)(2,1)S(1)}, u32[]{:S(2)}, u32[]{:S(2)}) %all-to-all-start.2) | async-done | bytes 262176 | tf_op jit(solution)/shard_map/all_to_all | solution.py:335
  61.4 2.8 %collective-permute-start.4 = (bf16[264,128]{1,0:T(8,128)(2,1)S(1)}, bf16[264,128]{1,0:T(8,128)(2,1)S(1)}, u32[]{:S(2)}, u32[]{:S(2)}) collective-permute-start(bf16[264,128]{1,0:T(8,128)(2,1)S(1)} %get-tuple-element.24), channel_id=1, source_target_pairs={{0,3},{1,0},{2,1},{3,2},{4,7},{5,4},{6,5},{7,6},{8,11},{9,8},{10,9... | collective-permute-start | bytes 202760 | tf_op jit(solution)/shard_map/ppermute | solution.py:346
  64.2 0.3 collective-permute-start.3
  64.5 0.7 collective-permute-start.2
  65.2 0.0 copy-done
  65.2 0.7 shard_map.64
  65.9 0.0 collective-permute-done.4.refs_2_
  66.0 2.9 %collective-permute-done.3.refs_1_ = bf16[264,128]{1,0:T(8,128)(2,1)S(1)} collective-permute-done((bf16[264,128]{1,0:T(8,128)(2,1)S(1)}, bf16[264,128]{1,0:T(8,128)(2,1)S(1)}, u32[]{:S(2)}, u32[]{:S(2)}) %collective-permute-start.3) | collective-permute-done | bytes 67616 | tf_op jit(solution)/shard_map/ppermute | solution.py:346
  68.9 1.7 %collective-permute-done.2.refs_0_ = bf16[264,128]{1,0:T(8,128)(2,1)S(1)} collective-permute-done((bf16[264,128]{1,0:T(8,128)(2,1)S(1)}, bf16[264,128]{1,0:T(8,128)(2,1)S(1)}, u32[]{:S(2)}, u32[]{:S(2)}) %collective-permute-start.2) | collective-permute-done | bytes 67616 | tf_op jit(solution)/shard_map/ppermute | solution.py:346
  70.6 4.4 %shard_map.70 = bf16[256,4096]{1,0:T(8,128)(2,1)} custom-call(s32[1]{0:T(128)} %bitcast.level_ref, f32[1,4096]{1,0:T(1,128)S(1)} %get-tuple-element.15.average_ref, bf16[256,4096]{1,0:T(8,128)(2,1)S(1)} %get-tuple-element.16.anomaly_ref, f32[264,128]{1,0:T(8,128)S(1)} %get-tuple-element.23.own_ref, bf16[264,128]{1,0:T(8,128)(2,1)S(1)} %collective-permute-done.2.refs_0_, ...), custom_call_target="tpu_custom_call" | custom-call | tf_op jit(solution)/shard_map/pallas_call | solution.py:270
  (5 shorter events, 0.1 us)
Async XLA Ops:
  0.0 35.7 %copy-start.1 = (s32[64,3]{0,1:T(4,128)S(1)}, s32[64,3]{0,1:T(4,128)}, u32[]{:S(2)}) copy-start(s32[64,3]{0,1:T(4,128)} %param.11) | copy-start | bytes 2308
  24.8 40.4 %copy-start = (bf16[1,256,4096]{2,1,0:T(8,128)(2,1)S(1)}, bf16[1,256,4096]{2,1,0:T(8,128)(2,1)}, u32[]{:S(2)}) copy-start(bf16[1,256,4096]{2,1,0:T(8,128)(2,1)} %param.6) | copy-start | bytes 6291460
  26.0 13.3 %all-to-all-start.1 = ((bf16[16,64,128]{2,1,0:T(8,128)(2,1)}), bf16[16,64,128]{2,1,0:T(8,128)(2,1)S(1)}, u32[]{:S(2)}, u32[]{:S(2)}) async-start(bf16[16,64,128]{2,1,0:T(8,128)(2,1)} %get-tuple-element.17), calls=%async_computation.1 | async-start | bytes 524288 | tf_op jit(solution)/shard_map/all_to_all | solution.py:318
  29.6 9.7 %collective-permute-start = (f32[2,384]{1,0:T(2,128)S(1)}, f32[2,384]{1,0:T(2,128)S(1)}, u32[]{:S(2)}, u32[]{:S(2)}) collective-permute-start(f32[2,384]{1,0:T(2,128)S(1)} %dynamic-slice_bitcast_fusion), channel_id=1, source_target_pairs={{0,32},{4,36},{8,40},{12,44},{16,48},{20,52},{24,56},{28,60},{32,0... | collective-permute-start | bytes 9224 | tf_op jit(solution)/shard_map/ppermute | solution.py:329
  40.4 20.9 %all-to-all-start.2 = ((bf16[64,16,128]{2,1,0:T(8,128)(2,1)}), bf16[64,16,128]{2,1,0:T(8,128)(2,1)S(1)}, u32[]{:S(2)}, u32[]{:S(2)}) async-start(bf16[64,16,128]{2,1,0:T(8,128)(2,1)} %shard_map.68), calls=%async_computation.2 | async-start | bytes 524288 | tf_op jit(solution)/shard_map/all_to_all | solution.py:335
  49.4 6.8 %collective-permute-start.1 = (f32[1,384]{1,0:T(1,128)S(1)}, f32[1,384]{1,0:T(1,128)S(1)}, u32[]{:S(2)}, u32[]{:S(2)}) collective-permute-start(f32[1,384]{1,0:T(1,128)S(1)} %constant_dynamic-slice_fusion), channel_id=1, source_target_pairs={{0,16},{4,20},{8,24},{12,28},{16,0},{20,4},{24,8},{28,12},{32,48},... | collective-permute-start | bytes 4616 | tf_op jit(solution)/shard_map/ppermute | solution.py:336
  61.4 4.6 %collective-permute-start.4 = (bf16[264,128]{1,0:T(8,128)(2,1)S(1)}, bf16[264,128]{1,0:T(8,128)(2,1)S(1)}, u32[]{:S(2)}, u32[]{:S(2)}) collective-permute-start(bf16[264,128]{1,0:T(8,128)(2,1)S(1)} %get-tuple-element.24), channel_id=1, source_target_pairs={{0,3},{1,0},{2,1},{3,2},{4,7},{5,4},{6,5},{7,6},{8,11},{9,8},{10,9... | collective-permute-start | bytes 202760 | tf_op jit(solution)/shard_map/ppermute | solution.py:346
  64.2 4.7 %collective-permute-start.3 = (bf16[264,128]{1,0:T(8,128)(2,1)S(1)}, bf16[264,128]{1,0:T(8,128)(2,1)S(1)}, u32[]{:S(2)}, u32[]{:S(2)}) collective-permute-start(bf16[264,128]{1,0:T(8,128)(2,1)S(1)} %get-tuple-element.24), channel_id=1, source_target_pairs={{0,2},{1,3},{2,0},{3,1},{4,6},{5,7},{6,4},{7,5},{8,10},{9,11},{10,... | collective-permute-start | bytes 202760 | tf_op jit(solution)/shard_map/ppermute | solution.py:346
  64.5 6.1 %collective-permute-start.2 = (bf16[264,128]{1,0:T(8,128)(2,1)S(1)}, bf16[264,128]{1,0:T(8,128)(2,1)S(1)}, u32[]{:S(2)}, u32[]{:S(2)}) collective-permute-start(bf16[264,128]{1,0:T(8,128)(2,1)S(1)} %get-tuple-element.24), channel_id=1, source_target_pairs={{0,1},{1,2},{2,3},{3,0},{4,5},{5,6},{6,7},{7,4},{8,9},{9,10},{10,1... | collective-permute-start | bytes 202760 | tf_op jit(solution)/shard_map/ppermute | solution.py:346

commit v5 on v4

--- a/solution.py
+++ b/solution.py
@@ -7,6 +7,7 @@
 from jax.experimental import pallas as pl
 from jax.experimental.pallas import tpu as pltpu
 from jax.sharding import PartitionSpec as P
+
 
 NSTEPS = 4
 TAPER = 0.6
@@ -160,11 +161,10 @@
         at, inner = GROUPS + group // 2, group % 2
         diagonal = sums[at : at + 1, inner * half : (inner + 1) * half]
         row = jnp.concatenate([sums[group : group + 1], diagonal], axis=1)
-        sums_ref[group // 2, inner : inner + 1, :] = row
+        sums_ref[group : group + 1, :] = row
 
 
 def mix_kernel(message_ref, high_ref, low_ref, mixed_ref):
-    places, rows, _ = message_ref.shape
     regions, piece, _ = mixed_ref.shape
     message = message_ref[...].reshape(regions, piece, LANES)
     parts = [
@@ -178,22 +178,14 @@
         mixed_ref[:, at : at + SUBLANES, :] = block.reshape(regions, SUBLANES, LANES)
 
 
-def gather_kernel(pieces_ref, extra_ref, own_ref, sent_ref):
+def gather_kernel(pieces_ref, own_ref, sent_ref):
     regions, piece, _ = pieces_ref.shape
-    size = regions // GROUPS * piece
     for place in range(regions // GROUPS):
         total = pieces_ref[region_at(place, 0)].astype(F32)
         for group in range(1, GROUPS):
             total = total + pieces_ref[region_at(place, group)].astype(F32)
         own_ref[place * piece : (place + 1) * piece, :] = total
         sent_ref[place * piece : (place + 1) * piece, :] = total.astype(BF16)
-    extra = extra_ref[...]
-    high = extra.astype(BF16).astype(F32)
-    low = extra - high
-    rows = [value[:, at : at + LANES] for value in (high, low) for at in range(0, 3 * LANES, LANES)]
-    rows = jnp.concatenate(rows + [jnp.zeros((2, LANES), F32)], axis=0)
-    own_ref[size:, :] = rows
-    sent_ref[size:, :] = rows.astype(BF16)
 
 
 def anomaly_kernel(ensemble_ref, average_ref, anomaly_ref):
@@ -205,7 +197,7 @@
         anomaly_ref[:, at : at + WIDTH] = (block - average).astype(BF16)
 
 
-def transform_kernel(levels, level_ref, average_ref, anomaly_ref, own_ref, *refs):
+def transform_kernel(levels, level_ref, average_ref, anomaly_ref, own_ref, extra_ref, *refs):
     half = LANES
     size = 2 * half
     output_ref, block_ref, semaphores = refs[-3:]
@@ -216,7 +208,7 @@
         apart = jnp.abs(level - source)
         factor = jnp.where(apart == 1, DECAY, jnp.where(apart == 2, DECAY**2, DECAY**3))
         everything = everything + factor * refs[ahead - 1][...].astype(F32)
-    extra = everything[size : size + 3] + everything[size + 3 : size + 6]
+    extra = extra_ref[...]
     tri = everything[:half]
     tri_t = tri.T
     cross = everything[half:size]
@@ -224,7 +216,7 @@
     col = iota((half, half), 1)
     first = jnp.where(row <= col, tri, tri_t)
     second = jnp.where(row > col, tri, tri_t)
-    second = jnp.where(row == col, extra[2:3], second)
+    second = jnp.where(row == col, extra[:, size:], second)
     matrix = jnp.concatenate(
         [jnp.concatenate([first, cross], axis=1), jnp.concatenate([cross.T, second], axis=1)], axis=0
     )
@@ -246,8 +238,7 @@
         inverse_iter = dot3(correction, inverse_split)
     root = inverse_iter / jnp.sqrt(norm_scale)
     root_split = split(root)
-    innovation = jnp.concatenate([extra[0:1], extra[1:2]], axis=1)
-    innovation = jnp.broadcast_to(innovation, (SUBLANES, size))
+    innovation = jnp.broadcast_to(extra[:, :size], (SUBLANES, size))
     inner = dot3(split(innovation), root_split)
     mean_shift = dot3(split(inner), root_split)[0:1, :]
     transform = (math.sqrt(size - 1.0) * root + mean_shift).astype(BF16)
@@ -277,12 +268,16 @@
     )(*args)
 
 
+def level_pairs(levels, ahead):
+    return [(level, (level + ahead) % levels) for level in range(levels)]
+
+
 def exchange(message, axes, count, groups=None):
     blocks = message.reshape(count, -1, message.shape[-1])
     return lax.all_to_all(blocks, axes, 0, 0, tiled=True, axis_index_groups=groups)
 
 
-def body(ensemble, obs_anomaly, innovation, obs_precision, owner_region, neighbours):
+def step(ensemble, obs_anomaly, innovation, obs_precision, owner_region, neighbours):
     regions = lax.axis_size("region")
     levels = lax.axis_size("level")
     my_region = lax.axis_index("region")
@@ -312,44 +307,40 @@
     )
     message, sums = call(
         functools.partial(covariance_kernel, capacity),
-        (shape((places, GROUPS * piece, LANES), BF16), shape((2, GROUPS // 2, members + LANES), F32)),
+        (shape((places, GROUPS * piece, LANES), BF16), shape((GROUPS, members + LANES), F32)),
         routed,
     )
     message = lax.all_to_all(message, "region", 0, 0, tiled=True, axis_index_groups=near)
 
-    def other_group(step):
+    mixed = call(mix_kernel, shape((regions, piece, LANES), BF16), message, high, low)
+    mixed, sums = lax.optimization_barrier((mixed, sums))
+    pieces = lax.all_to_all(mixed, "region", 0, 0, tiled=True)
+    parts = sums
+    for ahead in range(1, levels):
+        arrived = lax.ppermute(sums, "level", level_pairs(levels, ahead))
+        apart = jnp.abs(my_level - (my_level - ahead) % levels)
+        factor = sum(DECAY**distance * (apart == distance).astype(F32) for distance in range(levels))
+        parts = parts + factor * arrived
+
+    own, sent = call(
+        gather_kernel, (shape((members, LANES), F32), shape((members, LANES), BF16)), pieces
+    )
+    sent, parts = lax.optimization_barrier((sent, parts))
+    arrived = [
+        lax.ppermute(sent, "level", level_pairs(levels, ahead)) for ahead in range(1, levels)
+    ]
+    my_group = my_region // CORES % PLANES // PAIR
+    extra = lax.dynamic_slice_in_dim(parts, my_group, 1, 0)
+    for ahead in range(1, GROUPS):
         pairs = []
         for region in range(regions):
             x, z, core = region_parts(region)
-            pairs.append((region, (x * PLANES + (z ^ (step * PAIR))) * CORES + core))
-        return pairs
-
-    my_group = my_region // CORES % PLANES // PAIR
-    near_half, in_half = my_group // 2, my_group % 2
-    swapped = lax.ppermute(
-        lax.dynamic_index_in_dim(sums, 1 - near_half, 0, keepdims=False), "region", other_group(2)
-    )
-    kept = lax.dynamic_index_in_dim(sums, near_half, 0, keepdims=False) + swapped
-    mixed = call(mix_kernel, shape((regions, piece, LANES), BF16), message, high, low)
-    mixed, kept = lax.optimization_barrier((mixed, kept))
-    pieces = lax.all_to_all(mixed, "region", 0, 0, tiled=True)
-    swapped = lax.ppermute(
-        lax.dynamic_slice_in_dim(kept, 1 - in_half, 1, 0), "region", other_group(1)
-    )
-    part = lax.dynamic_slice_in_dim(kept, in_half, 1, 0) + swapped
-
-    height = members + SUBLANES
-    own, sent = call(
-        gather_kernel, (shape((height, LANES), F32), shape((height, LANES), BF16)), pieces, part
-    )
-    arrived = [
-        lax.ppermute(sent, "level", [(o, (o + ahead) % levels) for o in range(levels)])
-        for ahead in range(1, levels)
-    ]
+            pairs.append((region, (x * PLANES + (z + PAIR * ahead) % PLANES) * CORES + core))
+        part = lax.dynamic_slice_in_dim(parts, (my_group + ahead) % GROUPS, 1, 0)
+        arrived_part = lax.ppermute(part, "region", pairs)
+        extra = extra + arrived_part
     columns = ensemble.shape[2]
-    average, anomaly = call(
-        anomaly_kernel, (shape((1, columns), F32), shape((members, columns), BF16)), ensemble[0]
-    )
+    average, anomaly = call(anomaly_kernel, (shape((1, columns), F32), shape((members, columns), BF16)), ensemble[0])
     analysis = call(
         functools.partial(transform_kernel, levels),
         shape((members, columns), BF16),
@@ -357,6 +348,7 @@
         average,
         anomaly,
         own,
+        extra,
         *arrived,
         scalars=1,
         space=pl.ANY,
@@ -370,7 +362,7 @@
 
 def solution(mesh):
     return jax.shard_map(
-        body,
+        step,
         mesh=mesh,
         in_specs=(
             P("level", None, "region"),

time: 75.4 us -> 82.8 us (1.098)
  local copies, waits for them, and re-layouts: 0.02 us -> 2.93 us
  waiting for transfers between devices: 17.2 us -> 19.4 us
  starting transfers between devices: 24.7 us -> 26.6 us
    all_to_all x2, waiting for transfers between devices: 5.17 us -> 11.8 us  [the longest x1 7.05 us: step(): lax.all_to_all(message, 'region', 0, 0, tiled=True, axis_index_groups=near)]
    ppermute x5 -> x9, waiting for transfers between devices: 12 us -> 7.57 us  [the longest x3 4.26 us: step(): lax.ppermute(sent, 'level', level_pairs(levels, ahead))]
    unnamed x4 -> x8, local copies, waits for them, and re-layouts: 0.01 us -> 2.91 us
    ppermute x5 -> x9, starting transfers between devices: 12.3 us -> 13.9 us  [the longest x3 6.25 us: step(): arrived_part = lax.ppermute(part, 'region', pairs)]
  transfers between devices with their start and end apart: 7 -> 11, of which waited for: 5 -> 7; matrix products, arithmetic and copies ran while one was open for 0% -> 0% of each run, Pallas kernels for 2% -> 2%
where the time goes in v5:
time: 82.8 us; the launch traced here: 82.1 us
  starting transfers between devices  26.6 us (32%)
  blocking collectives  21.2 us (26%)
  waiting for transfers between devices  19.4 us (23%)
  Pallas kernels  11.8 us (14%)
  local copies, waits for them, and re-layouts  2.93 us (4%)
    all_to_all x1, blocking collectives, exchange(): lax.all_to_all(blocks, axes, 0, 0, tiled=True, axis_index_groups=groups)  21.2 us
    pallas_call x7, Pallas kernels, call(): pl.pallas_call(kernel, out_shape=shapes, in_specs=[pl.BlockSpec(memory_sp...  11.8 us
    all_to_all x1, starting transfers between devices, step(): pieces = lax.all_to_all(mixed, 'region', 0, 0, tiled=True)  9.25 us
    all_to_all x1, waiting for transfers between devices, step(): lax.all_to_all(message, 'region', 0, 0, tiled=True, axis_index_groups=near)  7.05 us
    ppermute x3, starting transfers between devices, step(): arrived_part = lax.ppermute(part, 'region', pairs)  6.25 us
    all_to_all x1, waiting for transfers between devices, step(): pieces = lax.all_to_all(mixed, 'region', 0, 0, tiled=True)  4.74 us
    ppermute x3, waiting for transfers between devices, step(): lax.ppermute(sent, 'level', level_pairs(levels, ahead))  4.26 us
    ppermute x3, starting transfers between devices, step(): arrived = lax.ppermute(sums, 'level', level_pairs(levels, ahead))  3.85 us
  transfers between devices with their start and end apart: 11, of which 7 were waited for; matrix products, arithmetic and copies ran while one was open for 0% of the time, Pallas kernels for 2%

profile of v5, /device:TPU:1, one launch (start us, length us, event | category | flops | bytes accessed | tf_op | source)
XLA Modules:
  0.0 82.1 jit_solution(15510501072243108074)
XLA Ops:
  0.0 3.6 %shard_map.65 = bf16[1664,256]{1,0:T(8,128)(2,1)} custom-call(s32[1,1024]{1,0:T(1,128)} %bitcast.12, bf16[1,1024]{1,0:T(2,128)(2,1)} %precision_ref.1, bf16[1,1024]{1,0:T(2,128)(2,1)} %innovation_ref.1, bf16[1024,256]{1,0:T(8,128)(2,1)} %bitcast.11, s32[3,64]{1,0:T(4,128)} %bitcast.8), custom_call_target="tpu_custom_call" | custom-call | tf_op jit(solution)/shard_map/pallas_call | solution.py:261
  3.6 21.2 %all_to_all.15.rows_ref = bf16[16,104,256]{2,1,0:T(8,128)(2,1)S(1)} all-to-all(bf16[16,104,256]{2,1,0:T(8,128)(2,1)} %bitcast.10), channel_id=1, replica_groups={{0,64,128,192,8,72,136,200,4,68,132,196,12,76,140,204},{16,80,144,208,2..., dimensions={0} | all-to-all | bytes 1703936 | tf_op jit(solution)/shard_map/all_to_all | solution.py:277
  24.8 1.2 %shard_map.66 = (bf16[16,64,128]{2,1,0:T(8,128)(2,1)}, f32[4,384]{1,0:T(4,128)S(1)}) custom-call(bf16[16,104,256]{2,1,0:T(8,128)(2,1)S(1)} %all_to_all.15.rows_ref), custom_call_target="tpu_custom_call" | custom-call | tf_op jit(solution)/shard_map/pallas_call | solution.py:261
  26.0 3.5 %all-to-all-start.1 = ((bf16[16,64,128]{2,1,0:T(8,128)(2,1)}), bf16[16,64,128]{2,1,0:T(8,128)(2,1)S(1)}, u32[]{:S(2)}, u32[]{:S(2)}) async-start(bf16[16,64,128]{2,1,0:T(8,128)(2,1)} %get-tuple-element.19), calls=%async_computation.1 | async-start | bytes 524288 | tf_op jit(solution)/shard_map/all_to_all | solution.py:313
  29.5 0.7 shard_map.67
  30.2 7.0 %all-to-all-done.1.message_ref = bf16[16,64,128]{2,1,0:T(8,128)(2,1)S(1)} async-done(((bf16[16,64,128]{2,1,0:T(8,128)(2,1)}), bf16[16,64,128]{2,1,0:T(8,128)(2,1)S(1)}, u32[]{:S(2)}, u32[]{:S(2)}) %all-to-all-start.1) | async-done | bytes 262176 | tf_op jit(solution)/shard_map/all_to_all | solution.py:313
  37.3 1.1 %shard_map.68 = bf16[64,16,128]{2,1,0:T(8,128)(2,1)} custom-call(bf16[16,64,128]{2,1,0:T(8,128)(2,1)S(1)} %all-to-all-done.1.message_ref, bf16[512,512]{1,0:T(8,128)(2,1)S(1)} %get-tuple-element.20.high_ref, bf16[512,512]{1,0:T(8,128)(2,1)S(1)} %get-tuple-element.21.low_ref), custom_call_target="tpu_custom_call" | custom-call | tf_op jit(solution)/shard_map/pallas_call | solution.py:261
  38.4 9.2 %all-to-all-start.2 = ((bf16[64,16,128]{2,1,0:T(8,128)(2,1)}), bf16[64,16,128]{2,1,0:T(8,128)(2,1)S(1)}, u32[]{:S(2)}, u32[]{:S(2)}) async-start(bf16[64,16,128]{2,1,0:T(8,128)(2,1)} %shard_map.68), calls=%async_computation.2 | async-start | bytes 524288 | tf_op jit(solution)/shard_map/all_to_all | solution.py:317
  47.7 2.8 %collective-permute-start.2 = (f32[4,384]{1,0:T(4,128)S(1)}, f32[4,384]{1,0:T(4,128)S(1)}, u32[]{:S(2)}, u32[]{:S(2)}) collective-permute-start(f32[4,384]{1,0:T(4,128)S(1)} %get-tuple-element.26), channel_id=1, source_target_pairs={{0,3},{1,0},{2,1},{3,2},{4,7},{5,4},{6,5},{7,6},{8,11},{9,8},{10,9... | collective-permute-start | bytes 18440 | tf_op jit(solution)/shard_map/ppermute | solution.py:320
  50.5 0.3 collective-permute-start.1
  50.9 0.7 collective-permute-start
  51.6 0.0 collective-permute-done.2
  51.6 3.2 %collective-permute-done.1 = f32[4,384]{1,0:T(4,128)S(1)} collective-permute-done((f32[4,384]{1,0:T(4,128)S(1)}, f32[4,384]{1,0:T(4,128)S(1)}, u32[]{:S(2)}, u32[]{:S(2)}) %collective-permute-start.1) | collective-permute-done | bytes 6176 | tf_op jit(solution)/shard_map/ppermute | solution.py:320
  54.8 0.1 collective-permute-done
  54.9 4.7 %all-to-all-done.2.pieces_ref = bf16[64,16,128]{2,1,0:T(8,128)(2,1)S(1)} async-done(((bf16[64,16,128]{2,1,0:T(8,128)(2,1)}), bf16[64,16,128]{2,1,0:T(8,128)(2,1)S(1)}, u32[]{:S(2)}, u32[]{:S(2)}) %all-to-all-start.2) | async-done | bytes 262176 | tf_op jit(solution)/shard_map/all_to_all | solution.py:317
  59.7 2.0 %collective-permute-start.3 = (f32[1,384]{1,0:T(1,128)S(1)}, f32[1,384]{1,0:T(1,128)S(1)}, u32[]{:S(2)}, u32[]{:S(2)}) collective-permute-start(f32[1,384]{1,0:T(1,128)S(1)} %get-tuple-element.29), channel_id=1, source_target_pairs={{0,16},{4,20},{8,24},{12,28},{16,32},{20,36},{24,40},{28,44},{32,4... | collective-permute-start | bytes 4616 | tf_op jit(solution)/shard_map/ppermute | solution.py:340
  61.6 1.7 %collective-permute-start.5 = (f32[1,384]{1,0:T(1,128)S(1)}, f32[1,384]{1,0:T(1,128)S(1)}, u32[]{:S(2)}, u32[]{:S(2)}) collective-permute-start(f32[1,384]{1,0:T(1,128)S(1)} %get-tuple-element.30), channel_id=1, source_target_pairs={{0,48},{4,52},{8,56},{12,60},{16,0},{20,4},{24,8},{28,12},{32,16},... | collective-permute-start | bytes 4616 | tf_op jit(solution)/shard_map/ppermute | solution.py:340
  63.3 2.6 %collective-permute-start.4 = (f32[1,384]{1,0:T(1,128)S(1)}, f32[1,384]{1,0:T(1,128)S(1)}, u32[]{:S(2)}, u32[]{:S(2)}) collective-permute-start(f32[1,384]{1,0:T(1,128)S(1)} %get-tuple-element.31), channel_id=1, source_target_pairs={{0,32},{4,36},{8,40},{12,44},{16,48},{20,52},{24,56},{28,60},{32,0... | collective-permute-start | bytes 4616 | tf_op jit(solution)/shard_map/ppermute | solution.py:340
  65.9 0.7 shard_map.64
  66.7 0.0 copy-start.1
  66.7 1.3 %copy-done.1 = bf16[256,4096]{1,0:T(8,128)(2,1)} copy-done((bf16[256,4096]{1,0:T(8,128)(2,1)}, bf16[256,4096]{1,0:T(8,128)(2,1)S(1)}, u32[]{:S(2)}) %copy-start.1) | copy-done | bytes 2097176
  68.0 2.7 %collective-permute-start.8 = (bf16[256,128]{1,0:T(8,128)(2,1)S(1)}, bf16[256,128]{1,0:T(8,128)(2,1)S(1)}, u32[]{:S(2)}, u32[]{:S(2)}) collective-permute-start(bf16[256,128]{1,0:T(8,128)(2,1)S(1)} %get-tuple-element.28), channel_id=1, source_target_pairs={{0,3},{1,0},{2,1},{3,2},{4,7},{5,4},{6,5},{7,6},{8,11},{9,8},{10,9... | collective-permute-start | bytes 196616 | tf_op jit(solution)/shard_map/ppermute | solution.py:330
  70.7 0.3 collective-permute-start.7
  71.1 0.0 collective-permute-done.3
  71.1 0.7 collective-permute-start.6
  71.8 0.0 collective-permute-done.5
  71.8 0.0 collective-permute-done.4
  71.8 0.3 collective-permute-done.8.refs_2_
  72.1 3.4 %collective-permute-done.7.refs_1_ = bf16[256,128]{1,0:T(8,128)(2,1)S(1)} collective-permute-done((bf16[256,128]{1,0:T(8,128)(2,1)S(1)}, bf16[256,128]{1,0:T(8,128)(2,1)S(1)}, u32[]{:S(2)}, u32[]{:S(2)}) %collective-permute-start.7) | collective-permute-done | bytes 65568 | tf_op jit(solution)/shard_map/ppermute | solution.py:330
  75.4 0.6 collective-permute-done.6.refs_0_
  76.0 1.6 %copy-done.2 = bf16[256,4096]{1,0:T(8,128)(2,1)S(1)} copy-done((bf16[256,4096]{1,0:T(8,128)(2,1)S(1)}, bf16[256,4096]{1,0:T(8,128)(2,1)}, u32[]{:S(2)}) %copy-start.2) | copy-done | bytes 2097176
  77.6 4.4 %shard_map.70 = bf16[256,4096]{1,0:T(8,128)(2,1)} custom-call(s32[1]{0:T(128)} %bitcast.level_ref, f32[1,4096]{1,0:T(1,128)S(1)} %get-tuple-element.17.average_ref, bf16[256,4096]{1,0:T(8,128)(2,1)S(1)} %copy-done.2, f32[256,128]{1,0:T(8,128)S(1)} %get-tuple-element.24.own_ref, f32[1,384]{1,0:T(1,128)S(1)} %add_add_fusion.extra_ref, ...), custom_call_target="tpu_custom_call" | custom-call | tf_op jit(solution)/shard_map/pallas_call | solution.py:261
  (9 shorter events, 0.1 us)
Async XLA Ops:
  0.0 29.5 %copy-start.3 = (s32[64,3]{0,1:T(4,128)S(1)}, s32[64,3]{0,1:T(4,128)}, u32[]{:S(2)}) copy-start(s32[64,3]{0,1:T(4,128)} %param.11) | copy-start | bytes 2308
  24.8 41.1 %copy-start = (bf16[1,256,4096]{2,1,0:T(8,128)(2,1)S(1)}, bf16[1,256,4096]{2,1,0:T(8,128)(2,1)}, u32[]{:S(2)}) copy-start(bf16[1,256,4096]{2,1,0:T(8,128)(2,1)} %param.6) | copy-start | bytes 6291460
  26.0 11.2 %all-to-all-start.1 = ((bf16[16,64,128]{2,1,0:T(8,128)(2,1)}), bf16[16,64,128]{2,1,0:T(8,128)(2,1)S(1)}, u32[]{:S(2)}, u32[]{:S(2)}) async-start(bf16[16,64,128]{2,1,0:T(8,128)(2,1)} %get-tuple-element.19), calls=%async_computation.1 | async-start | bytes 524288 | tf_op jit(solution)/shard_map/all_to_all | solution.py:313
  38.4 21.2 %all-to-all-start.2 = ((bf16[64,16,128]{2,1,0:T(8,128)(2,1)}), bf16[64,16,128]{2,1,0:T(8,128)(2,1)S(1)}, u32[]{:S(2)}, u32[]{:S(2)}) async-start(bf16[64,16,128]{2,1,0:T(8,128)(2,1)} %shard_map.68), calls=%async_computation.2 | async-start | bytes 524288 | tf_op jit(solution)/shard_map/all_to_all | solution.py:317
  47.7 3.9 %collective-permute-start.2 = (f32[4,384]{1,0:T(4,128)S(1)}, f32[4,384]{1,0:T(4,128)S(1)}, u32[]{:S(2)}, u32[]{:S(2)}) collective-permute-start(f32[4,384]{1,0:T(4,128)S(1)} %get-tuple-element.26), channel_id=1, source_target_pairs={{0,3},{1,0},{2,1},{3,2},{4,7},{5,4},{6,5},{7,6},{8,11},{9,8},{10,9... | collective-permute-start | bytes 18440 | tf_op jit(solution)/shard_map/ppermute | solution.py:320
  50.5 4.3 %collective-permute-start.1 = (f32[4,384]{1,0:T(4,128)S(1)}, f32[4,384]{1,0:T(4,128)S(1)}, u32[]{:S(2)}, u32[]{:S(2)}) collective-permute-start(f32[4,384]{1,0:T(4,128)S(1)} %get-tuple-element.26), channel_id=1, source_target_pairs={{0,2},{1,3},{2,0},{3,1},{4,6},{5,7},{6,4},{7,5},{8,10},{9,11},{10,... | collective-permute-start | bytes 18440 | tf_op jit(solution)/shard_map/ppermute | solution.py:320
  50.9 4.0 %collective-permute-start = (f32[4,384]{1,0:T(4,128)S(1)}, f32[4,384]{1,0:T(4,128)S(1)}, u32[]{:S(2)}, u32[]{:S(2)}) collective-permute-start(f32[4,384]{1,0:T(4,128)S(1)} %get-tuple-element.26), channel_id=1, source_target_pairs={{0,1},{1,2},{2,3},{3,0},{4,5},{5,6},{6,7},{7,4},{8,9},{9,10},{10,1... | collective-permute-start | bytes 18440 | tf_op jit(solution)/shard_map/ppermute | solution.py:320
  59.7 11.4 %collective-permute-start.3 = (f32[1,384]{1,0:T(1,128)S(1)}, f32[1,384]{1,0:T(1,128)S(1)}, u32[]{:S(2)}, u32[]{:S(2)}) collective-permute-start(f32[1,384]{1,0:T(1,128)S(1)} %get-tuple-element.29), channel_id=1, source_target_pairs={{0,16},{4,20},{8,24},{12,28},{16,32},{20,36},{24,40},{28,44},{32,4... | collective-permute-start | bytes 4616 | tf_op jit(solution)/shard_map/ppermute | solution.py:340
  61.6 10.1 %collective-permute-start.5 = (f32[1,384]{1,0:T(1,128)S(1)}, f32[1,384]{1,0:T(1,128)S(1)}, u32[]{:S(2)}, u32[]{:S(2)}) collective-permute-start(f32[1,384]{1,0:T(1,128)S(1)} %get-tuple-element.30), channel_id=1, source_target_pairs={{0,48},{4,52},{8,56},{12,60},{16,0},{20,4},{24,8},{28,12},{32,16},... | collective-permute-start | bytes 4616 | tf_op jit(solution)/shard_map/ppermute | solution.py:340
  63.3 8.4 %collective-permute-start.4 = (f32[1,384]{1,0:T(1,128)S(1)}, f32[1,384]{1,0:T(1,128)S(1)}, u32[]{:S(2)}, u32[]{:S(2)}) collective-permute-start(f32[1,384]{1,0:T(1,128)S(1)} %get-tuple-element.31), channel_id=1, source_target_pairs={{0,32},{4,36},{8,40},{12,44},{16,48},{20,52},{24,56},{28,60},{32,0... | collective-permute-start | bytes 4616 | tf_op jit(solution)/shard_map/ppermute | solution.py:340
  66.7 1.3 %copy-start.1 = (bf16[256,4096]{1,0:T(8,128)(2,1)}, bf16[256,4096]{1,0:T(8,128)(2,1)S(1)}, u32[]{:S(2)}) copy-start(bf16[256,4096]{1,0:T(8,128)(2,1)S(1)} %get-tuple-element.18.anomaly_ref) | copy-start | bytes 6291460
  68.0 4.1 %collective-permute-start.8 = (bf16[256,128]{1,0:T(8,128)(2,1)S(1)}, bf16[256,128]{1,0:T(8,128)(2,1)S(1)}, u32[]{:S(2)}, u32[]{:S(2)}) collective-permute-start(bf16[256,128]{1,0:T(8,128)(2,1)S(1)} %get-tuple-element.28), channel_id=1, source_target_pairs={{0,3},{1,0},{2,1},{3,2},{4,7},{5,4},{6,5},{7,6},{8,11},{9,8},{10,9... | collective-permute-start | bytes 196616 | tf_op jit(solution)/shard_map/ppermute | solution.py:330
  70.7 4.7 %collective-permute-start.7 = (bf16[256,128]{1,0:T(8,128)(2,1)S(1)}, bf16[256,128]{1,0:T(8,128)(2,1)S(1)}, u32[]{:S(2)}, u32[]{:S(2)}) collective-permute-start(bf16[256,128]{1,0:T(8,128)(2,1)S(1)} %get-tuple-element.28), channel_id=1, source_target_pairs={{0,2},{1,3},{2,0},{3,1},{4,6},{5,7},{6,4},{7,5},{8,10},{9,11},{10,... | collective-permute-start | bytes 196616 | tf_op jit(solution)/shard_map/ppermute | solution.py:330
  71.1 5.0 %collective-permute-start.6 = (bf16[256,128]{1,0:T(8,128)(2,1)S(1)}, bf16[256,128]{1,0:T(8,128)(2,1)S(1)}, u32[]{:S(2)}, u32[]{:S(2)}) collective-permute-start(bf16[256,128]{1,0:T(8,128)(2,1)S(1)} %get-tuple-element.28), channel_id=1, source_target_pairs={{0,1},{1,2},{2,3},{3,0},{4,5},{5,6},{6,7},{7,4},{8,9},{9,10},{10,1... | collective-permute-start | bytes 196616 | tf_op jit(solution)/shard_map/ppermute | solution.py:330
  76.0 1.6 %copy-start.2 = (bf16[256,4096]{1,0:T(8,128)(2,1)S(1)}, bf16[256,4096]{1,0:T(8,128)(2,1)}, u32[]{:S(2)}) copy-start(bf16[256,4096]{1,0:T(8,128)(2,1)} %copy-done.1) | copy-start | bytes 6291460

commit v6 on v4

--- a/solution.py
+++ b/solution.py
@@ -36,10 +36,17 @@
     return high, (value - high.astype(F32)).astype(BF16)
 
 
-def dot3(left, right, dims=((1,), (0,))):
+def dot3(left, right, dims=((1,), (0,)), halves=False):
     lh, ll = left
     rh, rl = right
-    return dot(lh, rh, dims) + (dot(lh, rl, dims) + dot(ll, rh, dims))
+    if dims != ((1,), (0,)):
+        return dot(lh, rh, dims) + (dot(lh, rl, dims) + dot(ll, rh, dims))
+    left = jnp.concatenate([lh, lh, ll], axis=1)
+    right = jnp.concatenate([rh, rl, rh], axis=0)
+    half = left.shape[0] // 2
+    if halves and half >= LANES:
+        return jnp.concatenate([dot(left[:half], right), dot(left[half:], right)], axis=0)
+    return dot(left, right)
 
 
 def region_parts(region):
@@ -71,13 +78,43 @@
 
 
 def place_kernel(
-    regions, capacity, owner_ref, precision_ref, innovation_ref, obs_ref, listed_ref, rows_ref
+    regions,
+    capacity,
+    owner_in,
+    precision_in,
+    obs_in,
+    innovation_in,
+    listed_in,
+    rows_out,
+    owner_ref,
+    precision_ref,
+    obs_ref,
+    innovation_ref,
+    listed_ref,
+    rows_ref,
+    arrivals,
+    departures,
 ):
+    copies = [
+        pltpu.make_async_copy(source, target, arrivals.at[index])
+        for index, (source, target) in enumerate(
+            [
+                (owner_in, owner_ref),
+                (precision_in, precision_ref),
+                (obs_in, obs_ref),
+                (innovation_in, innovation_ref),
+                (listed_in, listed_ref),
+            ]
+        )
+    ]
+    for copy in copies:
+        copy.start()
     count = owner_ref.shape[1]
     blocks = count // LANES
     region_ids = iota((regions, LANES), 0)
     earlier = iota((LANES, LANES), 0) < iota((LANES, LANES), 1)
     counter = jnp.concatenate([onehot(earlier), jnp.ones((LANES, LANES), BF16)], axis=1)
+    copies[0].wait()
     owners = owner_ref[...]
     named = [region_ids == owners[:, b * LANES : (b + 1) * LANES] for b in range(blocks)]
     ranks = dot(jnp.concatenate([onehot(hit) for hit in named], axis=0), counter)
@@ -89,9 +126,26 @@
         pieces.append(jnp.sum(slot, axis=0, keepdims=True))
         base = base + part[:, LANES:]
     slots = jnp.concatenate(pieces, axis=1).astype(jnp.int32)
+    copies[1].wait()
     precision = precision_ref[...].astype(F32)
     scale = jnp.sqrt(precision)
+    for copy in copies[2:]:
+        copy.wait()
     obs = obs_ref[...]
+
+    span = GROUPS * capacity
+    at_once = 8
+    sites = regions // GROUPS
+    for start in range(0, sites, at_once):
+        hit = slots == iota((at_once * span, count), 0) + start * span
+        placed = dot(jnp.where(hit, scale, 0.0).astype(BF16), obs).astype(BF16)
+        for k in range(at_once):
+            rows_ref[start + k, :span, :] = placed[k * span : (k + 1) * span]
+        if start == 0:
+            part = (slice(0, at_once), slice(0, span))
+            copy = pltpu.make_async_copy(rows_ref.at[part], rows_out.at[part], departures.at[0])
+            copy.start()
+            leaving = [copy]
 
     factor = precision * innovation_ref[...].astype(F32)
     hit = iota((regions, count), 0) == owners
@@ -99,7 +153,6 @@
     half = obs[:, LANES:].astype(F32)
     squares = split(dot(jnp.where(hit, precision, 0.0).astype(BF16), (half * half).astype(BF16)))
     weight = split(weights_transposed(listed_ref[...]))
-    sites = regions // GROUPS
     row = iota((regions, sites * EXTRA), 1)
     place, item = row // EXTRA, row % EXTRA
 
@@ -114,16 +167,14 @@
     left = dot3(chosen(second, is_diag), squares, over)
     right = dot3(chosen(second + 1, is_diag), squares, over)
     extra = (extra + jnp.concatenate([left, right], axis=1)).astype(BF16)
-
-    span = GROUPS * capacity
-    at_once = 4
-    for start in range(0, sites, at_once):
-        hit = slots == iota((at_once * span, count), 0) + start * span
-        placed = dot(jnp.where(hit, scale, 0.0).astype(BF16), obs).astype(BF16)
-        for k in range(at_once):
-            at = (start + k) * (span + EXTRA)
-            rows_ref[at : at + span, :] = placed[k * span : (k + 1) * span]
-            rows_ref[at + span : at + span + EXTRA, :] = extra[(start + k) * EXTRA : (start + k + 1) * EXTRA]
+    rows_ref[:, span:, :] = extra.reshape(sites, EXTRA, extra.shape[1])
+    rest = [(slice(0, at_once), slice(span, span + EXTRA)), (slice(at_once, sites), slice(0, span + EXTRA))]
+    for index, part in enumerate(rest):
+        copy = pltpu.make_async_copy(rows_ref.at[part], rows_out.at[part], departures.at[index + 1])
+        copy.start()
+        leaving.append(copy)
+    for copy in leaving:
+        copy.wait()
 
 
 def weight_kernel(listed_ref, high_ref, low_ref):
@@ -160,7 +211,7 @@
         at, inner = GROUPS + group // 2, group % 2
         diagonal = sums[at : at + 1, inner * half : (inner + 1) * half]
         row = jnp.concatenate([sums[group : group + 1], diagonal], axis=1)
-        sums_ref[group // 2, inner : inner + 1, :] = row
+        sums_ref[group : group + 1, :] = row
 
 
 def mix_kernel(message_ref, high_ref, low_ref, mixed_ref):
@@ -233,18 +284,18 @@
     squares = jnp.sum(jnp.sum(matrix * matrix, axis=0, keepdims=True), axis=1, keepdims=True)
     norm_scale = 0.5 * jnp.sqrt(squares)
     diagonal = jnp.where(same, 1.5, 0.0)
-    root_iter = matrix / norm_scale
+    root_iter = matrix * (1.0 / norm_scale)
     correction = diagonal - 0.5 * root_iter
     inverse_iter = correction
-    root_iter = dot3(split(root_iter), split(correction))
+    root_iter = dot3(split(root_iter), split(correction), halves=True)
     for newton_step in range(1, NSTEPS):
         inverse_split = split(inverse_iter)
         root_split = split(root_iter)
-        correction = split(diagonal - 0.5 * dot3(inverse_split, root_split))
+        correction = split(diagonal - 0.5 * dot3(inverse_split, root_split, halves=True))
         if newton_step < NSTEPS - 1:
             root_iter = dot3(root_split, correction)
         inverse_iter = dot3(correction, inverse_split)
-    root = inverse_iter / jnp.sqrt(norm_scale)
+    root = inverse_iter * (1.0 / jnp.sqrt(norm_scale))
     root_split = split(root)
     innovation = jnp.concatenate([extra[0:1], extra[1:2]], axis=1)
     innovation = jnp.broadcast_to(innovation, (SUBLANES, size))
@@ -265,8 +316,17 @@
         copy.wait()
 
 
-def call(kernel, shapes, *args, scratch=(), limit=VMEM_LIMIT, scalars=0, space=pltpu.VMEM):
-    spaces = [pltpu.SMEM] * scalars + [pltpu.VMEM] * (len(args) - scalars)
+def call(
+    kernel,
+    shapes,
+    *args,
+    scratch=(),
+    limit=VMEM_LIMIT,
+    scalars=0,
+    space=pltpu.VMEM,
+    inputs=pltpu.VMEM,
+):
+    spaces = [pltpu.SMEM] * scalars + [inputs] * (len(args) - scalars)
     return pl.pallas_call(
         kernel,
         out_shape=shapes,
@@ -275,11 +335,6 @@
         scratch_shapes=scratch,
         compiler_params=pltpu.CompilerParams(vmem_limit_bytes=limit),
     )(*args)
-
-
-def exchange(message, axes, count, groups=None):
-    blocks = message.reshape(count, -1, message.shape[-1])
-    return lax.all_to_all(blocks, axes, 0, 0, tiled=True, axis_index_groups=groups)
 
 
 def body(ensemble, obs_anomaly, innovation, obs_precision, owner_region, neighbours):
@@ -294,49 +349,54 @@
     owners = owner_region.reshape(1, local_obs)
     listed = neighbours.T
     shape = jax.ShapeDtypeStruct
+    block = (places, GROUPS * capacity + EXTRA, members)
     rows = call(
         functools.partial(place_kernel, regions, capacity),
-        shape((places * (GROUPS * capacity + EXTRA), members), BF16),
+        shape(block, BF16),
         owners,
         obs_precision,
+        obs_anomaly[0],
         innovation,
-        obs_anomaly[0],
         listed,
         limit=FIRST_LIMIT,
+        space=pl.ANY,
+        inputs=pl.ANY,
+        scratch=[
+            pltpu.VMEM(owners.shape, jnp.int32),
+            pltpu.VMEM(obs_precision.shape, BF16),
+            pltpu.VMEM((local_obs, members), BF16),
+            pltpu.VMEM(innovation.shape, BF16),
+            pltpu.VMEM(listed.shape, jnp.int32),
+            pltpu.VMEM(block, BF16),
+            pltpu.SemaphoreType.DMA((5,)),
+            pltpu.SemaphoreType.DMA((3,)),
+        ],
     )
     near = [[region_at(place, group) for place in range(places)] for group in range(GROUPS)]
-    routed = exchange(rows, "region", places, near)
+    routed = lax.all_to_all(rows, "region", 0, 0, tiled=True, axis_index_groups=near)
     piece = members // places
     high, low = call(
         weight_kernel, (shape((regions * SUBLANES, regions * SUBLANES), BF16),) * 2, listed
     )
-    message, sums = call(
+    message, parts = call(
         functools.partial(covariance_kernel, capacity),
-        (shape((places, GROUPS * piece, LANES), BF16), shape((2, GROUPS // 2, members + LANES), F32)),
+        (shape((places, GROUPS * piece, LANES), BF16), shape((GROUPS, members + LANES), F32)),
         routed,
     )
     message = lax.all_to_all(message, "region", 0, 0, tiled=True, axis_index_groups=near)
-
-    def other_group(step):
+    mixed = call(mix_kernel, shape((regions, piece, LANES), BF16), message, high, low)
+    mixed, parts = lax.optimization_barrier((mixed, parts))
+    pieces = lax.all_to_all(mixed, "region", 0, 0, tiled=True)
+
+    my_group = my_region // CORES % PLANES // PAIR
+    part = lax.dynamic_slice_in_dim(parts, my_group, 1, 0)
+    for ahead in range(1, GROUPS):
+        sent = lax.dynamic_slice_in_dim(parts, (my_group + ahead) % GROUPS, 1, 0)
         pairs = []
         for region in range(regions):
             x, z, core = region_parts(region)
-            pairs.append((region, (x * PLANES + (z ^ (step * PAIR))) * CORES + core))
-        return pairs
-
-    my_group = my_region // CORES % PLANES // PAIR
-    near_half, in_half = my_group // 2, my_group % 2
-    swapped = lax.ppermute(
-        lax.dynamic_index_in_dim(sums, 1 - near_half, 0, keepdims=False), "region", other_group(2)
-    )
-    kept = lax.dynamic_index_in_dim(sums, near_half, 0, keepdims=False) + swapped
-    mixed = call(mix_kernel, shape((regions, piece, LANES), BF16), message, high, low)
-    mixed, kept = lax.optimization_barrier((mixed, kept))
-    pieces = lax.all_to_all(mixed, "region", 0, 0, tiled=True)
-    swapped = lax.ppermute(
-        lax.dynamic_slice_in_dim(kept, 1 - in_half, 1, 0), "region", other_group(1)
-    )
-    part = lax.dynamic_slice_in_dim(kept, in_half, 1, 0) + swapped
+            pairs.append((region, (x * PLANES + (z + PAIR * ahead) % PLANES) * CORES + core))
+        part = part + lax.ppermute(sent, "region", pairs)
 
     height = members + SUBLANES
     own, sent = call(

time: 75.4 us -> 73.5 us (0.975)
  waiting for transfers between devices: 17.2 us -> 14.7 us
  starting transfers between devices: 24.7 us -> 25.5 us
    all_to_all x1, waiting for transfers between devices: 0.01 us -> 7.05 us  [body(): lax.all_to_all(message, 'region', 0, 0, tiled=True, axis_index_groups=near)]
    ppermute x2 -> x3, waiting for transfers between devices: 7.36 us -> 2.39 us  [body(): part = part + lax.ppermute(sent, 'region', pairs)]
    all_to_all x1, waiting for transfers between devices: 5.16 us -> 0.58 us  [body(): pieces = lax.all_to_all(mixed, 'region', 0, 0, tiled=True)]
    ppermute x2 -> x3, starting transfers between devices: 8.43 us -> 8.92 us  [body(): part = part + lax.ppermute(sent, 'region', pairs)]
  transfers between devices with their start and end apart: 7 -> 8, of which waited for: 5 -> 5; matrix products, arithmetic and copies ran while one was open for 0% -> 0% of each run, Pallas kernels for 2% -> 2%
where the time goes in v6:
time: 73.5 us; the launch traced here: 73.2 us
  starting transfers between devices  25.5 us (35%)
  blocking collectives  21.2 us (29%)
  waiting for transfers between devices  14.7 us (20%)
  Pallas kernels  11.6 us (16%)
    all_to_all x1, blocking collectives, body(): lax.all_to_all(rows, 'region', 0, 0, tiled=True, axis_index_groups=near)  21.2 us
    pallas_call x7, Pallas kernels, call(): pl.pallas_call(kernel, out_shape=shapes, in_specs=[pl.BlockSpec(memory_sp...  11.6 us
    all_to_all x1, starting transfers between devices, body(): pieces = lax.all_to_all(mixed, 'region', 0, 0, tiled=True)  9.24 us
    ppermute x3, starting transfers between devices, body(): part = part + lax.ppermute(sent, 'region', pairs)  8.92 us
    all_to_all x1, waiting for transfers between devices, body(): lax.all_to_all(message, 'region', 0, 0, tiled=True, axis_index_groups=near)  7.05 us
    ppermute x3, waiting for transfers between devices, body(): lax.ppermute(sent, 'level', [(o, (o + ahead) % levels) for o in range(lev...  4.69 us
    ppermute x3, starting transfers between devices, body(): lax.ppermute(sent, 'level', [(o, (o + ahead) % levels) for o in range(lev...  3.86 us
    all_to_all x1, starting transfers between devices, body(): lax.all_to_all(message, 'region', 0, 0, tiled=True, axis_index_groups=near)  3.49 us
  transfers between devices with their start and end apart: 8, of which 5 were waited for; matrix products, arithmetic and copies ran while one was open for 0% of the time, Pallas kernels for 2%

profile of v6, /device:TPU:1, one launch (start us, length us, event | category | flops | bytes accessed | tf_op | source)
XLA Modules:
  0.0 73.2 jit_solution(2232504599648730798)
XLA Ops:
  0.0 0.0 copy-start.1
  0.0 3.5 %shard_map.65 = bf16[16,104,256]{2,1,0:T(8,128)(2,1)} custom-call(s32[1,1024]{1,0:T(1,128)} %bitcast.10, bf16[1,1024]{1,0:T(2,128)(2,1)} %precision_in.1, bf16[1024,256]{1,0:T(8,128)(2,1)} %bitcast.9, bf16[1,1024]{1,0:T(2,128)(2,1)} %innovation_in.1, s32[3,64]{1,0:T(4,128)} %bitcast.7), custom_call_target="tpu_custom_call" | custom-call | tf_op jit(solution)/shard_map/pallas_call | solution.py:330
  3.5 21.2 %all_to_all.15.rows_ref = bf16[16,104,256]{2,1,0:T(8,128)(2,1)S(1)} all-to-all(bf16[16,104,256]{2,1,0:T(8,128)(2,1)} %shard_map.65), channel_id=1, replica_groups={{0,64,128,192,8,72,136,200,4,68,132,196,12,76,140,204},{16,80,144,208,2..., dimensions={0} | all-to-all | bytes 1703936 | tf_op jit(solution)/shard_map/all_to_all | solution.py:376
  24.7 0.0 copy-start
  24.7 1.2 %shard_map.66 = (bf16[16,64,128]{2,1,0:T(8,128)(2,1)}, f32[4,384]{1,0:T(4,128)S(1)}) custom-call(bf16[16,104,256]{2,1,0:T(8,128)(2,1)S(1)} %all_to_all.15.rows_ref), custom_call_target="tpu_custom_call" | custom-call | tf_op jit(solution)/shard_map/pallas_call | solution.py:330
  25.9 3.5 %all-to-all-start.1 = ((bf16[16,64,128]{2,1,0:T(8,128)(2,1)}), bf16[16,64,128]{2,1,0:T(8,128)(2,1)S(1)}, u32[]{:S(2)}, u32[]{:S(2)}) async-start(bf16[16,64,128]{2,1,0:T(8,128)(2,1)} %get-tuple-element.17), calls=%async_computation.1 | async-start | bytes 524288 | tf_op jit(solution)/shard_map/all_to_all | solution.py:386
  29.4 0.0 copy-done.1
  29.4 0.7 shard_map.67
  30.1 7.0 %all-to-all-done.1.message_ref = bf16[16,64,128]{2,1,0:T(8,128)(2,1)S(1)} async-done(((bf16[16,64,128]{2,1,0:T(8,128)(2,1)}), bf16[16,64,128]{2,1,0:T(8,128)(2,1)S(1)}, u32[]{:S(2)}, u32[]{:S(2)}) %all-to-all-start.1) | async-done | bytes 262176 | tf_op jit(solution)/shard_map/all_to_all | solution.py:386
  37.2 1.1 %shard_map.68 = bf16[64,16,128]{2,1,0:T(8,128)(2,1)} custom-call(bf16[16,64,128]{2,1,0:T(8,128)(2,1)S(1)} %all-to-all-done.1.message_ref, bf16[512,512]{1,0:T(8,128)(2,1)S(1)} %get-tuple-element.18.high_ref, bf16[512,512]{1,0:T(8,128)(2,1)S(1)} %get-tuple-element.19.low_ref), custom_call_target="tpu_custom_call" | custom-call | tf_op jit(solution)/shard_map/pallas_call | solution.py:330
  38.3 9.2 %all-to-all-start.2 = ((bf16[64,16,128]{2,1,0:T(8,128)(2,1)}), bf16[64,16,128]{2,1,0:T(8,128)(2,1)S(1)}, u32[]{:S(2)}, u32[]{:S(2)}) async-start(bf16[64,16,128]{2,1,0:T(8,128)(2,1)} %shard_map.68), calls=%async_computation.2 | async-start | bytes 524288 | tf_op jit(solution)/shard_map/all_to_all | solution.py:389
  47.7 2.3 %collective-permute-start = (f32[1,384]{1,0:T(1,128)S(1)}, f32[1,384]{1,0:T(1,128)S(1)}, u32[]{:S(2)}, u32[]{:S(2)}) collective-permute-start(f32[1,384]{1,0:T(1,128)S(1)} %get-tuple-element.25), channel_id=1, source_target_pairs={{0,16},{4,20},{8,24},{12,28},{16,32},{20,36},{24,40},{28,44},{32,4... | collective-permute-start | bytes 4616 | tf_op jit(solution)/shard_map/ppermute | solution.py:399
  50.0 1.3 %collective-permute-start.2 = (f32[1,384]{1,0:T(1,128)S(1)}, f32[1,384]{1,0:T(1,128)S(1)}, u32[]{:S(2)}, u32[]{:S(2)}) collective-permute-start(f32[1,384]{1,0:T(1,128)S(1)} %get-tuple-element.26), channel_id=1, source_target_pairs={{0,48},{4,52},{8,56},{12,60},{16,0},{20,4},{24,8},{28,12},{32,16},... | collective-permute-start | bytes 4616 | tf_op jit(solution)/shard_map/ppermute | solution.py:399
  51.3 5.3 %collective-permute-start.1 = (f32[1,384]{1,0:T(1,128)S(1)}, f32[1,384]{1,0:T(1,128)S(1)}, u32[]{:S(2)}, u32[]{:S(2)}) collective-permute-start(f32[1,384]{1,0:T(1,128)S(1)} %get-tuple-element.27), channel_id=1, source_target_pairs={{0,32},{4,36},{8,40},{12,44},{16,48},{20,52},{24,56},{28,60},{32,0... | collective-permute-start | bytes 4616 | tf_op jit(solution)/shard_map/ppermute | solution.py:399
  56.6 0.0 collective-permute-done
  56.6 0.0 collective-permute-done.2
  56.6 2.4 %collective-permute-done.1 = f32[1,384]{1,0:T(1,128)S(1)} collective-permute-done((f32[1,384]{1,0:T(1,128)S(1)}, f32[1,384]{1,0:T(1,128)S(1)}, u32[]{:S(2)}, u32[]{:S(2)}) %collective-permute-start.1) | collective-permute-done | bytes 1568 | tf_op jit(solution)/shard_map/ppermute | solution.py:399
  59.0 0.6 all-to-all-done.2.pieces_ref
  59.6 2.8 %collective-permute-start.5 = (bf16[264,128]{1,0:T(8,128)(2,1)S(1)}, bf16[264,128]{1,0:T(8,128)(2,1)S(1)}, u32[]{:S(2)}, u32[]{:S(2)}) collective-permute-start(bf16[264,128]{1,0:T(8,128)(2,1)S(1)} %get-tuple-element.24), channel_id=1, source_target_pairs={{0,3},{1,0},{2,1},{3,2},{4,7},{5,4},{6,5},{7,6},{8,11},{9,8},{10,9... | collective-permute-start | bytes 202760 | tf_op jit(solution)/shard_map/ppermute | solution.py:406
  62.5 0.3 collective-permute-start.4
  62.8 0.7 collective-permute-start.3
  63.5 0.0 copy-done
  63.5 0.7 shard_map.64
  64.2 0.0 collective-permute-done.5.refs_2_
  64.2 2.9 %collective-permute-done.4.refs_1_ = bf16[264,128]{1,0:T(8,128)(2,1)S(1)} collective-permute-done((bf16[264,128]{1,0:T(8,128)(2,1)S(1)}, bf16[264,128]{1,0:T(8,128)(2,1)S(1)}, u32[]{:S(2)}, u32[]{:S(2)}) %collective-permute-start.4) | collective-permute-done | bytes 67616 | tf_op jit(solution)/shard_map/ppermute | solution.py:406
  67.2 1.8 %collective-permute-done.3.refs_0_ = bf16[264,128]{1,0:T(8,128)(2,1)S(1)} collective-permute-done((bf16[264,128]{1,0:T(8,128)(2,1)S(1)}, bf16[264,128]{1,0:T(8,128)(2,1)S(1)}, u32[]{:S(2)}, u32[]{:S(2)}) %collective-permute-start.3) | collective-permute-done | bytes 67616 | tf_op jit(solution)/shard_map/ppermute | solution.py:406
  68.9 4.2 %shard_map.70 = bf16[256,4096]{1,0:T(8,128)(2,1)} custom-call(s32[1]{0:T(128)} %bitcast.level_ref, f32[1,4096]{1,0:T(1,128)S(1)} %get-tuple-element.15.average_ref, bf16[256,4096]{1,0:T(8,128)(2,1)S(1)} %get-tuple-element.16.anomaly_ref, f32[264,128]{1,0:T(8,128)S(1)} %get-tuple-element.23.own_ref, bf16[264,128]{1,0:T(8,128)(2,1)S(1)} %collective-permute-done.3.refs_0_, ...), custom_call_target="tpu_custom_call" | custom-call | tf_op jit(solution)/shard_map/pallas_call | solution.py:330
  (3 shorter events, 0.1 us)
Async XLA Ops:
  0.0 29.4 %copy-start.1 = (s32[64,3]{0,1:T(4,128)S(1)}, s32[64,3]{0,1:T(4,128)}, u32[]{:S(2)}) copy-start(s32[64,3]{0,1:T(4,128)} %param.11) | copy-start | bytes 2308
  24.7 38.8 %copy-start = (bf16[1,256,4096]{2,1,0:T(8,128)(2,1)S(1)}, bf16[1,256,4096]{2,1,0:T(8,128)(2,1)}, u32[]{:S(2)}) copy-start(bf16[1,256,4096]{2,1,0:T(8,128)(2,1)} %param.6) | copy-start | bytes 6291460
  25.9 11.2 %all-to-all-start.1 = ((bf16[16,64,128]{2,1,0:T(8,128)(2,1)}), bf16[16,64,128]{2,1,0:T(8,128)(2,1)S(1)}, u32[]{:S(2)}, u32[]{:S(2)}) async-start(bf16[16,64,128]{2,1,0:T(8,128)(2,1)} %get-tuple-element.17), calls=%async_computation.1 | async-start | bytes 524288 | tf_op jit(solution)/shard_map/all_to_all | solution.py:386
  38.3 21.3 %all-to-all-start.2 = ((bf16[64,16,128]{2,1,0:T(8,128)(2,1)}), bf16[64,16,128]{2,1,0:T(8,128)(2,1)S(1)}, u32[]{:S(2)}, u32[]{:S(2)}) async-start(bf16[64,16,128]{2,1,0:T(8,128)(2,1)} %shard_map.68), calls=%async_computation.2 | async-start | bytes 524288 | tf_op jit(solution)/shard_map/all_to_all | solution.py:389
  47.7 8.9 %collective-permute-start = (f32[1,384]{1,0:T(1,128)S(1)}, f32[1,384]{1,0:T(1,128)S(1)}, u32[]{:S(2)}, u32[]{:S(2)}) collective-permute-start(f32[1,384]{1,0:T(1,128)S(1)} %get-tuple-element.25), channel_id=1, source_target_pairs={{0,16},{4,20},{8,24},{12,28},{16,32},{20,36},{24,40},{28,44},{32,4... | collective-permute-start | bytes 4616 | tf_op jit(solution)/shard_map/ppermute | solution.py:399
  50.0 6.6 %collective-permute-start.2 = (f32[1,384]{1,0:T(1,128)S(1)}, f32[1,384]{1,0:T(1,128)S(1)}, u32[]{:S(2)}, u32[]{:S(2)}) collective-permute-start(f32[1,384]{1,0:T(1,128)S(1)} %get-tuple-element.26), channel_id=1, source_target_pairs={{0,48},{4,52},{8,56},{12,60},{16,0},{20,4},{24,8},{28,12},{32,16},... | collective-permute-start | bytes 4616 | tf_op jit(solution)/shard_map/ppermute | solution.py:399
  51.3 7.7 %collective-permute-start.1 = (f32[1,384]{1,0:T(1,128)S(1)}, f32[1,384]{1,0:T(1,128)S(1)}, u32[]{:S(2)}, u32[]{:S(2)}) collective-permute-start(f32[1,384]{1,0:T(1,128)S(1)} %get-tuple-element.27), channel_id=1, source_target_pairs={{0,32},{4,36},{8,40},{12,44},{16,48},{20,52},{24,56},{28,60},{32,0... | collective-permute-start | bytes 4616 | tf_op jit(solution)/shard_map/ppermute | solution.py:399
  59.6 4.6 %collective-permute-start.5 = (bf16[264,128]{1,0:T(8,128)(2,1)S(1)}, bf16[264,128]{1,0:T(8,128)(2,1)S(1)}, u32[]{:S(2)}, u32[]{:S(2)}) collective-permute-start(bf16[264,128]{1,0:T(8,128)(2,1)S(1)} %get-tuple-element.24), channel_id=1, source_target_pairs={{0,3},{1,0},{2,1},{3,2},{4,7},{5,4},{6,5},{7,6},{8,11},{9,8},{10,9... | collective-permute-start | bytes 202760 | tf_op jit(solution)/shard_map/ppermute | solution.py:406
  62.5 4.7 %collective-permute-start.4 = (bf16[264,128]{1,0:T(8,128)(2,1)S(1)}, bf16[264,128]{1,0:T(8,128)(2,1)S(1)}, u32[]{:S(2)}, u32[]{:S(2)}) collective-permute-start(bf16[264,128]{1,0:T(8,128)(2,1)S(1)} %get-tuple-element.24), channel_id=1, source_target_pairs={{0,2},{1,3},{2,0},{3,1},{4,6},{5,7},{6,4},{7,5},{8,10},{9,11},{10,... | collective-permute-start | bytes 202760 | tf_op jit(solution)/shard_map/ppermute | solution.py:406
  62.8 6.1 %collective-permute-start.3 = (bf16[264,128]{1,0:T(8,128)(2,1)S(1)}, bf16[264,128]{1,0:T(8,128)(2,1)S(1)}, u32[]{:S(2)}, u32[]{:S(2)}) collective-permute-start(bf16[264,128]{1,0:T(8,128)(2,1)S(1)} %get-tuple-element.24), channel_id=1, source_target_pairs={{0,1},{1,2},{2,3},{3,0},{4,5},{5,6},{6,7},{7,4},{8,9},{9,10},{10,1... | collective-permute-start | bytes 202760 | tf_op jit(solution)/shard_map/ppermute | solution.py:406

commit v7 on v6

--- a/solution.py
+++ b/solution.py
@@ -7,6 +7,7 @@
 from jax.experimental import pallas as pl
 from jax.experimental.pallas import tpu as pltpu
 from jax.sharding import PartitionSpec as P
+
 
 NSTEPS = 4
 TAPER = 0.6
@@ -16,7 +17,7 @@
 PAIR = 2
 GROUPS = PLANES // PAIR
 WIDTH = 512
-EXTRA = 8
+EXTRA = 16
 VMEM_LIMIT = 16 << 20
 FIRST_LIMIT = 62 << 20
 BF16 = jnp.bfloat16
@@ -83,14 +84,10 @@
     owner_in,
     precision_in,
     obs_in,
-    innovation_in,
-    listed_in,
     rows_out,
     owner_ref,
     precision_ref,
     obs_ref,
-    innovation_ref,
-    listed_ref,
     rows_ref,
     arrivals,
     departures,
@@ -98,13 +95,7 @@
     copies = [
         pltpu.make_async_copy(source, target, arrivals.at[index])
         for index, (source, target) in enumerate(
-            [
-                (owner_in, owner_ref),
-                (precision_in, precision_ref),
-                (obs_in, obs_ref),
-                (innovation_in, innovation_ref),
-                (listed_in, listed_ref),
-            ]
+            [(owner_in, owner_ref), (precision_in, precision_ref), (obs_in, obs_ref)]
         )
     ]
     for copy in copies:
@@ -129,8 +120,7 @@
     copies[1].wait()
     precision = precision_ref[...].astype(F32)
     scale = jnp.sqrt(precision)
-    for copy in copies[2:]:
-        copy.wait()
+    copies[2].wait()
     obs = obs_ref[...]
 
     span = GROUPS * capacity
@@ -140,41 +130,43 @@
         hit = slots == iota((at_once * span, count), 0) + start * span
         placed = dot(jnp.where(hit, scale, 0.0).astype(BF16), obs).astype(BF16)
         for k in range(at_once):
-            rows_ref[start + k, :span, :] = placed[k * span : (k + 1) * span]
+            rows_ref[start + k] = placed[k * span : (k + 1) * span]
         if start == 0:
-            part = (slice(0, at_once), slice(0, span))
+            part = slice(0, at_once)
             copy = pltpu.make_async_copy(rows_ref.at[part], rows_out.at[part], departures.at[0])
             copy.start()
             leaving = [copy]
 
-    factor = precision * innovation_ref[...].astype(F32)
-    hit = iota((regions, count), 0) == owners
-    sums = split(dot(jnp.where(hit, factor, 0.0).astype(BF16), obs))
-    half = obs[:, LANES:].astype(F32)
-    squares = split(dot(jnp.where(hit, precision, 0.0).astype(BF16), (half * half).astype(BF16)))
-    weight = split(weights_transposed(listed_ref[...]))
-    row = iota((regions, sites * EXTRA), 1)
-    place, item = row // EXTRA, row % EXTRA
-
-    def chosen(group, valid):
-        pick = onehot((iota((regions, sites * EXTRA), 0) == region_at(place, group)) & valid)
-        return split(dot(weight[0], pick) + dot(weight[1], pick))
-
-    over = ((0,), (0,))
-    second = (item - GROUPS) * 2
-    is_diag = (item >= GROUPS) & (item < GROUPS + GROUPS // 2)
-    extra = dot3(chosen(item, item < GROUPS), sums, over)
-    left = dot3(chosen(second, is_diag), squares, over)
-    right = dot3(chosen(second + 1, is_diag), squares, over)
-    extra = (extra + jnp.concatenate([left, right], axis=1)).astype(BF16)
-    rows_ref[:, span:, :] = extra.reshape(sites, EXTRA, extra.shape[1])
-    rest = [(slice(0, at_once), slice(span, span + EXTRA)), (slice(at_once, sites), slice(0, span + EXTRA))]
-    for index, part in enumerate(rest):
-        copy = pltpu.make_async_copy(rows_ref.at[part], rows_out.at[part], departures.at[index + 1])
-        copy.start()
-        leaving.append(copy)
+    part = slice(at_once, sites)
+    copy = pltpu.make_async_copy(rows_ref.at[part], rows_out.at[part], departures.at[1])
+    copy.start()
+    leaving.append(copy)
     for copy in leaving:
         copy.wait()
+
+
+def sums_kernel(owner_ref, precision_ref, innovation_ref, obs_ref, listed_ref, sums_ref):
+    count = owner_ref.shape[1]
+    regions = listed_ref.shape[1]
+    places, lines, _ = sums_ref.shape
+    obs = obs_ref[...]
+    precision = precision_ref[...].astype(F32)
+    factor = precision * innovation_ref[...].astype(F32)
+    hit = iota((regions, count), 0) == owner_ref[...]
+    sums = dot(jnp.where(hit, factor, 0.0).astype(BF16), obs)
+    half = obs[:, LANES:].astype(F32)
+    squares = dot(jnp.where(hit, precision, 0.0).astype(BF16), (half * half).astype(BF16))
+    weight = split(weights_transposed(listed_ref[...]))
+    row = iota((regions, places * lines), 1)
+    item = row % lines
+    pick = iota((regions, places * lines), 0) == region_at(row // lines, item // 3)
+    pick = onehot(pick & (item < 3 * GROUPS))
+    chosen = split(dot(weight[0], pick) + dot(weight[1], pick))
+    over = ((0,), (0,))
+    parts = [dot3(chosen, split(value), over) for value in (sums[:, :LANES], sums[:, LANES:], squares)]
+    kind = iota((places * lines, LANES), 0) % lines % 3
+    mixed = jnp.where(kind == 0, parts[0], jnp.where(kind == 1, parts[1], parts[2]))
+    sums_ref[...] = mixed.astype(BF16).reshape(places, lines, LANES)
 
 
 def weight_kernel(listed_ref, high_ref, low_ref):
@@ -193,7 +185,7 @@
     low_ref[...] = low
 
 
-def covariance_kernel(capacity, rows_ref, message_ref, sums_ref):
+def covariance_kernel(capacity, rows_ref, sums_ref, message_ref):
     half = LANES
     members = rows_ref.shape[2]
     places = message_ref.shape[0]
@@ -205,19 +197,17 @@
         corner = jnp.where(above, total[:half, :half], total[half:, half:])
         packed = jnp.concatenate([corner, total[:half, half:]], axis=0).astype(BF16)
         message_ref[:, group * piece : (group + 1) * piece, :] = packed.reshape(places, piece, LANES)
-    span = GROUPS * capacity
-    sums = jnp.sum(rows_ref[:, span : span + EXTRA, :].astype(F32), axis=0)
+    message_ref[:, GROUPS * piece :, :] = sums_ref[...]
+
+
+def mix_kernel(message_ref, high_ref, low_ref, mixed_ref, sums_ref):
+    regions, piece, _ = mixed_ref.shape
+    span = GROUPS * piece
+    message = message_ref[:, :span, :].reshape(regions, piece, LANES)
+    sums = jnp.sum(message_ref[:, span:, :].astype(F32), axis=0)
     for group in range(GROUPS):
-        at, inner = GROUPS + group // 2, group % 2
-        diagonal = sums[at : at + 1, inner * half : (inner + 1) * half]
-        row = jnp.concatenate([sums[group : group + 1], diagonal], axis=1)
-        sums_ref[group : group + 1, :] = row
-
-
-def mix_kernel(message_ref, high_ref, low_ref, mixed_ref):
-    places, rows, _ = message_ref.shape
-    regions, piece, _ = mixed_ref.shape
-    message = message_ref[...].reshape(regions, piece, LANES)
+        row = [sums[3 * group + part : 3 * group + part + 1] for part in range(3)]
+        sums_ref[group : group + 1, :] = jnp.concatenate(row, axis=1)
     parts = [
         message[:, at : at + SUBLANES, :].reshape(regions * SUBLANES, LANES) for at in range(0, piece, SUBLANES)
     ]
@@ -296,11 +286,9 @@
             root_iter = dot3(root_split, correction)
         inverse_iter = dot3(correction, inverse_split)
     root = inverse_iter * (1.0 / jnp.sqrt(norm_scale))
-    root_split = split(root)
     innovation = jnp.concatenate([extra[0:1], extra[1:2]], axis=1)
-    innovation = jnp.broadcast_to(innovation, (SUBLANES, size))
-    inner = dot3(split(innovation), root_split)
-    mean_shift = dot3(split(inner), root_split)[0:1, :]
+    inner = jnp.sum(root * innovation, axis=1, keepdims=True)
+    mean_shift = jnp.sum(inner * root, axis=0, keepdims=True)
     transform = (math.sqrt(size - 1.0) * root + mean_shift).astype(BF16)
     copies = []
     for step, at in enumerate(range(0, anomaly_ref.shape[1], WIDTH)):
@@ -337,7 +325,7 @@
     )(*args)
 
 
-def body(ensemble, obs_anomaly, innovation, obs_precision, owner_region, neighbours):
+def step(ensemble, obs_anomaly, innovation, obs_precision, owner_region, neighbours):
     regions = lax.axis_size("region")
     levels = lax.axis_size("level")
     my_region = lax.axis_index("region")
@@ -349,15 +337,13 @@
     owners = owner_region.reshape(1, local_obs)
     listed = neighbours.T
     shape = jax.ShapeDtypeStruct
-    block = (places, GROUPS * capacity + EXTRA, members)
+    block = (places, GROUPS * capacity, members)
     rows = call(
         functools.partial(place_kernel, regions, capacity),
         shape(block, BF16),
         owners,
         obs_precision,
         obs_anomaly[0],
-        innovation,
-        listed,
         limit=FIRST_LIMIT,
         space=pl.ANY,
         inputs=pl.ANY,
@@ -365,11 +351,9 @@
             pltpu.VMEM(owners.shape, jnp.int32),
             pltpu.VMEM(obs_precision.shape, BF16),
             pltpu.VMEM((local_obs, members), BF16),
-            pltpu.VMEM(innovation.shape, BF16),
-            pltpu.VMEM(listed.shape, jnp.int32),
             pltpu.VMEM(block, BF16),
-            pltpu.SemaphoreType.DMA((5,)),
             pltpu.SemaphoreType.DMA((3,)),
+            pltpu.SemaphoreType.DMA((2,)),
         ],
     )
     near = [[region_at(place, group) for place in range(places)] for group in range(GROUPS)]
@@ -378,14 +362,29 @@
     high, low = call(
         weight_kernel, (shape((regions * SUBLANES, regions * SUBLANES), BF16),) * 2, listed
     )
-    message, parts = call(
+    sums = call(
+        sums_kernel,
+        shape((places, EXTRA, LANES), BF16),
+        owners,
+        obs_precision,
+        innovation,
+        obs_anomaly[0],
+        listed,
+    )
+    message = call(
         functools.partial(covariance_kernel, capacity),
-        (shape((places, GROUPS * piece, LANES), BF16), shape((GROUPS, members + LANES), F32)),
+        shape((places, GROUPS * piece + EXTRA, LANES), BF16),
         routed,
+        sums,
     )
     message = lax.all_to_all(message, "region", 0, 0, tiled=True, axis_index_groups=near)
-    mixed = call(mix_kernel, shape((regions, piece, LANES), BF16), message, high, low)
-    mixed, parts = lax.optimization_barrier((mixed, parts))
+    mixed, parts = call(
+        mix_kernel,
+        (shape((regions, piece, LANES), BF16), shape((GROUPS, members + LANES), F32)),
+        message,
+        high,
+        low,
+    )
     pieces = lax.all_to_all(mixed, "region", 0, 0, tiled=True)
 
     my_group = my_region // CORES % PLANES // PAIR
@@ -408,7 +407,10 @@
     ]
     columns = ensemble.shape[2]
     average, anomaly = call(
-        anomaly_kernel, (shape((1, columns), F32), shape((members, columns), BF16)), ensemble[0]
+        anomaly_kernel,
+        (shape((1, columns), F32), shape((members, columns), BF16)),
+        ensemble[0],
+        limit=FIRST_LIMIT,
     )
     analysis = call(
         functools.partial(transform_kernel, levels),
@@ -430,7 +432,7 @@
 
 def solution(mesh):
     return jax.shard_map(
-        body,
+        step,
         mesh=mesh,
         in_specs=(
             P("level", None, "region"),

time: 73.5 us -> 75.2 us (1.023)
  blocking collectives: 21.2 us -> 0 us
  waiting for transfers between devices: 14.7 us -> 25.1 us
  starting transfers between devices: 25.5 us -> 32.6 us
  Pallas kernels: 11.6 us -> 14.4 us
  local copies, waits for them, and re-layouts: 0.02 us -> 2.34 us
    all_to_all x1 -> x0, blocking collectives: 21.2 us -> none  [body(): lax.all_to_all(rows, 'region', 0, 0, tiled=True, axis_index_groups=near)]
    all_to_all x2 -> x3, waiting for transfers between devices: 7.63 us -> 21 us  [the longest x1 12.7 us: step(): lax.all_to_all(rows, 'region', 0, 0, tiled=True, axis_index_groups=near)]
    all_to_all x2 -> x3, starting transfers between devices: 12.7 us -> 19.9 us  [the longest x1 9.2 us: step(): pieces = lax.all_to_all(mixed, 'region', 0, 0, tiled=True)]
    ppermute x6, waiting for transfers between devices: 7.08 us -> 4.16 us  [the longest x3 2.39 us: step(): part = part + lax.ppermute(sent, 'region', pairs)]
    pallas_call x7 -> x8, Pallas kernels: 11.6 us -> 14.4 us  [call(): pl.pallas_call(kernel, out_shape=shapes, in_specs=[pl.BlockSpec(memory_sp...]
    unnamed x4 -> x14, local copies, waits for them, and re-layouts: 0.01 us -> 2.33 us
  transfers between devices with their start and end apart: 8 -> 9, of which waited for: 5 -> 5; matrix products, arithmetic and copies ran while one was open for 0% -> 0% of each run, Pallas kernels for 2% -> 7%
where the time goes in v7:
time: 75.2 us; the launch traced here: 74.8 us
  starting transfers between devices  32.6 us (43%)
  waiting for transfers between devices  25.1 us (33%)
  Pallas kernels  14.4 us (19%)
  local copies, waits for them, and re-layouts  2.34 us (3%)
    pallas_call x8, Pallas kernels, call(): pl.pallas_call(kernel, out_shape=shapes, in_specs=[pl.BlockSpec(memory_sp...  14.4 us
    all_to_all x1, waiting for transfers between devices, step(): lax.all_to_all(rows, 'region', 0, 0, tiled=True, axis_index_groups=near)  12.7 us
    all_to_all x1, starting transfers between devices, step(): pieces = lax.all_to_all(mixed, 'region', 0, 0, tiled=True)  9.2 us
    ppermute x3, starting transfers between devices, step(): part = part + lax.ppermute(sent, 'region', pairs)  8.92 us
    all_to_all x1, waiting for transfers between devices, step(): lax.all_to_all(message, 'region', 0, 0, tiled=True, axis_index_groups=near)  7.75 us
    all_to_all x1, starting transfers between devices, step(): lax.all_to_all(rows, 'region', 0, 0, tiled=True, axis_index_groups=near)  7.17 us
    ppermute x3, starting transfers between devices, step(): lax.ppermute(sent, 'level', [(o, (o + ahead) % levels) for o in range(lev...  3.85 us
    all_to_all x1, starting transfers between devices, step(): lax.all_to_all(message, 'region', 0, 0, tiled=True, axis_index_groups=near)  3.5 us
  transfers between devices with their start and end apart: 9, of which 5 were waited for; matrix products, arithmetic and copies ran while one was open for 0% of the time, Pallas kernels for 7%

profile of v7, /device:TPU:1, one launch (start us, length us, event | category | flops | bytes accessed | tf_op | source)
XLA Modules:
  0.0 74.8 jit_solution(14692740214249171911)
XLA Ops:
  0.0 0.0 copy-start.5
  0.0 3.0 %shard_map.65 = bf16[16,96,256]{2,1,0:T(8,128)(2,1)} custom-call(s32[1,1024]{1,0:T(1,128)} %bitcast.8, bf16[1,1024]{1,0:T(2,128)(2,1)} %precision_ref.1, bf16[1024,256]{1,0:T(8,128)(2,1)} %bitcast.6), custom_call_target="tpu_custom_call" | custom-call | tf_op jit(solution)/shard_map/pallas_call | solution.py:318
  3.1 7.2 %all-to-all-start = ((bf16[16,96,256]{2,1,0:T(8,128)(2,1)}), bf16[16,96,256]{2,1,0:T(8,128)(2,1)S(1)}, u32[]{:S(2)}, u32[]{:S(2)}) async-start(bf16[16,96,256]{2,1,0:T(8,128)(2,1)} %shard_map.65), calls=%async_computation | async-start | bytes 1572864 | tf_op jit(solution)/shard_map/all_to_all | solution.py:360
  10.2 0.0 copy-done.3
  10.3 0.0 copy-done.1
  10.3 0.0 copy-done.5
  10.3 0.0 copy-done.6
  10.3 0.6 shard_map.66.sums_ref
  10.9 12.7 %all-to-all-done.rows_ref = bf16[16,96,256]{2,1,0:T(8,128)(2,1)S(1)} async-done(((bf16[16,96,256]{2,1,0:T(8,128)(2,1)}), bf16[16,96,256]{2,1,0:T(8,128)(2,1)S(1)}, u32[]{:S(2)}, u32[]{:S(2)}) %all-to-all-start) | async-done | bytes 786464 | tf_op jit(solution)/shard_map/all_to_all | solution.py:360
  23.6 1.2 %shard_map.67 = bf16[16,80,128]{2,1,0:T(8,128)(2,1)} custom-call(bf16[16,96,256]{2,1,0:T(8,128)(2,1)S(1)} %all-to-all-done.rows_ref, bf16[16,16,128]{2,1,0:T(8,128)(2,1)S(1)} %shard_map.66.sums_ref), custom_call_target="tpu_custom_call" | custom-call | tf_op jit(solution)/shard_map/pallas_call | solution.py:318
  24.8 3.5 %all-to-all-start.1 = ((bf16[16,80,128]{2,1,0:T(8,128)(2,1)}), bf16[16,80,128]{2,1,0:T(8,128)(2,1)S(1)}, u32[]{:S(2)}, u32[]{:S(2)}) async-start(bf16[16,80,128]{2,1,0:T(8,128)(2,1)} %shard_map.67), calls=%async_computation.1 | async-start | bytes 655360 | tf_op jit(solution)/shard_map/all_to_all | solution.py:380
  28.3 0.7 shard_map.68
  29.0 7.8 %all-to-all-done.1.message_ref = bf16[16,80,128]{2,1,0:T(8,128)(2,1)S(1)} async-done(((bf16[16,80,128]{2,1,0:T(8,128)(2,1)}), bf16[16,80,128]{2,1,0:T(8,128)(2,1)S(1)}, u32[]{:S(2)}, u32[]{:S(2)}) %all-to-all-start.1) | async-done | bytes 327712 | tf_op jit(solution)/shard_map/all_to_all | solution.py:380
  36.7 1.1 %shard_map.69 = (bf16[64,16,128]{2,1,0:T(8,128)(2,1)}, f32[4,384]{1,0:T(4,128)S(1)}) custom-call(bf16[16,80,128]{2,1,0:T(8,128)(2,1)S(1)} %all-to-all-done.1.message_ref, bf16[512,512]{1,0:T(8,128)(2,1)S(1)} %get-tuple-element.15.high_ref, bf16[512,512]{1,0:T(8,128)(2,1)S(1)} %get-tuple-element.16.low_ref), custom_call_target="tpu_custom_call" | custom-call | tf_op jit(solution)/shard_map/pallas_call | solution.py:318
  37.9 9.2 %all-to-all-start.2 = ((bf16[64,16,128]{2,1,0:T(8,128)(2,1)}), bf16[64,16,128]{2,1,0:T(8,128)(2,1)S(1)}, u32[]{:S(2)}, u32[]{:S(2)}) async-start(bf16[64,16,128]{2,1,0:T(8,128)(2,1)} %get-tuple-element.17), calls=%async_computation.2 | async-start | bytes 524288 | tf_op jit(solution)/shard_map/all_to_all | solution.py:388
  47.2 2.3 %collective-permute-start = (f32[1,384]{1,0:T(1,128)S(1)}, f32[1,384]{1,0:T(1,128)S(1)}, u32[]{:S(2)}, u32[]{:S(2)}) collective-permute-start(f32[1,384]{1,0:T(1,128)S(1)} %get-tuple-element.21), channel_id=1, source_target_pairs={{0,16},{4,20},{8,24},{12,28},{16,32},{20,36},{24,40},{28,44},{32,4... | collective-permute-start | bytes 4616 | tf_op jit(solution)/shard_map/ppermute | solution.py:398
  49.5 1.3 %collective-permute-start.2 = (f32[1,384]{1,0:T(1,128)S(1)}, f32[1,384]{1,0:T(1,128)S(1)}, u32[]{:S(2)}, u32[]{:S(2)}) collective-permute-start(f32[1,384]{1,0:T(1,128)S(1)} %get-tuple-element.22), channel_id=1, source_target_pairs={{0,48},{4,52},{8,56},{12,60},{16,0},{20,4},{24,8},{28,12},{32,16},... | collective-permute-start | bytes 4616 | tf_op jit(solution)/shard_map/ppermute | solution.py:398
  50.9 5.3 %collective-permute-start.1 = (f32[1,384]{1,0:T(1,128)S(1)}, f32[1,384]{1,0:T(1,128)S(1)}, u32[]{:S(2)}, u32[]{:S(2)}) collective-permute-start(f32[1,384]{1,0:T(1,128)S(1)} %get-tuple-element.23), channel_id=1, source_target_pairs={{0,32},{4,36},{8,40},{12,44},{16,48},{20,52},{24,56},{28,60},{32,0... | collective-permute-start | bytes 4616 | tf_op jit(solution)/shard_map/ppermute | solution.py:398
  56.1 0.0 collective-permute-done
  56.1 0.0 collective-permute-done.2
  56.1 2.4 %collective-permute-done.1 = f32[1,384]{1,0:T(1,128)S(1)} collective-permute-done((f32[1,384]{1,0:T(1,128)S(1)}, f32[1,384]{1,0:T(1,128)S(1)}, u32[]{:S(2)}, u32[]{:S(2)}) %collective-permute-start.1) | collective-permute-done | bytes 1568 | tf_op jit(solution)/shard_map/ppermute | solution.py:398
  58.5 0.6 all-to-all-done.2.pieces_ref
  59.2 2.8 %collective-permute-start.5 = (bf16[264,128]{1,0:T(8,128)(2,1)S(1)}, bf16[264,128]{1,0:T(8,128)(2,1)S(1)}, u32[]{:S(2)}, u32[]{:S(2)}) collective-permute-start(bf16[264,128]{1,0:T(8,128)(2,1)S(1)} %get-tuple-element.20), channel_id=1, source_target_pairs={{0,3},{1,0},{2,1},{3,2},{4,7},{5,4},{6,5},{7,6},{8,11},{9,8},{10,9... | collective-permute-start | bytes 202760 | tf_op jit(solution)/shard_map/ppermute | solution.py:405
  62.0 0.3 collective-permute-start.4
  62.3 0.7 collective-permute-start.3
  63.0 3.7 %shard_map.64 = (f32[1,4096]{1,0:T(1,128)}, bf16[256,4096]{1,0:T(8,128)(2,1)}) custom-call(bf16[256,4096]{1,0:T(8,128)(2,1)} %bitcast.12), custom_call_target="tpu_custom_call" | custom-call | tf_op jit(solution)/shard_map/pallas_call | solution.py:318
  66.7 0.0 collective-permute-done.5.refs_2_
  66.7 0.0 collective-permute-done.4.refs_1_
  66.7 1.8 %collective-permute-done.3.refs_0_ = bf16[264,128]{1,0:T(8,128)(2,1)S(1)} collective-permute-done((bf16[264,128]{1,0:T(8,128)(2,1)S(1)}, bf16[264,128]{1,0:T(8,128)(2,1)S(1)}, u32[]{:S(2)}, u32[]{:S(2)}) %collective-permute-start.3) | collective-permute-done | bytes 67616 | tf_op jit(solution)/shard_map/ppermute | solution.py:405
  68.5 1.6 %copy-done = bf16[256,4096]{1,0:T(8,128)(2,1)S(1)} copy-done((bf16[256,4096]{1,0:T(8,128)(2,1)S(1)}, bf16[256,4096]{1,0:T(8,128)(2,1)}, u32[]{:S(2)}) %copy-start) | copy-done | bytes 2097176
  70.0 0.7 copy-done.2
  70.8 4.0 %shard_map.71 = bf16[256,4096]{1,0:T(8,128)(2,1)} custom-call(s32[1]{0:T(128)} %bitcast.level_ref, f32[1,4096]{1,0:T(1,128)S(1)} %copy-done.2, bf16[256,4096]{1,0:T(8,128)(2,1)S(1)} %copy-done, f32[264,128]{1,0:T(8,128)S(1)} %get-tuple-element.19.own_ref, bf16[264,128]{1,0:T(8,128)(2,1)S(1)} %collective-permute-done.3.refs_0_, ...), custom_call_target="tpu_custom_call" | custom-call | tf_op jit(solution)/shard_map/pallas_call | solution.py:318
  (10 shorter events, 0.1 us)
Async XLA Ops:
  0.0 10.2 %copy-start.4 = (bf16[1,1024]{1,0:T(2,128)(2,1)S(1)}, bf16[1,1024]{1,0:T(2,128)(2,1)}, u32[]{:S(2)}) copy-start(bf16[1,1024]{1,0:T(2,128)(2,1)} %precision_ref.1) | copy-start | bytes 6148
  0.0 10.2 %copy-start.3 = (s32[1,1024,1]{1,2,0:T(1,128)S(1)}, s32[1,1024,1]{1,2,0:T(1,128)}, u32[]{:S(2)}) copy-start(s32[1,1024,1]{1,2,0:T(1,128)} %param.10) | copy-start | bytes 12292
  0.0 10.3 %copy-start.1 = (bf16[1,1024,256]{2,1,0:T(8,128)(2,1)S(1)}, bf16[1,1024,256]{2,1,0:T(8,128)(2,1)}, u32[]{:S(2)}) copy-start(bf16[1,1024,256]{2,1,0:T(8,128)(2,1)} %param.7) | copy-start | bytes 1572868
  0.0 10.3 %copy-start.5 = (s32[64,3]{0,1:T(4,128)S(1)}, s32[64,3]{0,1:T(4,128)}, u32[]{:S(2)}) copy-start(s32[64,3]{0,1:T(4,128)} %param.11) | copy-start | bytes 2308
  0.0 10.3 %copy-start.6 = (bf16[1,1024]{1,0:T(2,128)(2,1)S(1)}, bf16[1,1024]{1,0:T(2,128)(2,1)}, u32[]{:S(2)}) copy-start(bf16[1,1024]{1,0:T(2,128)(2,1)} %innovation_ref.1) | copy-start | bytes 6148
  3.1 20.5 %all-to-all-start = ((bf16[16,96,256]{2,1,0:T(8,128)(2,1)}), bf16[16,96,256]{2,1,0:T(8,128)(2,1)S(1)}, u32[]{:S(2)}, u32[]{:S(2)}) async-start(bf16[16,96,256]{2,1,0:T(8,128)(2,1)} %shard_map.65), calls=%async_computation | async-start | bytes 1572864 | tf_op jit(solution)/shard_map/all_to_all | solution.py:360
  24.8 12.0 %all-to-all-start.1 = ((bf16[16,80,128]{2,1,0:T(8,128)(2,1)}), bf16[16,80,128]{2,1,0:T(8,128)(2,1)S(1)}, u32[]{:S(2)}, u32[]{:S(2)}) async-start(bf16[16,80,128]{2,1,0:T(8,128)(2,1)} %shard_map.67), calls=%async_computation.1 | async-start | bytes 655360 | tf_op jit(solution)/shard_map/all_to_all | solution.py:380
  37.9 21.2 %all-to-all-start.2 = ((bf16[64,16,128]{2,1,0:T(8,128)(2,1)}), bf16[64,16,128]{2,1,0:T(8,128)(2,1)S(1)}, u32[]{:S(2)}, u32[]{:S(2)}) async-start(bf16[64,16,128]{2,1,0:T(8,128)(2,1)} %get-tuple-element.17), calls=%async_computation.2 | async-start | bytes 524288 | tf_op jit(solution)/shard_map/all_to_all | solution.py:388
  47.2 8.9 %collective-permute-start = (f32[1,384]{1,0:T(1,128)S(1)}, f32[1,384]{1,0:T(1,128)S(1)}, u32[]{:S(2)}, u32[]{:S(2)}) collective-permute-start(f32[1,384]{1,0:T(1,128)S(1)} %get-tuple-element.21), channel_id=1, source_target_pairs={{0,16},{4,20},{8,24},{12,28},{16,32},{20,36},{24,40},{28,44},{32,4... | collective-permute-start | bytes 4616 | tf_op jit(solution)/shard_map/ppermute | solution.py:398
  49.5 6.6 %collective-permute-start.2 = (f32[1,384]{1,0:T(1,128)S(1)}, f32[1,384]{1,0:T(1,128)S(1)}, u32[]{:S(2)}, u32[]{:S(2)}) collective-permute-start(f32[1,384]{1,0:T(1,128)S(1)} %get-tuple-element.22), channel_id=1, source_target_pairs={{0,48},{4,52},{8,56},{12,60},{16,0},{20,4},{24,8},{28,12},{32,16},... | collective-permute-start | bytes 4616 | tf_op jit(solution)/shard_map/ppermute | solution.py:398
  50.9 7.7 %collective-permute-start.1 = (f32[1,384]{1,0:T(1,128)S(1)}, f32[1,384]{1,0:T(1,128)S(1)}, u32[]{:S(2)}, u32[]{:S(2)}) collective-permute-start(f32[1,384]{1,0:T(1,128)S(1)} %get-tuple-element.23), channel_id=1, source_target_pairs={{0,32},{4,36},{8,40},{12,44},{16,48},{20,52},{24,56},{28,60},{32,0... | collective-permute-start | bytes 4616 | tf_op jit(solution)/shard_map/ppermute | solution.py:398
  59.2 7.5 %collective-permute-start.5 = (bf16[264,128]{1,0:T(8,128)(2,1)S(1)}, bf16[264,128]{1,0:T(8,128)(2,1)S(1)}, u32[]{:S(2)}, u32[]{:S(2)}) collective-permute-start(bf16[264,128]{1,0:T(8,128)(2,1)S(1)} %get-tuple-element.20), channel_id=1, source_target_pairs={{0,3},{1,0},{2,1},{3,2},{4,7},{5,4},{6,5},{7,6},{8,11},{9,8},{10,9... | collective-permute-start | bytes 202760 | tf_op jit(solution)/shard_map/ppermute | solution.py:405
  62.0 4.7 %collective-permute-start.4 = (bf16[264,128]{1,0:T(8,128)(2,1)S(1)}, bf16[264,128]{1,0:T(8,128)(2,1)S(1)}, u32[]{:S(2)}, u32[]{:S(2)}) collective-permute-start(bf16[264,128]{1,0:T(8,128)(2,1)S(1)} %get-tuple-element.20), channel_id=1, source_target_pairs={{0,2},{1,3},{2,0},{3,1},{4,6},{5,7},{6,4},{7,5},{8,10},{9,11},{10,... | collective-permute-start | bytes 202760 | tf_op jit(solution)/shard_map/ppermute | solution.py:405
  62.3 6.1 %collective-permute-start.3 = (bf16[264,128]{1,0:T(8,128)(2,1)S(1)}, bf16[264,128]{1,0:T(8,128)(2,1)S(1)}, u32[]{:S(2)}, u32[]{:S(2)}) collective-permute-start(bf16[264,128]{1,0:T(8,128)(2,1)S(1)} %get-tuple-element.20), channel_id=1, source_target_pairs={{0,1},{1,2},{2,3},{3,0},{4,5},{5,6},{6,7},{7,4},{8,9},{9,10},{10,1... | collective-permute-start | bytes 202760 | tf_op jit(solution)/shard_map/ppermute | solution.py:405
  68.5 1.6 %copy-start = (bf16[256,4096]{1,0:T(8,128)(2,1)S(1)}, bf16[256,4096]{1,0:T(8,128)(2,1)}, u32[]{:S(2)}) copy-start(bf16[256,4096]{1,0:T(8,128)(2,1)} %get-tuple-element.14.anomaly_ref) | copy-start | bytes 6291460
  70.0 0.7 copy-start.2

commit v8 on v7

--- a/solution.py
+++ b/solution.py
@@ -124,23 +124,20 @@
     obs = obs_ref[...]
 
     span = GROUPS * capacity
-    at_once = 8
+    at_once = 4
+    leaving = []
     sites = regions // GROUPS
     for start in range(0, sites, at_once):
         hit = slots == iota((at_once * span, count), 0) + start * span
         placed = dot(jnp.where(hit, scale, 0.0).astype(BF16), obs).astype(BF16)
         for k in range(at_once):
             rows_ref[start + k] = placed[k * span : (k + 1) * span]
-        if start == 0:
-            part = slice(0, at_once)
-            copy = pltpu.make_async_copy(rows_ref.at[part], rows_out.at[part], departures.at[0])
-            copy.start()
-            leaving = [copy]
-
-    part = slice(at_once, sites)
-    copy = pltpu.make_async_copy(rows_ref.at[part], rows_out.at[part], departures.at[1])
-    copy.start()
-    leaving.append(copy)
+        part = slice(start, start + at_once)
+        copy = pltpu.make_async_copy(
+            rows_ref.at[part], rows_out.at[part], departures.at[start // at_once]
+        )
+        copy.start()
+        leaving.append(copy)
     for copy in leaving:
         copy.wait()
 
@@ -273,18 +270,28 @@
     matrix = matrix + jnp.where(same, size - 1.0, 0.0)
     squares = jnp.sum(jnp.sum(matrix * matrix, axis=0, keepdims=True), axis=1, keepdims=True)
     norm_scale = 0.5 * jnp.sqrt(squares)
+    inverse_scale = 1.0 / norm_scale
     diagonal = jnp.where(same, 1.5, 0.0)
-    root_iter = matrix * (1.0 / norm_scale)
-    correction = diagonal - 0.5 * root_iter
-    inverse_iter = correction
-    root_iter = dot3(split(root_iter), split(correction), halves=True)
+    first_split = split(matrix)
+    second_power = dot3(first_split, first_split, halves=True)
+    third_power = dot3(first_split, split(second_power), halves=True)
+    product = matrix * inverse_scale
+    inverse_iter = diagonal - 0.5 * product
+    product = (
+        2.25 * product
+        - (1.5 * inverse_scale**2) * second_power
+        + (0.25 * inverse_scale**3) * third_power
+    )
     for newton_step in range(1, NSTEPS):
-        inverse_split = split(inverse_iter)
-        root_split = split(root_iter)
-        correction = split(diagonal - 0.5 * dot3(inverse_split, root_split, halves=True))
+        factor = split(product)
         if newton_step < NSTEPS - 1:
-            root_iter = dot3(root_split, correction)
-        inverse_iter = dot3(correction, inverse_split)
+            square = dot3(factor, factor)
+            inverse_step = dot3(split(inverse_iter), factor)
+            cube = dot3(factor, split(square), halves=True)
+            product = 2.25 * product - 1.5 * square + 0.25 * cube
+        else:
+            inverse_step = dot3(split(inverse_iter), factor, halves=True)
+        inverse_iter = 1.5 * inverse_iter - 0.5 * inverse_step
     root = inverse_iter * (1.0 / jnp.sqrt(norm_scale))
     innovation = jnp.concatenate([extra[0:1], extra[1:2]], axis=1)
     inner = jnp.sum(root * innovation, axis=1, keepdims=True)
@@ -353,7 +360,7 @@
             pltpu.VMEM((local_obs, members), BF16),
             pltpu.VMEM(block, BF16),
             pltpu.SemaphoreType.DMA((3,)),
-            pltpu.SemaphoreType.DMA((2,)),
+            pltpu.SemaphoreType.DMA((4,)),
         ],
     )
     near = [[region_at(place, group) for place in range(places)] for group in range(GROUPS)]
@@ -395,16 +402,17 @@
         for region in range(regions):
             x, z, core = region_parts(region)
             pairs.append((region, (x * PLANES + (z + PAIR * ahead) % PLANES) * CORES + core))
-        part = part + lax.ppermute(sent, "region", pairs)
+        arrived_part = lax.ppermute(sent, "region", pairs)
+        part = part + arrived_part
 
     height = members + SUBLANES
     own, sent = call(
         gather_kernel, (shape((height, LANES), F32), shape((height, LANES), BF16)), pieces, part
     )
-    arrived = [
-        lax.ppermute(sent, "level", [(o, (o + ahead) % levels) for o in range(levels)])
-        for ahead in range(1, levels)
-    ]
+    arrived = []
+    for ahead in range(1, levels):
+        pairs = [(level, (level + ahead) % levels) for level in range(levels)]
+        arrived.append(lax.ppermute(sent, "level", pairs))
     columns = ensemble.shape[2]
     average, anomaly = call(
         anomaly_kernel,

time: 75.2 us -> 75 us (level)
  no operation moved by 1% of the time
where the time goes in v8:
time: 75 us; the launch traced here: 74.5 us
  starting transfers between devices  32.6 us (43%)
  waiting for transfers between devices  25.1 us (33%)
  Pallas kernels  14.1 us (19%)
  local copies, waits for them, and re-layouts  2.34 us (3%)
    pallas_call x8, Pallas kernels, call(): pl.pallas_call(kernel, out_shape=shapes, in_specs=[pl.BlockSpec(memory_sp...  14.1 us
    all_to_all x1, waiting for transfers between devices, step(): lax.all_to_all(rows, 'region', 0, 0, tiled=True, axis_index_groups=near)  12.7 us
    all_to_all x1, starting transfers between devices, step(): pieces = lax.all_to_all(mixed, 'region', 0, 0, tiled=True)  9.21 us
    ppermute x3, starting transfers between devices, step(): arrived_part = lax.ppermute(sent, 'region', pairs)  8.92 us
    all_to_all x1, waiting for transfers between devices, step(): lax.all_to_all(message, 'region', 0, 0, tiled=True, axis_index_groups=near)  7.75 us
    all_to_all x1, starting transfers between devices, step(): lax.all_to_all(rows, 'region', 0, 0, tiled=True, axis_index_groups=near)  7.17 us
    ppermute x3, starting transfers between devices, step(): arrived.append(lax.ppermute(sent, 'level', pairs))  3.85 us
    all_to_all x1, starting transfers between devices, step(): lax.all_to_all(message, 'region', 0, 0, tiled=True, axis_index_groups=near)  3.5 us
  transfers between devices with their start and end apart: 9, of which 5 were waited for; matrix products, arithmetic and copies ran while one was open for 0% of the time, Pallas kernels for 7%

profile of v8, /device:TPU:1, one launch (start us, length us, event | category | flops | bytes accessed | tf_op | source)
XLA Modules:
  0.0 74.5 jit_solution(290062644151371511)
XLA Ops:
  0.0 0.0 copy-start.5
  0.0 2.9 %shard_map.65 = bf16[16,96,256]{2,1,0:T(8,128)(2,1)} custom-call(s32[1,1024]{1,0:T(1,128)} %bitcast.8, bf16[1,1024]{1,0:T(2,128)(2,1)} %precision_ref.1, bf16[1024,256]{1,0:T(8,128)(2,1)} %bitcast.6), custom_call_target="tpu_custom_call" | custom-call | tf_op jit(solution)/shard_map/pallas_call | solution.py:325
  3.0 7.2 %all-to-all-start = ((bf16[16,96,256]{2,1,0:T(8,128)(2,1)}), bf16[16,96,256]{2,1,0:T(8,128)(2,1)S(1)}, u32[]{:S(2)}, u32[]{:S(2)}) async-start(bf16[16,96,256]{2,1,0:T(8,128)(2,1)} %shard_map.65), calls=%async_computation | async-start | bytes 1572864 | tf_op jit(solution)/shard_map/all_to_all | solution.py:367
  10.1 0.0 copy-done.3
  10.2 0.0 copy-done.1
  10.2 0.0 copy-done.5
  10.2 0.0 copy-done.6
  10.2 0.6 shard_map.66.sums_ref
  10.8 12.7 %all-to-all-done.rows_ref = bf16[16,96,256]{2,1,0:T(8,128)(2,1)S(1)} async-done(((bf16[16,96,256]{2,1,0:T(8,128)(2,1)}), bf16[16,96,256]{2,1,0:T(8,128)(2,1)S(1)}, u32[]{:S(2)}, u32[]{:S(2)}) %all-to-all-start) | async-done | bytes 786464 | tf_op jit(solution)/shard_map/all_to_all | solution.py:367
  23.5 1.2 %shard_map.67 = bf16[16,80,128]{2,1,0:T(8,128)(2,1)} custom-call(bf16[16,96,256]{2,1,0:T(8,128)(2,1)S(1)} %all-to-all-done.rows_ref, bf16[16,16,128]{2,1,0:T(8,128)(2,1)S(1)} %shard_map.66.sums_ref), custom_call_target="tpu_custom_call" | custom-call | tf_op jit(solution)/shard_map/pallas_call | solution.py:325
  24.7 3.5 %all-to-all-start.1 = ((bf16[16,80,128]{2,1,0:T(8,128)(2,1)}), bf16[16,80,128]{2,1,0:T(8,128)(2,1)S(1)}, u32[]{:S(2)}, u32[]{:S(2)}) async-start(bf16[16,80,128]{2,1,0:T(8,128)(2,1)} %shard_map.67), calls=%async_computation.1 | async-start | bytes 655360 | tf_op jit(solution)/shard_map/all_to_all | solution.py:387
  28.2 0.7 shard_map.68
  28.9 7.8 %all-to-all-done.1.message_ref = bf16[16,80,128]{2,1,0:T(8,128)(2,1)S(1)} async-done(((bf16[16,80,128]{2,1,0:T(8,128)(2,1)}), bf16[16,80,128]{2,1,0:T(8,128)(2,1)S(1)}, u32[]{:S(2)}, u32[]{:S(2)}) %all-to-all-start.1) | async-done | bytes 327712 | tf_op jit(solution)/shard_map/all_to_all | solution.py:387
  36.6 1.1 %shard_map.69 = (bf16[64,16,128]{2,1,0:T(8,128)(2,1)}, f32[4,384]{1,0:T(4,128)S(1)}) custom-call(bf16[16,80,128]{2,1,0:T(8,128)(2,1)S(1)} %all-to-all-done.1.message_ref, bf16[512,512]{1,0:T(8,128)(2,1)S(1)} %get-tuple-element.15.high_ref, bf16[512,512]{1,0:T(8,128)(2,1)S(1)} %get-tuple-element.16.low_ref), custom_call_target="tpu_custom_call" | custom-call | tf_op jit(solution)/shard_map/pallas_call | solution.py:325
  37.8 9.2 %all-to-all-start.2 = ((bf16[64,16,128]{2,1,0:T(8,128)(2,1)}), bf16[64,16,128]{2,1,0:T(8,128)(2,1)S(1)}, u32[]{:S(2)}, u32[]{:S(2)}) async-start(bf16[64,16,128]{2,1,0:T(8,128)(2,1)} %get-tuple-element.17), calls=%async_computation.2 | async-start | bytes 524288 | tf_op jit(solution)/shard_map/all_to_all | solution.py:395
  47.1 2.3 %collective-permute-start = (f32[1,384]{1,0:T(1,128)S(1)}, f32[1,384]{1,0:T(1,128)S(1)}, u32[]{:S(2)}, u32[]{:S(2)}) collective-permute-start(f32[1,384]{1,0:T(1,128)S(1)} %get-tuple-element.21), channel_id=1, source_target_pairs={{0,16},{4,20},{8,24},{12,28},{16,32},{20,36},{24,40},{28,44},{32,4... | collective-permute-start | bytes 4616 | tf_op jit(solution)/shard_map/ppermute | solution.py:405
  49.5 1.3 %collective-permute-start.2 = (f32[1,384]{1,0:T(1,128)S(1)}, f32[1,384]{1,0:T(1,128)S(1)}, u32[]{:S(2)}, u32[]{:S(2)}) collective-permute-start(f32[1,384]{1,0:T(1,128)S(1)} %get-tuple-element.22), channel_id=1, source_target_pairs={{0,48},{4,52},{8,56},{12,60},{16,0},{20,4},{24,8},{28,12},{32,16},... | collective-permute-start | bytes 4616 | tf_op jit(solution)/shard_map/ppermute | solution.py:405
  50.8 5.3 %collective-permute-start.1 = (f32[1,384]{1,0:T(1,128)S(1)}, f32[1,384]{1,0:T(1,128)S(1)}, u32[]{:S(2)}, u32[]{:S(2)}) collective-permute-start(f32[1,384]{1,0:T(1,128)S(1)} %get-tuple-element.23), channel_id=1, source_target_pairs={{0,32},{4,36},{8,40},{12,44},{16,48},{20,52},{24,56},{28,60},{32,0... | collective-permute-start | bytes 4616 | tf_op jit(solution)/shard_map/ppermute | solution.py:405
  56.0 0.0 collective-permute-done
  56.0 0.0 collective-permute-done.2
  56.0 2.4 %collective-permute-done.1 = f32[1,384]{1,0:T(1,128)S(1)} collective-permute-done((f32[1,384]{1,0:T(1,128)S(1)}, f32[1,384]{1,0:T(1,128)S(1)}, u32[]{:S(2)}, u32[]{:S(2)}) %collective-permute-start.1) | collective-permute-done | bytes 1568 | tf_op jit(solution)/shard_map/ppermute | solution.py:405
  58.4 0.6 all-to-all-done.2.pieces_ref
  59.1 2.8 %collective-permute-start.5 = (bf16[264,128]{1,0:T(8,128)(2,1)S(1)}, bf16[264,128]{1,0:T(8,128)(2,1)S(1)}, u32[]{:S(2)}, u32[]{:S(2)}) collective-permute-start(bf16[264,128]{1,0:T(8,128)(2,1)S(1)} %get-tuple-element.20), channel_id=1, source_target_pairs={{0,3},{1,0},{2,1},{3,2},{4,7},{5,4},{6,5},{7,6},{8,11},{9,8},{10,9... | collective-permute-start | bytes 202760 | tf_op jit(solution)/shard_map/ppermute | solution.py:415
  61.9 0.3 collective-permute-start.4
  62.2 0.7 collective-permute-start.3
  62.9 3.7 %shard_map.64 = (f32[1,4096]{1,0:T(1,128)}, bf16[256,4096]{1,0:T(8,128)(2,1)}) custom-call(bf16[256,4096]{1,0:T(8,128)(2,1)} %bitcast.12), custom_call_target="tpu_custom_call" | custom-call | tf_op jit(solution)/shard_map/pallas_call | solution.py:325
  66.6 0.0 collective-permute-done.5.refs_2_
  66.6 0.0 collective-permute-done.4.refs_1_
  66.6 1.8 %collective-permute-done.3.refs_0_ = bf16[264,128]{1,0:T(8,128)(2,1)S(1)} collective-permute-done((bf16[264,128]{1,0:T(8,128)(2,1)S(1)}, bf16[264,128]{1,0:T(8,128)(2,1)S(1)}, u32[]{:S(2)}, u32[]{:S(2)}) %collective-permute-start.3) | collective-permute-done | bytes 67616 | tf_op jit(solution)/shard_map/ppermute | solution.py:415
  68.4 1.6 %copy-done = bf16[256,4096]{1,0:T(8,128)(2,1)S(1)} copy-done((bf16[256,4096]{1,0:T(8,128)(2,1)S(1)}, bf16[256,4096]{1,0:T(8,128)(2,1)}, u32[]{:S(2)}) %copy-start) | copy-done | bytes 2097176
  69.9 0.7 copy-done.2
  70.7 3.8 %shard_map.71 = bf16[256,4096]{1,0:T(8,128)(2,1)} custom-call(s32[1]{0:T(128)} %bitcast.level_ref, f32[1,4096]{1,0:T(1,128)S(1)} %copy-done.2, bf16[256,4096]{1,0:T(8,128)(2,1)S(1)} %copy-done, f32[264,128]{1,0:T(8,128)S(1)} %get-tuple-element.19.own_ref, bf16[264,128]{1,0:T(8,128)(2,1)S(1)} %collective-permute-done.3.refs_0_, ...), custom_call_target="tpu_custom_call" | custom-call | tf_op jit(solution)/shard_map/pallas_call | solution.py:325
  (10 shorter events, 0.1 us)
Async XLA Ops:
  0.0 10.1 %copy-start.4 = (bf16[1,1024]{1,0:T(2,128)(2,1)S(1)}, bf16[1,1024]{1,0:T(2,128)(2,1)}, u32[]{:S(2)}) copy-start(bf16[1,1024]{1,0:T(2,128)(2,1)} %precision_ref.1) | copy-start | bytes 6148
  0.0 10.1 %copy-start.3 = (s32[1,1024,1]{1,2,0:T(1,128)S(1)}, s32[1,1024,1]{1,2,0:T(1,128)}, u32[]{:S(2)}) copy-start(s32[1,1024,1]{1,2,0:T(1,128)} %param.10) | copy-start | bytes 12292
  0.0 10.2 %copy-start.1 = (bf16[1,1024,256]{2,1,0:T(8,128)(2,1)S(1)}, bf16[1,1024,256]{2,1,0:T(8,128)(2,1)}, u32[]{:S(2)}) copy-start(bf16[1,1024,256]{2,1,0:T(8,128)(2,1)} %param.7) | copy-start | bytes 1572868
  0.0 10.2 %copy-start.5 = (s32[64,3]{0,1:T(4,128)S(1)}, s32[64,3]{0,1:T(4,128)}, u32[]{:S(2)}) copy-start(s32[64,3]{0,1:T(4,128)} %param.11) | copy-start | bytes 2308
  0.0 10.2 %copy-start.6 = (bf16[1,1024]{1,0:T(2,128)(2,1)S(1)}, bf16[1,1024]{1,0:T(2,128)(2,1)}, u32[]{:S(2)}) copy-start(bf16[1,1024]{1,0:T(2,128)(2,1)} %innovation_ref.1) | copy-start | bytes 6148
  3.0 20.5 %all-to-all-start = ((bf16[16,96,256]{2,1,0:T(8,128)(2,1)}), bf16[16,96,256]{2,1,0:T(8,128)(2,1)S(1)}, u32[]{:S(2)}, u32[]{:S(2)}) async-start(bf16[16,96,256]{2,1,0:T(8,128)(2,1)} %shard_map.65), calls=%async_computation | async-start | bytes 1572864 | tf_op jit(solution)/shard_map/all_to_all | solution.py:367
  24.7 12.0 %all-to-all-start.1 = ((bf16[16,80,128]{2,1,0:T(8,128)(2,1)}), bf16[16,80,128]{2,1,0:T(8,128)(2,1)S(1)}, u32[]{:S(2)}, u32[]{:S(2)}) async-start(bf16[16,80,128]{2,1,0:T(8,128)(2,1)} %shard_map.67), calls=%async_computation.1 | async-start | bytes 655360 | tf_op jit(solution)/shard_map/all_to_all | solution.py:387
  37.8 21.2 %all-to-all-start.2 = ((bf16[64,16,128]{2,1,0:T(8,128)(2,1)}), bf16[64,16,128]{2,1,0:T(8,128)(2,1)S(1)}, u32[]{:S(2)}, u32[]{:S(2)}) async-start(bf16[64,16,128]{2,1,0:T(8,128)(2,1)} %get-tuple-element.17), calls=%async_computation.2 | async-start | bytes 524288 | tf_op jit(solution)/shard_map/all_to_all | solution.py:395
  47.1 8.9 %collective-permute-start = (f32[1,384]{1,0:T(1,128)S(1)}, f32[1,384]{1,0:T(1,128)S(1)}, u32[]{:S(2)}, u32[]{:S(2)}) collective-permute-start(f32[1,384]{1,0:T(1,128)S(1)} %get-tuple-element.21), channel_id=1, source_target_pairs={{0,16},{4,20},{8,24},{12,28},{16,32},{20,36},{24,40},{28,44},{32,4... | collective-permute-start | bytes 4616 | tf_op jit(solution)/shard_map/ppermute | solution.py:405
  49.5 6.6 %collective-permute-start.2 = (f32[1,384]{1,0:T(1,128)S(1)}, f32[1,384]{1,0:T(1,128)S(1)}, u32[]{:S(2)}, u32[]{:S(2)}) collective-permute-start(f32[1,384]{1,0:T(1,128)S(1)} %get-tuple-element.22), channel_id=1, source_target_pairs={{0,48},{4,52},{8,56},{12,60},{16,0},{20,4},{24,8},{28,12},{32,16},... | collective-permute-start | bytes 4616 | tf_op jit(solution)/shard_map/ppermute | solution.py:405
  50.8 7.7 %collective-permute-start.1 = (f32[1,384]{1,0:T(1,128)S(1)}, f32[1,384]{1,0:T(1,128)S(1)}, u32[]{:S(2)}, u32[]{:S(2)}) collective-permute-start(f32[1,384]{1,0:T(1,128)S(1)} %get-tuple-element.23), channel_id=1, source_target_pairs={{0,32},{4,36},{8,40},{12,44},{16,48},{20,52},{24,56},{28,60},{32,0... | collective-permute-start | bytes 4616 | tf_op jit(solution)/shard_map/ppermute | solution.py:405
  59.1 7.5 %collective-permute-start.5 = (bf16[264,128]{1,0:T(8,128)(2,1)S(1)}, bf16[264,128]{1,0:T(8,128)(2,1)S(1)}, u32[]{:S(2)}, u32[]{:S(2)}) collective-permute-start(bf16[264,128]{1,0:T(8,128)(2,1)S(1)} %get-tuple-element.20), channel_id=1, source_target_pairs={{0,3},{1,0},{2,1},{3,2},{4,7},{5,4},{6,5},{7,6},{8,11},{9,8},{10,9... | collective-permute-start | bytes 202760 | tf_op jit(solution)/shard_map/ppermute | solution.py:415
  61.9 4.7 %collective-permute-start.4 = (bf16[264,128]{1,0:T(8,128)(2,1)S(1)}, bf16[264,128]{1,0:T(8,128)(2,1)S(1)}, u32[]{:S(2)}, u32[]{:S(2)}) collective-permute-start(bf16[264,128]{1,0:T(8,128)(2,1)S(1)} %get-tuple-element.20), channel_id=1, source_target_pairs={{0,2},{1,3},{2,0},{3,1},{4,6},{5,7},{6,4},{7,5},{8,10},{9,11},{10,... | collective-permute-start | bytes 202760 | tf_op jit(solution)/shard_map/ppermute | solution.py:415
  62.2 6.1 %collective-permute-start.3 = (bf16[264,128]{1,0:T(8,128)(2,1)S(1)}, bf16[264,128]{1,0:T(8,128)(2,1)S(1)}, u32[]{:S(2)}, u32[]{:S(2)}) collective-permute-start(bf16[264,128]{1,0:T(8,128)(2,1)S(1)} %get-tuple-element.20), channel_id=1, source_target_pairs={{0,1},{1,2},{2,3},{3,0},{4,5},{5,6},{6,7},{7,4},{8,9},{9,10},{10,1... | collective-permute-start | bytes 202760 | tf_op jit(solution)/shard_map/ppermute | solution.py:415
  68.4 1.6 %copy-start = (bf16[256,4096]{1,0:T(8,128)(2,1)S(1)}, bf16[256,4096]{1,0:T(8,128)(2,1)}, u32[]{:S(2)}) copy-start(bf16[256,4096]{1,0:T(8,128)(2,1)} %get-tuple-element.14.anomaly_ref) | copy-start | bytes 6291460
  69.9 0.7 copy-start.2

commit v9 on v8

--- a/solution.py
+++ b/solution.py
@@ -17,7 +17,7 @@
 PAIR = 2
 GROUPS = PLANES // PAIR
 WIDTH = 512
-EXTRA = 16
+EXTRA = 8
 VMEM_LIMIT = 16 << 20
 FIRST_LIMIT = 62 << 20
 BF16 = jnp.bfloat16
@@ -145,7 +145,7 @@
 def sums_kernel(owner_ref, precision_ref, innovation_ref, obs_ref, listed_ref, sums_ref):
     count = owner_ref.shape[1]
     regions = listed_ref.shape[1]
-    places, lines, _ = sums_ref.shape
+    groups, lines, _ = sums_ref.shape
     obs = obs_ref[...]
     precision = precision_ref[...].astype(F32)
     factor = precision * innovation_ref[...].astype(F32)
@@ -154,16 +154,16 @@
     half = obs[:, LANES:].astype(F32)
     squares = dot(jnp.where(hit, precision, 0.0).astype(BF16), (half * half).astype(BF16))
     weight = split(weights_transposed(listed_ref[...]))
-    row = iota((regions, places * lines), 1)
-    item = row % lines
-    pick = iota((regions, places * lines), 0) == region_at(row // lines, item // 3)
-    pick = onehot(pick & (item < 3 * GROUPS))
+    row = iota((regions, groups * lines), 1)
+    item = row % EXTRA
+    region = region_at(row % lines // EXTRA, row // lines)
+    pick = onehot((iota((regions, groups * lines), 0) == region) & (item < 3))
     chosen = split(dot(weight[0], pick) + dot(weight[1], pick))
     over = ((0,), (0,))
     parts = [dot3(chosen, split(value), over) for value in (sums[:, :LANES], sums[:, LANES:], squares)]
-    kind = iota((places * lines, LANES), 0) % lines % 3
+    kind = iota((groups * lines, LANES), 0) % EXTRA
     mixed = jnp.where(kind == 0, parts[0], jnp.where(kind == 1, parts[1], parts[2]))
-    sums_ref[...] = mixed.astype(BF16).reshape(places, lines, LANES)
+    sums_ref[...] = mixed.astype(BF16).reshape(groups, lines, LANES)
 
 
 def weight_kernel(listed_ref, high_ref, low_ref):
@@ -182,7 +182,7 @@
     low_ref[...] = low
 
 
-def covariance_kernel(capacity, rows_ref, sums_ref, message_ref):
+def covariance_kernel(capacity, rows_ref, sums_ref, message_out, message_ref, semaphores):
     half = LANES
     members = rows_ref.shape[2]
     places = message_ref.shape[0]
@@ -194,7 +194,20 @@
         corner = jnp.where(above, total[:half, :half], total[half:, half:])
         packed = jnp.concatenate([corner, total[:half, half:]], axis=0).astype(BF16)
         message_ref[:, group * piece : (group + 1) * piece, :] = packed.reshape(places, piece, LANES)
-    message_ref[:, GROUPS * piece :, :] = sums_ref[...]
+        if group == GROUPS // 2 - 1:
+            part = slice(0, (group + 1) * piece)
+            first = pltpu.make_async_copy(
+                message_ref.at[:, part], message_out.at[:, part], semaphores.at[0]
+            )
+            first.start()
+    message_ref[:, GROUPS * piece :, :] = sums_ref[...].reshape(places, EXTRA, LANES)
+    part = slice(GROUPS // 2 * piece, GROUPS * piece + EXTRA)
+    second = pltpu.make_async_copy(
+        message_ref.at[:, part], message_out.at[:, part], semaphores.at[1]
+    )
+    second.start()
+    first.wait()
+    second.wait()
 
 
 def mix_kernel(message_ref, high_ref, low_ref, mixed_ref, sums_ref):
@@ -202,9 +215,7 @@
     span = GROUPS * piece
     message = message_ref[:, :span, :].reshape(regions, piece, LANES)
     sums = jnp.sum(message_ref[:, span:, :].astype(F32), axis=0)
-    for group in range(GROUPS):
-        row = [sums[3 * group + part : 3 * group + part + 1] for part in range(3)]
-        sums_ref[group : group + 1, :] = jnp.concatenate(row, axis=1)
+    sums_ref[...] = jnp.concatenate([sums[part : part + 1] for part in range(3)], axis=1)
     parts = [
         message[:, at : at + SUBLANES, :].reshape(regions * SUBLANES, LANES) for at in range(0, piece, SUBLANES)
     ]
@@ -371,39 +382,42 @@
     )
     sums = call(
         sums_kernel,
-        shape((places, EXTRA, LANES), BF16),
+        shape((GROUPS, places * EXTRA, LANES), BF16),
         owners,
         obs_precision,
         innovation,
         obs_anomaly[0],
         listed,
     )
-    message = call(
-        functools.partial(covariance_kernel, capacity),
-        shape((places, GROUPS * piece + EXTRA, LANES), BF16),
-        routed,
-        sums,
-    )
-    message = lax.all_to_all(message, "region", 0, 0, tiled=True, axis_index_groups=near)
-    mixed, parts = call(
-        mix_kernel,
-        (shape((regions, piece, LANES), BF16), shape((GROUPS, members + LANES), F32)),
-        message,
-        high,
-        low,
-    )
-    pieces = lax.all_to_all(mixed, "region", 0, 0, tiled=True)
-
     my_group = my_region // CORES % PLANES // PAIR
-    part = lax.dynamic_slice_in_dim(parts, my_group, 1, 0)
+    total = lax.dynamic_index_in_dim(sums, my_group, 0, keepdims=False).astype(F32)
     for ahead in range(1, GROUPS):
-        sent = lax.dynamic_slice_in_dim(parts, (my_group + ahead) % GROUPS, 1, 0)
+        sent = lax.dynamic_index_in_dim(sums, (my_group + ahead) % GROUPS, 0, keepdims=False)
         pairs = []
         for region in range(regions):
             x, z, core = region_parts(region)
             pairs.append((region, (x * PLANES + (z + PAIR * ahead) % PLANES) * CORES + core))
         arrived_part = lax.ppermute(sent, "region", pairs)
-        part = part + arrived_part
+        total = total + arrived_part.astype(F32)
+    total = total.astype(BF16)
+    block = (places, GROUPS * piece + EXTRA, LANES)
+    message = call(
+        functools.partial(covariance_kernel, capacity),
+        shape(block, BF16),
+        routed,
+        total,
+        space=pltpu.HBM,
+        scratch=[pltpu.VMEM(block, BF16), pltpu.SemaphoreType.DMA((2,))],
+    )
+    message = lax.all_to_all(message, "region", 0, 0, tiled=True, axis_index_groups=near)
+    mixed, part = call(
+        mix_kernel,
+        (shape((regions, piece, LANES), BF16), shape((1, members + LANES), F32)),
+        message,
+        high,
+        low,
+    )
+    pieces = lax.all_to_all(mixed, "region", 0, 0, tiled=True)
 
     height = members + SUBLANES
     own, sent = call(

time: 75 us -> 76.6 us (1.021)
  blocking collectives: 0 us -> 17.1 us
  waiting for transfers between devices: 25.1 us -> 17 us
  starting transfers between devices: 32.6 us -> 26 us
    all_to_all x0 -> x1, blocking collectives: none -> 17.1 us  [step(): pieces = lax.all_to_all(mixed, 'region', 0, 0, tiled=True)]
    all_to_all x1, waiting for transfers between devices: 12.7 us -> 0.01 us  [step(): lax.all_to_all(rows, 'region', 0, 0, tiled=True, axis_index_groups=near)]
    all_to_all x1 -> x0, starting transfers between devices: 9.21 us -> none  [step(): pieces = lax.all_to_all(mixed, 'region', 0, 0, tiled=True)]
    ppermute x3, waiting for transfers between devices: 2.39 us -> 7.84 us  [step(): arrived_part = lax.ppermute(sent, 'region', pairs)]
    all_to_all x1, starting transfers between devices: 3.5 us -> 5.28 us  [step(): lax.all_to_all(message, 'region', 0, 0, tiled=True, axis_index_groups=near)]
  transfers between devices with their start and end apart: 9 -> 8, of which waited for: 5 -> 4; matrix products, arithmetic and copies ran while one was open for 0% -> 0% of each run, Pallas kernels for 7% -> 7%
where the time goes in v9:
time: 76.6 us; the launch traced here: 76.1 us
  starting transfers between devices  26 us (34%)
  blocking collectives  17.1 us (22%)
  waiting for transfers between devices  17 us (22%)
  Pallas kernels  13.6 us (18%)
  local copies, waits for them, and re-layouts  2.34 us (3%)
    all_to_all x1, blocking collectives, step(): pieces = lax.all_to_all(mixed, 'region', 0, 0, tiled=True)  17.1 us
    pallas_call x8, Pallas kernels, call(): pl.pallas_call(kernel, out_shape=shapes, in_specs=[pl.BlockSpec(memory_sp...  13.6 us
    ppermute x3, starting transfers between devices, step(): arrived_part = lax.ppermute(sent, 'region', pairs)  9.67 us
    ppermute x3, waiting for transfers between devices, step(): arrived_part = lax.ppermute(sent, 'region', pairs)  7.84 us
    all_to_all x1, waiting for transfers between devices, step(): lax.all_to_all(message, 'region', 0, 0, tiled=True, axis_index_groups=near)  7.37 us
    all_to_all x1, starting transfers between devices, step(): lax.all_to_all(rows, 'region', 0, 0, tiled=True, axis_index_groups=near)  7.17 us
    all_to_all x1, starting transfers between devices, step(): lax.all_to_all(message, 'region', 0, 0, tiled=True, axis_index_groups=near)  5.28 us
    ppermute x3, starting transfers between devices, step(): arrived.append(lax.ppermute(sent, 'level', pairs))  3.85 us
  transfers between devices with their start and end apart: 8, of which 4 were waited for; matrix products, arithmetic and copies ran while one was open for 0% of the time, Pallas kernels for 7%

profile of v9, /device:TPU:1, one launch (start us, length us, event | category | flops | bytes accessed | tf_op | source)
XLA Modules:
  0.0 76.1 jit_solution(9901096761329230364)
XLA Ops:
  0.0 0.0 copy-start.5
  0.0 0.0 copy-start.6
  0.0 2.9 %shard_map.65 = bf16[16,96,256]{2,1,0:T(8,128)(2,1)} custom-call(s32[1,1024]{1,0:T(1,128)} %bitcast.17, bf16[1,1024]{1,0:T(2,128)(2,1)} %precision_ref.1, bf16[1024,256]{1,0:T(8,128)(2,1)} %bitcast.15), custom_call_target="tpu_custom_call" | custom-call | tf_op jit(solution)/shard_map/pallas_call | solution.py:336
  3.0 7.2 %all-to-all-start = ((bf16[16,96,256]{2,1,0:T(8,128)(2,1)}), bf16[16,96,256]{2,1,0:T(8,128)(2,1)S(1)}, u32[]{:S(2)}, u32[]{:S(2)}) async-start(bf16[16,96,256]{2,1,0:T(8,128)(2,1)} %shard_map.65), calls=%async_computation | async-start | bytes 1572864 | tf_op jit(solution)/shard_map/all_to_all | solution.py:378
  10.1 0.0 copy-done.3
  10.2 0.0 copy-done.1
  10.2 0.0 copy-done.5
  10.2 0.0 copy-done.6
  10.2 0.9 %shard_map.66 = bf16[4,128,128]{2,1,0:T(8,128)(2,1)S(1)} custom-call(s32[1,1024]{1,0:T(1,128)S(1)} %bitcast.18, bf16[1,1024]{1,0:T(2,128)(2,1)S(1)} %copy-done.4, bf16[1,1024]{1,0:T(2,128)(2,1)S(1)} %copy-done.6, bf16[1024,256]{1,0:T(8,128)(2,1)S(1)} %bitcast.16, s32[3,64]{1,0:T(4,128)S(1)} %bitcast.19), custom_call_target="tpu_custom_call" | custom-call | tf_op jit(solution)/shard_map/pallas_call | solution.py:336
  11.1 3.1 %collective-permute-start = (bf16[128,128]{1,0:T(8,128)(2,1)S(1)}, bf16[128,128]{1,0:T(8,128)(2,1)S(1)}, u32[]{:S(2)}, u32[]{:S(2)}) collective-permute-start(bf16[128,128]{1,0:T(8,128)(2,1)S(1)} %get-tuple-element.21), channel_id=1, source_target_pairs={{0,16},{4,20},{8,24},{12,28},{16,32},{20,36},{24,40},{28,44},{32,4... | collective-permute-start | bytes 98312 | tf_op jit(solution)/shard_map/ppermute | solution.py:400
  14.1 2.2 %collective-permute-start.2 = (bf16[128,128]{1,0:T(8,128)(2,1)S(1)}, bf16[128,128]{1,0:T(8,128)(2,1)S(1)}, u32[]{:S(2)}, u32[]{:S(2)}) collective-permute-start(bf16[128,128]{1,0:T(8,128)(2,1)S(1)} %get-tuple-element.22), channel_id=1, source_target_pairs={{0,48},{4,52},{8,56},{12,60},{16,0},{20,4},{24,8},{28,12},{32,16},... | collective-permute-start | bytes 98312 | tf_op jit(solution)/shard_map/ppermute | solution.py:400
  16.4 4.4 %collective-permute-start.1 = (bf16[128,128]{1,0:T(8,128)(2,1)S(1)}, bf16[128,128]{1,0:T(8,128)(2,1)S(1)}, u32[]{:S(2)}, u32[]{:S(2)}) collective-permute-start(bf16[128,128]{1,0:T(8,128)(2,1)S(1)} %get-tuple-element.23), channel_id=1, source_target_pairs={{0,32},{4,36},{8,40},{12,44},{16,48},{20,52},{24,56},{28,60},{32,0... | collective-permute-start | bytes 98312 | tf_op jit(solution)/shard_map/ppermute | solution.py:400
  20.7 5.6 %collective-permute-done = bf16[128,128]{1,0:T(8,128)(2,1)S(1)} collective-permute-done((bf16[128,128]{1,0:T(8,128)(2,1)S(1)}, bf16[128,128]{1,0:T(8,128)(2,1)S(1)}, u32[]{:S(2)}, u32[]{:S(2)}) %collective-permute-start) | collective-permute-done | bytes 32800 | tf_op jit(solution)/shard_map/ppermute | solution.py:400
  26.4 0.0 collective-permute-done.2
  26.4 2.2 %collective-permute-done.1 = bf16[128,128]{1,0:T(8,128)(2,1)S(1)} collective-permute-done((bf16[128,128]{1,0:T(8,128)(2,1)S(1)}, bf16[128,128]{1,0:T(8,128)(2,1)S(1)}, u32[]{:S(2)}, u32[]{:S(2)}) %collective-permute-start.1) | collective-permute-done | bytes 32800 | tf_op jit(solution)/shard_map/ppermute | solution.py:400
  28.6 0.0 all-to-all-done.rows_ref
  28.6 1.2 %shard_map.67 = bf16[16,72,128]{2,1,0:T(8,128)(2,1)} custom-call(bf16[16,96,256]{2,1,0:T(8,128)(2,1)S(1)} %all-to-all-done.rows_ref, bf16[128,128]{1,0:T(8,128)(2,1)S(1)} %fusion.2.sums_ref), custom_call_target="tpu_custom_call" | custom-call | tf_op jit(solution)/shard_map/pallas_call | solution.py:336
  29.8 5.3 %all-to-all-start.1 = ((bf16[16,72,128]{2,1,0:T(8,128)(2,1)}), bf16[16,72,128]{2,1,0:T(8,128)(2,1)S(1)}, u32[]{:S(2)}, u32[]{:S(2)}) async-start(bf16[16,72,128]{2,1,0:T(8,128)(2,1)} %shard_map.67), calls=%async_computation.1 | async-start | bytes 589824 | tf_op jit(solution)/shard_map/all_to_all | solution.py:412
  35.1 0.7 shard_map.68
  35.8 7.4 %all-to-all-done.1.message_ref = bf16[16,72,128]{2,1,0:T(8,128)(2,1)S(1)} async-done(((bf16[16,72,128]{2,1,0:T(8,128)(2,1)}), bf16[16,72,128]{2,1,0:T(8,128)(2,1)S(1)}, u32[]{:S(2)}, u32[]{:S(2)}) %all-to-all-start.1) | async-done | bytes 294944 | tf_op jit(solution)/shard_map/all_to_all | solution.py:412
  43.2 0.4 shard_map.69
  43.6 17.1 %all_to_all.15.pieces_ref = bf16[64,16,128]{2,1,0:T(8,128)(2,1)S(1)} all-to-all(bf16[64,16,128]{2,1,0:T(8,128)(2,1)S(1)} %get-tuple-element.17), channel_id=1, replica_groups=mesh['region'=64,'level'=4] {'region'}, dimensions={0} | all-to-all | bytes 524288 | tf_op jit(solution)/shard_map/all_to_all | solution.py:420
  60.7 2.8 %collective-permute-start.5 = (bf16[264,128]{1,0:T(8,128)(2,1)S(1)}, bf16[264,128]{1,0:T(8,128)(2,1)S(1)}, u32[]{:S(2)}, u32[]{:S(2)}) collective-permute-start(bf16[264,128]{1,0:T(8,128)(2,1)S(1)} %get-tuple-element.20), channel_id=1, source_target_pairs={{0,3},{1,0},{2,1},{3,2},{4,7},{5,4},{6,5},{7,6},{8,11},{9,8},{10,9... | collective-permute-start | bytes 202760 | tf_op jit(solution)/shard_map/ppermute | solution.py:429
  63.5 0.3 collective-permute-start.4
  63.9 0.7 collective-permute-start.3
  64.6 3.7 %shard_map.64 = (f32[1,4096]{1,0:T(1,128)}, bf16[256,4096]{1,0:T(8,128)(2,1)}) custom-call(bf16[256,4096]{1,0:T(8,128)(2,1)} %bitcast.21), custom_call_target="tpu_custom_call" | custom-call | tf_op jit(solution)/shard_map/pallas_call | solution.py:336
  68.2 0.0 collective-permute-done.5.refs_2_
  68.2 0.0 collective-permute-done.4.refs_1_
  68.2 1.8 %collective-permute-done.3.refs_0_ = bf16[264,128]{1,0:T(8,128)(2,1)S(1)} collective-permute-done((bf16[264,128]{1,0:T(8,128)(2,1)S(1)}, bf16[264,128]{1,0:T(8,128)(2,1)S(1)}, u32[]{:S(2)}, u32[]{:S(2)}) %collective-permute-start.3) | collective-permute-done | bytes 67616 | tf_op jit(solution)/shard_map/ppermute | solution.py:429
  70.0 1.6 %copy-done = bf16[256,4096]{1,0:T(8,128)(2,1)S(1)} copy-done((bf16[256,4096]{1,0:T(8,128)(2,1)S(1)}, bf16[256,4096]{1,0:T(8,128)(2,1)}, u32[]{:S(2)}) %copy-start) | copy-done | bytes 2097176
  71.6 0.7 copy-done.2
  72.3 3.8 %shard_map.71 = bf16[256,4096]{1,0:T(8,128)(2,1)} custom-call(s32[1]{0:T(128)} %bitcast.level_ref, f32[1,4096]{1,0:T(1,128)S(1)} %copy-done.2, bf16[256,4096]{1,0:T(8,128)(2,1)S(1)} %copy-done, f32[264,128]{1,0:T(8,128)S(1)} %get-tuple-element.19.own_ref, bf16[264,128]{1,0:T(8,128)(2,1)S(1)} %collective-permute-done.3.refs_0_, ...), custom_call_target="tpu_custom_call" | custom-call | tf_op jit(solution)/shard_map/pallas_call | solution.py:336
  (9 shorter events, 0.1 us)
Async XLA Ops:
  0.0 10.1 %copy-start.4 = (bf16[1,1024]{1,0:T(2,128)(2,1)S(1)}, bf16[1,1024]{1,0:T(2,128)(2,1)}, u32[]{:S(2)}) copy-start(bf16[1,1024]{1,0:T(2,128)(2,1)} %precision_ref.1) | copy-start | bytes 6148
  0.0 10.1 %copy-start.3 = (s32[1,1024,1]{1,2,0:T(1,128)S(1)}, s32[1,1024,1]{1,2,0:T(1,128)}, u32[]{:S(2)}) copy-start(s32[1,1024,1]{1,2,0:T(1,128)} %param.10) | copy-start | bytes 12292
  0.0 10.2 %copy-start.1 = (bf16[1,1024,256]{2,1,0:T(8,128)(2,1)S(1)}, bf16[1,1024,256]{2,1,0:T(8,128)(2,1)}, u32[]{:S(2)}) copy-start(bf16[1,1024,256]{2,1,0:T(8,128)(2,1)} %param.7) | copy-start | bytes 1572868
  0.0 10.2 %copy-start.5 = (s32[64,3]{0,1:T(4,128)S(1)}, s32[64,3]{0,1:T(4,128)}, u32[]{:S(2)}) copy-start(s32[64,3]{0,1:T(4,128)} %param.11) | copy-start | bytes 2308
  0.0 10.2 %copy-start.6 = (bf16[1,1024]{1,0:T(2,128)(2,1)S(1)}, bf16[1,1024]{1,0:T(2,128)(2,1)}, u32[]{:S(2)}) copy-start(bf16[1,1024]{1,0:T(2,128)(2,1)} %innovation_ref.1) | copy-start | bytes 6148
  3.0 25.7 %all-to-all-start = ((bf16[16,96,256]{2,1,0:T(8,128)(2,1)}), bf16[16,96,256]{2,1,0:T(8,128)(2,1)S(1)}, u32[]{:S(2)}, u32[]{:S(2)}) async-start(bf16[16,96,256]{2,1,0:T(8,128)(2,1)} %shard_map.65), calls=%async_computation | async-start | bytes 1572864 | tf_op jit(solution)/shard_map/all_to_all | solution.py:378
  11.1 15.3 %collective-permute-start = (bf16[128,128]{1,0:T(8,128)(2,1)S(1)}, bf16[128,128]{1,0:T(8,128)(2,1)S(1)}, u32[]{:S(2)}, u32[]{:S(2)}) collective-permute-start(bf16[128,128]{1,0:T(8,128)(2,1)S(1)} %get-tuple-element.21), channel_id=1, source_target_pairs={{0,16},{4,20},{8,24},{12,28},{16,32},{20,36},{24,40},{28,44},{32,4... | collective-permute-start | bytes 98312 | tf_op jit(solution)/shard_map/ppermute | solution.py:400
  14.1 12.2 %collective-permute-start.2 = (bf16[128,128]{1,0:T(8,128)(2,1)S(1)}, bf16[128,128]{1,0:T(8,128)(2,1)S(1)}, u32[]{:S(2)}, u32[]{:S(2)}) collective-permute-start(bf16[128,128]{1,0:T(8,128)(2,1)S(1)} %get-tuple-element.22), channel_id=1, source_target_pairs={{0,48},{4,52},{8,56},{12,60},{16,0},{20,4},{24,8},{28,12},{32,16},... | collective-permute-start | bytes 98312 | tf_op jit(solution)/shard_map/ppermute | solution.py:400
  16.4 12.2 %collective-permute-start.1 = (bf16[128,128]{1,0:T(8,128)(2,1)S(1)}, bf16[128,128]{1,0:T(8,128)(2,1)S(1)}, u32[]{:S(2)}, u32[]{:S(2)}) collective-permute-start(bf16[128,128]{1,0:T(8,128)(2,1)S(1)} %get-tuple-element.23), channel_id=1, source_target_pairs={{0,32},{4,36},{8,40},{12,44},{16,48},{20,52},{24,56},{28,60},{32,0... | collective-permute-start | bytes 98312 | tf_op jit(solution)/shard_map/ppermute | solution.py:400
  29.8 13.4 %all-to-all-start.1 = ((bf16[16,72,128]{2,1,0:T(8,128)(2,1)}), bf16[16,72,128]{2,1,0:T(8,128)(2,1)S(1)}, u32[]{:S(2)}, u32[]{:S(2)}) async-start(bf16[16,72,128]{2,1,0:T(8,128)(2,1)} %shard_map.67), calls=%async_computation.1 | async-start | bytes 589824 | tf_op jit(solution)/shard_map/all_to_all | solution.py:412
  60.7 7.5 %collective-permute-start.5 = (bf16[264,128]{1,0:T(8,128)(2,1)S(1)}, bf16[264,128]{1,0:T(8,128)(2,1)S(1)}, u32[]{:S(2)}, u32[]{:S(2)}) collective-permute-start(bf16[264,128]{1,0:T(8,128)(2,1)S(1)} %get-tuple-element.20), channel_id=1, source_target_pairs={{0,3},{1,0},{2,1},{3,2},{4,7},{5,4},{6,5},{7,6},{8,11},{9,8},{10,9... | collective-permute-start | bytes 202760 | tf_op jit(solution)/shard_map/ppermute | solution.py:429
  63.5 4.7 %collective-permute-start.4 = (bf16[264,128]{1,0:T(8,128)(2,1)S(1)}, bf16[264,128]{1,0:T(8,128)(2,1)S(1)}, u32[]{:S(2)}, u32[]{:S(2)}) collective-permute-start(bf16[264,128]{1,0:T(8,128)(2,1)S(1)} %get-tuple-element.20), channel_id=1, source_target_pairs={{0,2},{1,3},{2,0},{3,1},{4,6},{5,7},{6,4},{7,5},{8,10},{9,11},{10,... | collective-permute-start | bytes 202760 | tf_op jit(solution)/shard_map/ppermute | solution.py:429
  63.9 6.1 %collective-permute-start.3 = (bf16[264,128]{1,0:T(8,128)(2,1)S(1)}, bf16[264,128]{1,0:T(8,128)(2,1)S(1)}, u32[]{:S(2)}, u32[]{:S(2)}) collective-permute-start(bf16[264,128]{1,0:T(8,128)(2,1)S(1)} %get-tuple-element.20), channel_id=1, source_target_pairs={{0,1},{1,2},{2,3},{3,0},{4,5},{5,6},{6,7},{7,4},{8,9},{9,10},{10,1... | collective-permute-start | bytes 202760 | tf_op jit(solution)/shard_map/ppermute | solution.py:429
  70.0 1.6 %copy-start = (bf16[256,4096]{1,0:T(8,128)(2,1)S(1)}, bf16[256,4096]{1,0:T(8,128)(2,1)}, u32[]{:S(2)}) copy-start(bf16[256,4096]{1,0:T(8,128)(2,1)} %get-tuple-element.14.anomaly_ref) | copy-start | bytes 6291460
  71.6 0.7 copy-start.2

commit v10 on v9

--- a/solution.py
+++ b/solution.py
@@ -17,6 +17,7 @@
 PAIR = 2
 GROUPS = PLANES // PAIR
 WIDTH = 512
+ROWS = 3
 EXTRA = 8
 VMEM_LIMIT = 16 << 20
 FIRST_LIMIT = 62 << 20
@@ -155,13 +156,12 @@
     squares = dot(jnp.where(hit, precision, 0.0).astype(BF16), (half * half).astype(BF16))
     weight = split(weights_transposed(listed_ref[...]))
     row = iota((regions, groups * lines), 1)
-    item = row % EXTRA
-    region = region_at(row % lines // EXTRA, row // lines)
-    pick = onehot((iota((regions, groups * lines), 0) == region) & (item < 3))
+    region = region_at(row % lines // ROWS, row // lines)
+    pick = onehot(iota((regions, groups * lines), 0) == region)
     chosen = split(dot(weight[0], pick) + dot(weight[1], pick))
     over = ((0,), (0,))
     parts = [dot3(chosen, split(value), over) for value in (sums[:, :LANES], sums[:, LANES:], squares)]
-    kind = iota((groups * lines, LANES), 0) % EXTRA
+    kind = iota((groups * lines, LANES), 0) % ROWS
     mixed = jnp.where(kind == 0, parts[0], jnp.where(kind == 1, parts[1], parts[2]))
     sums_ref[...] = mixed.astype(BF16).reshape(groups, lines, LANES)
 
@@ -200,7 +200,13 @@
                 message_ref.at[:, part], message_out.at[:, part], semaphores.at[0]
             )
             first.start()
-    message_ref[:, GROUPS * piece :, :] = sums_ref[...].reshape(places, EXTRA, LANES)
+    wide = (places * EXTRA, 2 * places * ROWS)
+    line = iota(wide, 0)
+    item = line % EXTRA
+    source = item // ROWS * (places * ROWS) + line // EXTRA * ROWS + item % ROWS
+    spread = (item < 2 * ROWS) & (source == iota(wide, 1))
+    sums = dot(onehot(spread), sums_ref[...]).astype(BF16)
+    message_ref[:, GROUPS * piece :, :] = sums.reshape(places, EXTRA, LANES)
     part = slice(GROUPS // 2 * piece, GROUPS * piece + EXTRA)
     second = pltpu.make_async_copy(
         message_ref.at[:, part], message_out.at[:, part], semaphores.at[1]
@@ -215,7 +221,9 @@
     span = GROUPS * piece
     message = message_ref[:, :span, :].reshape(regions, piece, LANES)
     sums = jnp.sum(message_ref[:, span:, :].astype(F32), axis=0)
-    sums_ref[...] = jnp.concatenate([sums[part : part + 1] for part in range(3)], axis=1)
+    for index in range(2):
+        row = [sums[at : at + 1] for at in range(index * ROWS, (index + 1) * ROWS)]
+        sums_ref[index : index + 1, :] = jnp.concatenate(row, axis=1)
     parts = [
         message[:, at : at + SUBLANES, :].reshape(regions * SUBLANES, LANES) for at in range(0, piece, SUBLANES)
     ]
@@ -382,7 +390,7 @@
     )
     sums = call(
         sums_kernel,
-        shape((GROUPS, places * EXTRA, LANES), BF16),
+        shape((GROUPS, places * ROWS, LANES), BF16),
         owners,
         obs_precision,
         innovation,
@@ -390,16 +398,21 @@
         listed,
     )
     my_group = my_region // CORES % PLANES // PAIR
-    total = lax.dynamic_index_in_dim(sums, my_group, 0, keepdims=False).astype(F32)
-    for ahead in range(1, GROUPS):
-        sent = lax.dynamic_index_in_dim(sums, (my_group + ahead) % GROUPS, 0, keepdims=False)
+
+    def group_pairs(ahead):
         pairs = []
         for region in range(regions):
             x, z, core = region_parts(region)
             pairs.append((region, (x * PLANES + (z + PAIR * ahead) % PLANES) * CORES + core))
-        arrived_part = lax.ppermute(sent, "region", pairs)
+        return pairs
+
+    total = lax.dynamic_index_in_dim(sums, my_group, 0, keepdims=False).astype(F32)
+    for ahead in (1, GROUPS - 1):
+        sent = lax.dynamic_index_in_dim(sums, (my_group + ahead) % GROUPS, 0, keepdims=False)
+        arrived_part = lax.ppermute(sent, "region", group_pairs(ahead))
         total = total + arrived_part.astype(F32)
-    total = total.astype(BF16)
+    far = lax.dynamic_index_in_dim(sums, (my_group + 2) % GROUPS, 0, keepdims=False)
+    total = jnp.concatenate([total.astype(BF16), far], axis=0)
     block = (places, GROUPS * piece + EXTRA, LANES)
     message = call(
         functools.partial(covariance_kernel, capacity),
@@ -412,13 +425,15 @@
     message = lax.all_to_all(message, "region", 0, 0, tiled=True, axis_index_groups=near)
     mixed, part = call(
         mix_kernel,
-        (shape((regions, piece, LANES), BF16), shape((1, members + LANES), F32)),
+        (shape((regions, piece, LANES), BF16), shape((2, members + LANES), F32)),
         message,
         high,
         low,
     )
     pieces = lax.all_to_all(mixed, "region", 0, 0, tiled=True)
 
+    arrived_part = lax.ppermute(part[1:2], "region", group_pairs(2))
+    part = part[0:1] + arrived_part
     height = members + SUBLANES
     own, sent = call(
         gather_kernel, (shape((height, LANES), F32), shape((height, LANES), BF16)), pieces, part

time: 76.6 us -> 75.1 us (0.980)
  blocking collectives: 17.1 us -> 0 us
  waiting for transfers between devices: 17 us -> 24.9 us
  starting transfers between devices: 26 us -> 33.2 us
    all_to_all x1 -> x0, blocking collectives: 17.1 us -> none  [step(): pieces = lax.all_to_all(mixed, 'region', 0, 0, tiled=True)]
    ppermute x3, waiting for transfers between devices: 7.84 us -> 15 us  [the longest x2 9.06 us: step(): arrived_part = lax.ppermute(sent, 'region', group_pairs(ahead))]
    all_to_all x0 -> x1, starting transfers between devices: none -> 6.19 us  [step(): pieces = lax.all_to_all(mixed, 'region', 0, 0, tiled=True)]
    ppermute x3, starting transfers between devices: 9.67 us -> 10.6 us  [the longest x1 5.35 us: step(): arrived_part = lax.ppermute(part[1:2], 'region', group_pairs(2))]
  transfers between devices with their start and end apart: 8 -> 9, of which waited for: 4 -> 5; matrix products, arithmetic and copies ran while one was open for 0% -> 0% of each run, Pallas kernels for 7% -> 7%
where the time goes in v10:
time: 75.1 us; the launch traced here: 74.7 us
  starting transfers between devices  33.2 us (44%)
  waiting for transfers between devices  24.9 us (33%)
  Pallas kernels  14.1 us (19%)
  local copies, waits for them, and re-layouts  2.35 us (3%)
    pallas_call x8, Pallas kernels, call(): pl.pallas_call(kernel, out_shape=shapes, in_specs=[pl.BlockSpec(memory_sp...  14.1 us
    ppermute x2, waiting for transfers between devices, step(): arrived_part = lax.ppermute(sent, 'region', group_pairs(ahead))  9.06 us
    all_to_all x1, waiting for transfers between devices, step(): lax.all_to_all(message, 'region', 0, 0, tiled=True, axis_index_groups=near)  7.36 us
    all_to_all x1, starting transfers between devices, step(): lax.all_to_all(rows, 'region', 0, 0, tiled=True, axis_index_groups=near)  7.17 us
    all_to_all x1, starting transfers between devices, step(): pieces = lax.all_to_all(mixed, 'region', 0, 0, tiled=True)  6.19 us
    ppermute x1, waiting for transfers between devices, step(): arrived_part = lax.ppermute(part[1:2], 'region', group_pairs(2))  5.97 us
    ppermute x1, starting transfers between devices, step(): arrived_part = lax.ppermute(part[1:2], 'region', group_pairs(2))  5.35 us
    all_to_all x1, starting transfers between devices, step(): lax.all_to_all(message, 'region', 0, 0, tiled=True, axis_index_groups=near)  5.32 us
  transfers between devices with their start and end apart: 9, of which 5 were waited for; matrix products, arithmetic and copies ran while one was open for 0% of the time, Pallas kernels for 7%

profile of v10, /device:TPU:1, one launch (start us, length us, event | category | flops | bytes accessed | tf_op | source)
XLA Modules:
  0.0 74.7 jit_solution(16022002866305430758)
XLA Ops:
  0.0 0.0 copy-start.5
  0.0 2.9 %shard_map.65 = bf16[16,96,256]{2,1,0:T(8,128)(2,1)} custom-call(s32[1,1024]{1,0:T(1,128)} %bitcast.17, bf16[1,1024]{1,0:T(2,128)(2,1)} %precision_ref.1, bf16[1024,256]{1,0:T(8,128)(2,1)} %bitcast.15), custom_call_target="tpu_custom_call" | custom-call | tf_op jit(solution)/shard_map/pallas_call | solution.py:344
  3.0 7.2 %all-to-all-start = ((bf16[16,96,256]{2,1,0:T(8,128)(2,1)}), bf16[16,96,256]{2,1,0:T(8,128)(2,1)S(1)}, u32[]{:S(2)}, u32[]{:S(2)}) async-start(bf16[16,96,256]{2,1,0:T(8,128)(2,1)} %shard_map.65), calls=%async_computation | async-start | bytes 1572864 | tf_op jit(solution)/shard_map/all_to_all | solution.py:386
  10.1 0.0 copy-done.3
  10.2 0.0 copy-done.1
  10.2 0.0 copy-done.5
  10.2 0.0 copy-done.6
  10.2 0.6 shard_map.66
  10.8 3.1 %collective-permute-start = (bf16[48,128]{1,0:T(8,128)(2,1)S(1)}, bf16[48,128]{1,0:T(8,128)(2,1)S(1)}, u32[]{:S(2)}, u32[]{:S(2)}) collective-permute-start(bf16[48,128]{1,0:T(8,128)(2,1)S(1)} %get-tuple-element.21), channel_id=1, source_target_pairs={{0,16},{4,20},{8,24},{12,28},{16,32},{20,36},{24,40},{28,44},{32,4... | collective-permute-start | bytes 36872 | tf_op jit(solution)/shard_map/ppermute | solution.py:412
  13.9 2.2 %collective-permute-start.1 = (bf16[48,128]{1,0:T(8,128)(2,1)S(1)}, bf16[48,128]{1,0:T(8,128)(2,1)S(1)}, u32[]{:S(2)}, u32[]{:S(2)}) collective-permute-start(bf16[48,128]{1,0:T(8,128)(2,1)S(1)} %get-tuple-element.23), channel_id=1, source_target_pairs={{0,48},{4,52},{8,56},{12,60},{16,0},{20,4},{24,8},{28,12},{32,16},... | collective-permute-start | bytes 36872 | tf_op jit(solution)/shard_map/ppermute | solution.py:412
  16.1 9.1 %collective-permute-done = bf16[48,128]{1,0:T(8,128)(2,1)S(1)} collective-permute-done((bf16[48,128]{1,0:T(8,128)(2,1)S(1)}, bf16[48,128]{1,0:T(8,128)(2,1)S(1)}, u32[]{:S(2)}, u32[]{:S(2)}) %collective-permute-start) | collective-permute-done | bytes 12320 | tf_op jit(solution)/shard_map/ppermute | solution.py:412
  25.2 0.0 collective-permute-done.1
  25.2 0.0 all-to-all-done.rows_ref
  25.2 1.2 %shard_map.67 = bf16[16,72,128]{2,1,0:T(8,128)(2,1)} custom-call(bf16[16,96,256]{2,1,0:T(8,128)(2,1)S(1)} %all-to-all-done.rows_ref, bf16[96,128]{1,0:T(8,128)(2,1)S(1)} %pad_maximum_fusion.sums_ref), custom_call_target="tpu_custom_call" | custom-call | tf_op jit(solution)/shard_map/pallas_call | solution.py:344
  26.4 5.3 %all-to-all-start.1 = ((bf16[16,72,128]{2,1,0:T(8,128)(2,1)}), bf16[16,72,128]{2,1,0:T(8,128)(2,1)S(1)}, u32[]{:S(2)}, u32[]{:S(2)}) async-start(bf16[16,72,128]{2,1,0:T(8,128)(2,1)} %shard_map.67), calls=%async_computation.1 | async-start | bytes 589824 | tf_op jit(solution)/shard_map/all_to_all | solution.py:425
  31.7 0.7 shard_map.68
  32.4 7.4 %all-to-all-done.1.message_ref = bf16[16,72,128]{2,1,0:T(8,128)(2,1)S(1)} async-done(((bf16[16,72,128]{2,1,0:T(8,128)(2,1)}), bf16[16,72,128]{2,1,0:T(8,128)(2,1)S(1)}, u32[]{:S(2)}, u32[]{:S(2)}) %all-to-all-start.1) | async-done | bytes 294944 | tf_op jit(solution)/shard_map/all_to_all | solution.py:425
  39.8 1.2 %shard_map.69 = (bf16[64,16,128]{2,1,0:T(8,128)(2,1)}, f32[2,384]{1,0:T(2,128)S(1)}) custom-call(bf16[16,72,128]{2,1,0:T(8,128)(2,1)S(1)} %all-to-all-done.1.message_ref, bf16[512,512]{1,0:T(8,128)(2,1)S(1)} %get-tuple-element.15.high_ref, bf16[512,512]{1,0:T(8,128)(2,1)S(1)} %get-tuple-element.16.low_ref), custom_call_target="tpu_custom_call" | custom-call | tf_op jit(solution)/shard_map/pallas_call | solution.py:344
  40.9 6.2 %all-to-all-start.2 = ((bf16[64,16,128]{2,1,0:T(8,128)(2,1)}), bf16[64,16,128]{2,1,0:T(8,128)(2,1)S(1)}, u32[]{:S(2)}, u32[]{:S(2)}) async-start(bf16[64,16,128]{2,1,0:T(8,128)(2,1)} %get-tuple-element.17), calls=%async_computation.2 | async-start | bytes 524288 | tf_op jit(solution)/shard_map/all_to_all | solution.py:433
  47.2 5.3 %collective-permute-start.2 = (f32[1,384]{1,0:T(1,128)S(1)}, f32[1,384]{1,0:T(1,128)S(1)}, u32[]{:S(2)}, u32[]{:S(2)}) collective-permute-start(f32[1,384]{1,0:T(1,128)S(1)} %slice.7), channel_id=1, source_target_pairs={{0,32},{4,36},{8,40},{12,44},{16,48},{20,52},{24,56},{28,60},{32,0... | collective-permute-start | bytes 4616 | tf_op jit(solution)/shard_map/ppermute | solution.py:435
  52.5 6.0 %collective-permute-done.2 = f32[1,384]{1,0:T(1,128)S(1)} collective-permute-done((f32[1,384]{1,0:T(1,128)S(1)}, f32[1,384]{1,0:T(1,128)S(1)}, u32[]{:S(2)}, u32[]{:S(2)}) %collective-permute-start.2) | collective-permute-done | bytes 1568 | tf_op jit(solution)/shard_map/ppermute | solution.py:435
  58.5 0.7 all-to-all-done.2.pieces_ref
  59.2 2.8 %collective-permute-start.5 = (bf16[264,128]{1,0:T(8,128)(2,1)S(1)}, bf16[264,128]{1,0:T(8,128)(2,1)S(1)}, u32[]{:S(2)}, u32[]{:S(2)}) collective-permute-start(bf16[264,128]{1,0:T(8,128)(2,1)S(1)} %get-tuple-element.20), channel_id=1, source_target_pairs={{0,3},{1,0},{2,1},{3,2},{4,7},{5,4},{6,5},{7,6},{8,11},{9,8},{10,9... | collective-permute-start | bytes 202760 | tf_op jit(solution)/shard_map/ppermute | solution.py:444
  62.0 0.3 collective-permute-start.4
  62.4 0.7 collective-permute-start.3
  63.1 3.7 %shard_map.64 = (f32[1,4096]{1,0:T(1,128)}, bf16[256,4096]{1,0:T(8,128)(2,1)}) custom-call(bf16[256,4096]{1,0:T(8,128)(2,1)} %bitcast.21), custom_call_target="tpu_custom_call" | custom-call | tf_op jit(solution)/shard_map/pallas_call | solution.py:344
  66.7 0.0 collective-permute-done.5.refs_2_
  66.7 0.0 collective-permute-done.4.refs_1_
  66.7 1.8 %collective-permute-done.3.refs_0_ = bf16[264,128]{1,0:T(8,128)(2,1)S(1)} collective-permute-done((bf16[264,128]{1,0:T(8,128)(2,1)S(1)}, bf16[264,128]{1,0:T(8,128)(2,1)S(1)}, u32[]{:S(2)}, u32[]{:S(2)}) %collective-permute-start.3) | collective-permute-done | bytes 67616 | tf_op jit(solution)/shard_map/ppermute | solution.py:444
  68.5 1.6 %copy-done = bf16[256,4096]{1,0:T(8,128)(2,1)S(1)} copy-done((bf16[256,4096]{1,0:T(8,128)(2,1)S(1)}, bf16[256,4096]{1,0:T(8,128)(2,1)}, u32[]{:S(2)}) %copy-start) | copy-done | bytes 2097176
  70.1 0.7 copy-done.2
  70.8 3.8 %shard_map.71 = bf16[256,4096]{1,0:T(8,128)(2,1)} custom-call(s32[1]{0:T(128)} %bitcast.level_ref, f32[1,4096]{1,0:T(1,128)S(1)} %copy-done.2, bf16[256,4096]{1,0:T(8,128)(2,1)S(1)} %copy-done, f32[264,128]{1,0:T(8,128)S(1)} %get-tuple-element.19.own_ref, bf16[264,128]{1,0:T(8,128)(2,1)S(1)} %collective-permute-done.3.refs_0_, ...), custom_call_target="tpu_custom_call" | custom-call | tf_op jit(solution)/shard_map/pallas_call | solution.py:344
  (13 shorter events, 0.1 us)
Async XLA Ops:
  0.0 10.1 %copy-start.4 = (bf16[1,1024]{1,0:T(2,128)(2,1)S(1)}, bf16[1,1024]{1,0:T(2,128)(2,1)}, u32[]{:S(2)}) copy-start(bf16[1,1024]{1,0:T(2,128)(2,1)} %precision_ref.1) | copy-start | bytes 6148
  0.0 10.1 %copy-start.3 = (s32[1,1024,1]{1,2,0:T(1,128)S(1)}, s32[1,1024,1]{1,2,0:T(1,128)}, u32[]{:S(2)}) copy-start(s32[1,1024,1]{1,2,0:T(1,128)} %param.10) | copy-start | bytes 12292
  0.0 10.2 %copy-start.1 = (bf16[1,1024,256]{2,1,0:T(8,128)(2,1)S(1)}, bf16[1,1024,256]{2,1,0:T(8,128)(2,1)}, u32[]{:S(2)}) copy-start(bf16[1,1024,256]{2,1,0:T(8,128)(2,1)} %param.7) | copy-start | bytes 1572868
  0.0 10.2 %copy-start.5 = (s32[64,3]{0,1:T(4,128)S(1)}, s32[64,3]{0,1:T(4,128)}, u32[]{:S(2)}) copy-start(s32[64,3]{0,1:T(4,128)} %param.11) | copy-start | bytes 2308
  0.0 10.2 %copy-start.6 = (bf16[1,1024]{1,0:T(2,128)(2,1)S(1)}, bf16[1,1024]{1,0:T(2,128)(2,1)}, u32[]{:S(2)}) copy-start(bf16[1,1024]{1,0:T(2,128)(2,1)} %innovation_ref.1) | copy-start | bytes 6148
  3.0 22.2 %all-to-all-start = ((bf16[16,96,256]{2,1,0:T(8,128)(2,1)}), bf16[16,96,256]{2,1,0:T(8,128)(2,1)S(1)}, u32[]{:S(2)}, u32[]{:S(2)}) async-start(bf16[16,96,256]{2,1,0:T(8,128)(2,1)} %shard_map.65), calls=%async_computation | async-start | bytes 1572864 | tf_op jit(solution)/shard_map/all_to_all | solution.py:386
  10.8 14.3 %collective-permute-start = (bf16[48,128]{1,0:T(8,128)(2,1)S(1)}, bf16[48,128]{1,0:T(8,128)(2,1)S(1)}, u32[]{:S(2)}, u32[]{:S(2)}) collective-permute-start(bf16[48,128]{1,0:T(8,128)(2,1)S(1)} %get-tuple-element.21), channel_id=1, source_target_pairs={{0,16},{4,20},{8,24},{12,28},{16,32},{20,36},{24,40},{28,44},{32,4... | collective-permute-start | bytes 36872 | tf_op jit(solution)/shard_map/ppermute | solution.py:412
  13.9 11.3 %collective-permute-start.1 = (bf16[48,128]{1,0:T(8,128)(2,1)S(1)}, bf16[48,128]{1,0:T(8,128)(2,1)S(1)}, u32[]{:S(2)}, u32[]{:S(2)}) collective-permute-start(bf16[48,128]{1,0:T(8,128)(2,1)S(1)} %get-tuple-element.23), channel_id=1, source_target_pairs={{0,48},{4,52},{8,56},{12,60},{16,0},{20,4},{24,8},{28,12},{32,16},... | collective-permute-start | bytes 36872 | tf_op jit(solution)/shard_map/ppermute | solution.py:412
  26.4 13.4 %all-to-all-start.1 = ((bf16[16,72,128]{2,1,0:T(8,128)(2,1)}), bf16[16,72,128]{2,1,0:T(8,128)(2,1)S(1)}, u32[]{:S(2)}, u32[]{:S(2)}) async-start(bf16[16,72,128]{2,1,0:T(8,128)(2,1)} %shard_map.67), calls=%async_computation.1 | async-start | bytes 589824 | tf_op jit(solution)/shard_map/all_to_all | solution.py:425
  40.9 18.2 %all-to-all-start.2 = ((bf16[64,16,128]{2,1,0:T(8,128)(2,1)}), bf16[64,16,128]{2,1,0:T(8,128)(2,1)S(1)}, u32[]{:S(2)}, u32[]{:S(2)}) async-start(bf16[64,16,128]{2,1,0:T(8,128)(2,1)} %get-tuple-element.17), calls=%async_computation.2 | async-start | bytes 524288 | tf_op jit(solution)/shard_map/all_to_all | solution.py:433
  47.2 11.3 %collective-permute-start.2 = (f32[1,384]{1,0:T(1,128)S(1)}, f32[1,384]{1,0:T(1,128)S(1)}, u32[]{:S(2)}, u32[]{:S(2)}) collective-permute-start(f32[1,384]{1,0:T(1,128)S(1)} %slice.7), channel_id=1, source_target_pairs={{0,32},{4,36},{8,40},{12,44},{16,48},{20,52},{24,56},{28,60},{32,0... | collective-permute-start | bytes 4616 | tf_op jit(solution)/shard_map/ppermute | solution.py:435
  59.2 7.5 %collective-permute-start.5 = (bf16[264,128]{1,0:T(8,128)(2,1)S(1)}, bf16[264,128]{1,0:T(8,128)(2,1)S(1)}, u32[]{:S(2)}, u32[]{:S(2)}) collective-permute-start(bf16[264,128]{1,0:T(8,128)(2,1)S(1)} %get-tuple-element.20), channel_id=1, source_target_pairs={{0,3},{1,0},{2,1},{3,2},{4,7},{5,4},{6,5},{7,6},{8,11},{9,8},{10,9... | collective-permute-start | bytes 202760 | tf_op jit(solution)/shard_map/ppermute | solution.py:444
  62.0 4.7 %collective-permute-start.4 = (bf16[264,128]{1,0:T(8,128)(2,1)S(1)}, bf16[264,128]{1,0:T(8,128)(2,1)S(1)}, u32[]{:S(2)}, u32[]{:S(2)}) collective-permute-start(bf16[264,128]{1,0:T(8,128)(2,1)S(1)} %get-tuple-element.20), channel_id=1, source_target_pairs={{0,2},{1,3},{2,0},{3,1},{4,6},{5,7},{6,4},{7,5},{8,10},{9,11},{10,... | collective-permute-start | bytes 202760 | tf_op jit(solution)/shard_map/ppermute | solution.py:444
  62.4 6.2 %collective-permute-start.3 = (bf16[264,128]{1,0:T(8,128)(2,1)S(1)}, bf16[264,128]{1,0:T(8,128)(2,1)S(1)}, u32[]{:S(2)}, u32[]{:S(2)}) collective-permute-start(bf16[264,128]{1,0:T(8,128)(2,1)S(1)} %get-tuple-element.20), channel_id=1, source_target_pairs={{0,1},{1,2},{2,3},{3,0},{4,5},{5,6},{6,7},{7,4},{8,9},{9,10},{10,1... | collective-permute-start | bytes 202760 | tf_op jit(solution)/shard_map/ppermute | solution.py:444
  68.5 1.6 %copy-start = (bf16[256,4096]{1,0:T(8,128)(2,1)S(1)}, bf16[256,4096]{1,0:T(8,128)(2,1)}, u32[]{:S(2)}) copy-start(bf16[256,4096]{1,0:T(8,128)(2,1)} %get-tuple-element.14.anomaly_ref) | copy-start | bytes 6291460
  70.1 0.7 copy-start.2

commit v11 on v9

--- a/solution.py
+++ b/solution.py
@@ -17,6 +17,7 @@
 PAIR = 2
 GROUPS = PLANES // PAIR
 WIDTH = 512
+ROWS = 3
 EXTRA = 8
 VMEM_LIMIT = 16 << 20
 FIRST_LIMIT = 62 << 20
@@ -155,13 +156,12 @@
     squares = dot(jnp.where(hit, precision, 0.0).astype(BF16), (half * half).astype(BF16))
     weight = split(weights_transposed(listed_ref[...]))
     row = iota((regions, groups * lines), 1)
-    item = row % EXTRA
-    region = region_at(row % lines // EXTRA, row // lines)
-    pick = onehot((iota((regions, groups * lines), 0) == region) & (item < 3))
+    region = region_at(row % lines // ROWS, row // lines)
+    pick = onehot(iota((regions, groups * lines), 0) == region)
     chosen = split(dot(weight[0], pick) + dot(weight[1], pick))
     over = ((0,), (0,))
     parts = [dot3(chosen, split(value), over) for value in (sums[:, :LANES], sums[:, LANES:], squares)]
-    kind = iota((groups * lines, LANES), 0) % EXTRA
+    kind = iota((groups * lines, LANES), 0) % ROWS
     mixed = jnp.where(kind == 0, parts[0], jnp.where(kind == 1, parts[1], parts[2]))
     sums_ref[...] = mixed.astype(BF16).reshape(groups, lines, LANES)
 
@@ -200,7 +200,11 @@
                 message_ref.at[:, part], message_out.at[:, part], semaphores.at[0]
             )
             first.start()
-    message_ref[:, GROUPS * piece :, :] = sums_ref[...].reshape(places, EXTRA, LANES)
+    wide = (places * EXTRA, places * ROWS)
+    line = iota(wide, 0)
+    spread = (line % EXTRA < ROWS) & (line // EXTRA * ROWS + line % EXTRA == iota(wide, 1))
+    sums = dot(onehot(spread), sums_ref[...]).astype(BF16)
+    message_ref[:, GROUPS * piece :, :] = sums.reshape(places, EXTRA, LANES)
     part = slice(GROUPS // 2 * piece, GROUPS * piece + EXTRA)
     second = pltpu.make_async_copy(
         message_ref.at[:, part], message_out.at[:, part], semaphores.at[1]
@@ -382,7 +386,7 @@
     )
     sums = call(
         sums_kernel,
-        shape((GROUPS, places * EXTRA, LANES), BF16),
+        shape((GROUPS, places * ROWS, LANES), BF16),
         owners,
         obs_precision,
         innovation,

time: 76.6 us -> 75 us (0.979)
  waiting for transfers between devices: 17 us -> 15.1 us
  starting transfers between devices: 26 us -> 26.8 us
    ppermute x3, waiting for transfers between devices: 7.84 us -> 5.97 us  [step(): arrived_part = lax.ppermute(sent, 'region', pairs)]
    all_to_all x1, starting transfers between devices: 5.28 us -> 6.07 us  [step(): lax.all_to_all(message, 'region', 0, 0, tiled=True, axis_index_groups=near)]
where the time goes in v11:
time: 75 us; the launch traced here: 74.6 us
  starting transfers between devices  26.8 us (36%)
  blocking collectives  16.8 us (22%)
  waiting for transfers between devices  15.1 us (20%)
  Pallas kernels  13.4 us (18%)
  local copies, waits for them, and re-layouts  2.34 us (3%)
    all_to_all x1, blocking collectives, step(): pieces = lax.all_to_all(mixed, 'region', 0, 0, tiled=True)  16.8 us
    pallas_call x8, Pallas kernels, call(): pl.pallas_call(kernel, out_shape=shapes, in_specs=[pl.BlockSpec(memory_sp...  13.4 us
    ppermute x3, starting transfers between devices, step(): arrived_part = lax.ppermute(sent, 'region', pairs)  9.67 us
    all_to_all x1, waiting for transfers between devices, step(): lax.all_to_all(message, 'region', 0, 0, tiled=True, axis_index_groups=near)  7.36 us
    all_to_all x1, starting transfers between devices, step(): lax.all_to_all(rows, 'region', 0, 0, tiled=True, axis_index_groups=near)  7.17 us
    all_to_all x1, starting transfers between devices, step(): lax.all_to_all(message, 'region', 0, 0, tiled=True, axis_index_groups=near)  6.07 us
    ppermute x3, waiting for transfers between devices, step(): arrived_part = lax.ppermute(sent, 'region', pairs)  5.97 us
    ppermute x3, starting transfers between devices, step(): arrived.append(lax.ppermute(sent, 'level', pairs))  3.85 us
  transfers between devices with their start and end apart: 8, of which 4 were waited for; matrix products, arithmetic and copies ran while one was open for 0% of the time, Pallas kernels for 7%

profile of v11, /device:TPU:1, one launch (start us, length us, event | category | flops | bytes accessed | tf_op | source)
XLA Modules:
  0.0 74.6 jit_solution(2783236097555162678)
XLA Ops:
  0.0 0.0 copy-start.5
  0.0 0.0 copy-start.6
  0.0 2.9 %shard_map.65 = bf16[16,96,256]{2,1,0:T(8,128)(2,1)} custom-call(s32[1,1024]{1,0:T(1,128)} %bitcast.17, bf16[1,1024]{1,0:T(2,128)(2,1)} %precision_ref.1, bf16[1024,256]{1,0:T(8,128)(2,1)} %bitcast.15), custom_call_target="tpu_custom_call" | custom-call | tf_op jit(solution)/shard_map/pallas_call | solution.py:340
  3.0 7.2 %all-to-all-start = ((bf16[16,96,256]{2,1,0:T(8,128)(2,1)}), bf16[16,96,256]{2,1,0:T(8,128)(2,1)S(1)}, u32[]{:S(2)}, u32[]{:S(2)}) async-start(bf16[16,96,256]{2,1,0:T(8,128)(2,1)} %shard_map.65), calls=%async_computation | async-start | bytes 1572864 | tf_op jit(solution)/shard_map/all_to_all | solution.py:382
  10.1 0.0 copy-done.3
  10.2 0.0 copy-done.1
  10.2 0.0 copy-done.5
  10.2 0.0 copy-done.6
  10.2 0.6 shard_map.66
  10.8 3.1 %collective-permute-start = (bf16[48,128]{1,0:T(8,128)(2,1)S(1)}, bf16[48,128]{1,0:T(8,128)(2,1)S(1)}, u32[]{:S(2)}, u32[]{:S(2)}) collective-permute-start(bf16[48,128]{1,0:T(8,128)(2,1)S(1)} %get-tuple-element.21), channel_id=1, source_target_pairs={{0,16},{4,20},{8,24},{12,28},{16,32},{20,36},{24,40},{28,44},{32,4... | collective-permute-start | bytes 36872 | tf_op jit(solution)/shard_map/ppermute | solution.py:404
  13.9 2.2 %collective-permute-start.2 = (bf16[48,128]{1,0:T(8,128)(2,1)S(1)}, bf16[48,128]{1,0:T(8,128)(2,1)S(1)}, u32[]{:S(2)}, u32[]{:S(2)}) collective-permute-start(bf16[48,128]{1,0:T(8,128)(2,1)S(1)} %get-tuple-element.22), channel_id=1, source_target_pairs={{0,48},{4,52},{8,56},{12,60},{16,0},{20,4},{24,8},{28,12},{32,16},... | collective-permute-start | bytes 36872 | tf_op jit(solution)/shard_map/ppermute | solution.py:404
  16.1 4.4 %collective-permute-start.1 = (bf16[48,128]{1,0:T(8,128)(2,1)S(1)}, bf16[48,128]{1,0:T(8,128)(2,1)S(1)}, u32[]{:S(2)}, u32[]{:S(2)}) collective-permute-start(bf16[48,128]{1,0:T(8,128)(2,1)S(1)} %get-tuple-element.23), channel_id=1, source_target_pairs={{0,32},{4,36},{8,40},{12,44},{16,48},{20,52},{24,56},{28,60},{32,0... | collective-permute-start | bytes 36872 | tf_op jit(solution)/shard_map/ppermute | solution.py:404
  20.5 4.7 %collective-permute-done = bf16[48,128]{1,0:T(8,128)(2,1)S(1)} collective-permute-done((bf16[48,128]{1,0:T(8,128)(2,1)S(1)}, bf16[48,128]{1,0:T(8,128)(2,1)S(1)}, u32[]{:S(2)}, u32[]{:S(2)}) %collective-permute-start) | collective-permute-done | bytes 12320 | tf_op jit(solution)/shard_map/ppermute | solution.py:404
  25.2 0.0 collective-permute-done.2
  25.2 1.3 %collective-permute-done.1 = bf16[48,128]{1,0:T(8,128)(2,1)S(1)} collective-permute-done((bf16[48,128]{1,0:T(8,128)(2,1)S(1)}, bf16[48,128]{1,0:T(8,128)(2,1)S(1)}, u32[]{:S(2)}, u32[]{:S(2)}) %collective-permute-start.1) | collective-permute-done | bytes 12320 | tf_op jit(solution)/shard_map/ppermute | solution.py:404
  26.5 0.0 all-to-all-done.rows_ref
  26.5 1.2 %shard_map.67 = bf16[16,72,128]{2,1,0:T(8,128)(2,1)} custom-call(bf16[16,96,256]{2,1,0:T(8,128)(2,1)S(1)} %all-to-all-done.rows_ref, bf16[48,128]{1,0:T(8,128)(2,1)S(1)} %fusion.2.sums_ref), custom_call_target="tpu_custom_call" | custom-call | tf_op jit(solution)/shard_map/pallas_call | solution.py:340
  27.7 6.1 %all-to-all-start.1 = ((bf16[16,72,128]{2,1,0:T(8,128)(2,1)}), bf16[16,72,128]{2,1,0:T(8,128)(2,1)S(1)}, u32[]{:S(2)}, u32[]{:S(2)}) async-start(bf16[16,72,128]{2,1,0:T(8,128)(2,1)} %shard_map.67), calls=%async_computation.1 | async-start | bytes 589824 | tf_op jit(solution)/shard_map/all_to_all | solution.py:416
  33.8 0.7 shard_map.68
  34.5 7.4 %all-to-all-done.1.message_ref = bf16[16,72,128]{2,1,0:T(8,128)(2,1)S(1)} async-done(((bf16[16,72,128]{2,1,0:T(8,128)(2,1)}), bf16[16,72,128]{2,1,0:T(8,128)(2,1)S(1)}, u32[]{:S(2)}, u32[]{:S(2)}) %all-to-all-start.1) | async-done | bytes 294944 | tf_op jit(solution)/shard_map/all_to_all | solution.py:416
  41.8 0.4 shard_map.69
  42.3 16.8 %all_to_all.15.pieces_ref = bf16[64,16,128]{2,1,0:T(8,128)(2,1)S(1)} all-to-all(bf16[64,16,128]{2,1,0:T(8,128)(2,1)S(1)} %get-tuple-element.17), channel_id=1, replica_groups=mesh['region'=64,'level'=4] {'region'}, dimensions={0} | all-to-all | bytes 524288 | tf_op jit(solution)/shard_map/all_to_all | solution.py:424
  59.1 2.8 %collective-permute-start.5 = (bf16[264,128]{1,0:T(8,128)(2,1)S(1)}, bf16[264,128]{1,0:T(8,128)(2,1)S(1)}, u32[]{:S(2)}, u32[]{:S(2)}) collective-permute-start(bf16[264,128]{1,0:T(8,128)(2,1)S(1)} %get-tuple-element.20), channel_id=1, source_target_pairs={{0,3},{1,0},{2,1},{3,2},{4,7},{5,4},{6,5},{7,6},{8,11},{9,8},{10,9... | collective-permute-start | bytes 202760 | tf_op jit(solution)/shard_map/ppermute | solution.py:433
  62.0 0.4 collective-permute-start.4
  62.3 0.7 collective-permute-start.3
  63.0 3.7 %shard_map.64 = (f32[1,4096]{1,0:T(1,128)}, bf16[256,4096]{1,0:T(8,128)(2,1)}) custom-call(bf16[256,4096]{1,0:T(8,128)(2,1)} %bitcast.21), custom_call_target="tpu_custom_call" | custom-call | tf_op jit(solution)/shard_map/pallas_call | solution.py:340
  66.7 0.0 collective-permute-done.5.refs_2_
  66.7 0.0 collective-permute-done.4.refs_1_
  66.7 1.7 %collective-permute-done.3.refs_0_ = bf16[264,128]{1,0:T(8,128)(2,1)S(1)} collective-permute-done((bf16[264,128]{1,0:T(8,128)(2,1)S(1)}, bf16[264,128]{1,0:T(8,128)(2,1)S(1)}, u32[]{:S(2)}, u32[]{:S(2)}) %collective-permute-start.3) | collective-permute-done | bytes 67616 | tf_op jit(solution)/shard_map/ppermute | solution.py:433
  68.4 1.6 %copy-done = bf16[256,4096]{1,0:T(8,128)(2,1)S(1)} copy-done((bf16[256,4096]{1,0:T(8,128)(2,1)S(1)}, bf16[256,4096]{1,0:T(8,128)(2,1)}, u32[]{:S(2)}) %copy-start) | copy-done | bytes 2097176
  70.0 0.7 copy-done.2
  70.7 3.8 %shard_map.71 = bf16[256,4096]{1,0:T(8,128)(2,1)} custom-call(s32[1]{0:T(128)} %bitcast.level_ref, f32[1,4096]{1,0:T(1,128)S(1)} %copy-done.2, bf16[256,4096]{1,0:T(8,128)(2,1)S(1)} %copy-done, f32[264,128]{1,0:T(8,128)S(1)} %get-tuple-element.19.own_ref, bf16[264,128]{1,0:T(8,128)(2,1)S(1)} %collective-permute-done.3.refs_0_, ...), custom_call_target="tpu_custom_call" | custom-call | tf_op jit(solution)/shard_map/pallas_call | solution.py:340
  (9 shorter events, 0.1 us)
Async XLA Ops:
  0.0 10.1 %copy-start.4 = (bf16[1,1024]{1,0:T(2,128)(2,1)S(1)}, bf16[1,1024]{1,0:T(2,128)(2,1)}, u32[]{:S(2)}) copy-start(bf16[1,1024]{1,0:T(2,128)(2,1)} %precision_ref.1) | copy-start | bytes 6148
  0.0 10.1 %copy-start.3 = (s32[1,1024,1]{1,2,0:T(1,128)S(1)}, s32[1,1024,1]{1,2,0:T(1,128)}, u32[]{:S(2)}) copy-start(s32[1,1024,1]{1,2,0:T(1,128)} %param.10) | copy-start | bytes 12292
  0.0 10.2 %copy-start.1 = (bf16[1,1024,256]{2,1,0:T(8,128)(2,1)S(1)}, bf16[1,1024,256]{2,1,0:T(8,128)(2,1)}, u32[]{:S(2)}) copy-start(bf16[1,1024,256]{2,1,0:T(8,128)(2,1)} %param.7) | copy-start | bytes 1572868
  0.0 10.2 %copy-start.5 = (s32[64,3]{0,1:T(4,128)S(1)}, s32[64,3]{0,1:T(4,128)}, u32[]{:S(2)}) copy-start(s32[64,3]{0,1:T(4,128)} %param.11) | copy-start | bytes 2308
  0.0 10.2 %copy-start.6 = (bf16[1,1024]{1,0:T(2,128)(2,1)S(1)}, bf16[1,1024]{1,0:T(2,128)(2,1)}, u32[]{:S(2)}) copy-start(bf16[1,1024]{1,0:T(2,128)(2,1)} %innovation_ref.1) | copy-start | bytes 6148
  3.0 23.5 %all-to-all-start = ((bf16[16,96,256]{2,1,0:T(8,128)(2,1)}), bf16[16,96,256]{2,1,0:T(8,128)(2,1)S(1)}, u32[]{:S(2)}, u32[]{:S(2)}) async-start(bf16[16,96,256]{2,1,0:T(8,128)(2,1)} %shard_map.65), calls=%async_computation | async-start | bytes 1572864 | tf_op jit(solution)/shard_map/all_to_all | solution.py:382
  10.8 14.3 %collective-permute-start = (bf16[48,128]{1,0:T(8,128)(2,1)S(1)}, bf16[48,128]{1,0:T(8,128)(2,1)S(1)}, u32[]{:S(2)}, u32[]{:S(2)}) collective-permute-start(bf16[48,128]{1,0:T(8,128)(2,1)S(1)} %get-tuple-element.21), channel_id=1, source_target_pairs={{0,16},{4,20},{8,24},{12,28},{16,32},{20,36},{24,40},{28,44},{32,4... | collective-permute-start | bytes 36872 | tf_op jit(solution)/shard_map/ppermute | solution.py:404
  13.9 11.3 %collective-permute-start.2 = (bf16[48,128]{1,0:T(8,128)(2,1)S(1)}, bf16[48,128]{1,0:T(8,128)(2,1)S(1)}, u32[]{:S(2)}, u32[]{:S(2)}) collective-permute-start(bf16[48,128]{1,0:T(8,128)(2,1)S(1)} %get-tuple-element.22), channel_id=1, source_target_pairs={{0,48},{4,52},{8,56},{12,60},{16,0},{20,4},{24,8},{28,12},{32,16},... | collective-permute-start | bytes 36872 | tf_op jit(solution)/shard_map/ppermute | solution.py:404
  16.1 10.4 %collective-permute-start.1 = (bf16[48,128]{1,0:T(8,128)(2,1)S(1)}, bf16[48,128]{1,0:T(8,128)(2,1)S(1)}, u32[]{:S(2)}, u32[]{:S(2)}) collective-permute-start(bf16[48,128]{1,0:T(8,128)(2,1)S(1)} %get-tuple-element.23), channel_id=1, source_target_pairs={{0,32},{4,36},{8,40},{12,44},{16,48},{20,52},{24,56},{28,60},{32,0... | collective-permute-start | bytes 36872 | tf_op jit(solution)/shard_map/ppermute | solution.py:404
  27.7 14.1 %all-to-all-start.1 = ((bf16[16,72,128]{2,1,0:T(8,128)(2,1)}), bf16[16,72,128]{2,1,0:T(8,128)(2,1)S(1)}, u32[]{:S(2)}, u32[]{:S(2)}) async-start(bf16[16,72,128]{2,1,0:T(8,128)(2,1)} %shard_map.67), calls=%async_computation.1 | async-start | bytes 589824 | tf_op jit(solution)/shard_map/all_to_all | solution.py:416
  59.1 7.5 %collective-permute-start.5 = (bf16[264,128]{1,0:T(8,128)(2,1)S(1)}, bf16[264,128]{1,0:T(8,128)(2,1)S(1)}, u32[]{:S(2)}, u32[]{:S(2)}) collective-permute-start(bf16[264,128]{1,0:T(8,128)(2,1)S(1)} %get-tuple-element.20), channel_id=1, source_target_pairs={{0,3},{1,0},{2,1},{3,2},{4,7},{5,4},{6,5},{7,6},{8,11},{9,8},{10,9... | collective-permute-start | bytes 202760 | tf_op jit(solution)/shard_map/ppermute | solution.py:433
  62.0 4.7 %collective-permute-start.4 = (bf16[264,128]{1,0:T(8,128)(2,1)S(1)}, bf16[264,128]{1,0:T(8,128)(2,1)S(1)}, u32[]{:S(2)}, u32[]{:S(2)}) collective-permute-start(bf16[264,128]{1,0:T(8,128)(2,1)S(1)} %get-tuple-element.20), channel_id=1, source_target_pairs={{0,2},{1,3},{2,0},{3,1},{4,6},{5,7},{6,4},{7,5},{8,10},{9,11},{10,... | collective-permute-start | bytes 202760 | tf_op jit(solution)/shard_map/ppermute | solution.py:433
  62.3 6.1 %collective-permute-start.3 = (bf16[264,128]{1,0:T(8,128)(2,1)S(1)}, bf16[264,128]{1,0:T(8,128)(2,1)S(1)}, u32[]{:S(2)}, u32[]{:S(2)}) collective-permute-start(bf16[264,128]{1,0:T(8,128)(2,1)S(1)} %get-tuple-element.20), channel_id=1, source_target_pairs={{0,1},{1,2},{2,3},{3,0},{4,5},{5,6},{6,7},{7,4},{8,9},{9,10},{10,1... | collective-permute-start | bytes 202760 | tf_op jit(solution)/shard_map/ppermute | solution.py:433
  68.4 1.6 %copy-start = (bf16[256,4096]{1,0:T(8,128)(2,1)S(1)}, bf16[256,4096]{1,0:T(8,128)(2,1)}, u32[]{:S(2)}) copy-start(bf16[256,4096]{1,0:T(8,128)(2,1)} %get-tuple-element.14.anomaly_ref) | copy-start | bytes 6291460
  70.0 0.7 copy-start.2
